TPU v7x, 32 devices: a whole 2x2x4 slice. The times are simulated.
32 devices in a mesh: groups: 2 (over y), orient: 4 (over z), img: 2 (over x), brick: 2 (over core).
Axes of the slice: x: 2, y: 2, z: 4, core: 2. Of those that a mesh axis runs over, the one named last changes fastest.
Arguments:
- images: bfloat16 [1024, 4096], P(('groups', 'orient', 'img', 'brick')), parts along dimension 0, may hold values from -8 to 8
- offsets: int32 [1024, 2], P('groups'), parts along dimension 0, may hold values from -6 to 6
- slices: bfloat16 [2048, 4096], P(('groups', 'orient')), parts along dimension 0, may hold values from -3 to 3
- seg_map: int32 [8192, 1], replicated, may hold values from 0 to 15; in each aligned block of 512 rows (0 to 511, 512 to 1023, ...) at most 64 rows name the same one
- interp: int32 [16, 8, 256, 256], P(('orient', 'img', 'brick')), may hold values from 0 to 4095
Outputs:
- brick_values: float32 [32, 2, 256], P(('groups', 'orient', 'img', 'brick')), parts along dimension 0
- brick_weight: float32 [32, 256], P(('groups', 'orient', 'img', 'brick')), parts along dimension 0
There are 2 independent parts, one for each index of `groups`. A program takes and returns all parts, laid end to end along the dimension named above; an argument that names none is the same for every part. Nothing has to cross between parts.
Inputs may be any that keep to these rules, and one draw needn't show every extreme that they name: `seg_map`: in each aligned block of 512 rows no brick is named by more than 64 rows; in every draw some block names some brick exactly 64 times.
All inputs are finite; a program needn't handle non-finite values.
Results may differ from a plain program's by a relative error of at most 0.019.
Values may be sent and summed in bfloat16 or wider, within the bound.
No kernel may reach another device: no remote copies, remote signals or barrier semaphores. Data moves between devices by JAX's collectives and lax.ppermute only.
A program may use at most 64 MiB of HBM per device.

v0:
```python
import jax
import jax.numpy as jnp
from jax import lax
from jax.sharding import PartitionSpec as P

K = 2048
SHIFTS = 16
SEG = 256


frame_side = 64
interp_scale = 1.0 / 256.0


def combined_all(array, axis, combine):
    everything = jax.tree.map(lambda part: lax.all_gather(part, axis), array)
    leading = jax.tree.map(lambda part: part[0], everything)

    def turn(k, so_far):
        return combine(so_far, jax.tree.map(lambda part: part[k], everything))

    return lax.fori_loop(1, lax.axis_size(axis), turn, leading)


def shift_images(image_rows, image_offsets):
    row_count = image_rows.shape[0]
    coeffs = image_rows.shape[1] // 2
    coef_index = jnp.arange(coeffs, dtype=jnp.int32)
    column_freq = coef_index % frame_side - frame_side // 2
    row_freq = coef_index // frame_side
    shift_index = jnp.arange(SHIFTS, dtype=jnp.int32)
    shift_x = image_offsets[:, 0][:, None] + (shift_index % 4 - 2)[None, :]
    shift_y = image_offsets[:, 1][:, None] + (shift_index // 4 - 2)[None, :]
    phase_index = jnp.mod(
        shift_x[:, :, None] * column_freq[None, None, :]
        + shift_y[:, :, None] * row_freq[None, None, :],
        frame_side,
    )
    angle = phase_index.astype(jnp.float32) * (2.0 * jnp.pi / frame_side)
    cosine = jnp.cos(angle)
    sine = jnp.sin(angle)
    real_part = image_rows[:, :coeffs].astype(jnp.float32)[:, None, :]
    imag_part = image_rows[:, coeffs:].astype(jnp.float32)[:, None, :]
    out_real = real_part * cosine + imag_part * sine
    out_imag = imag_part * cosine - real_part * sine
    joined = jnp.concatenate([out_real, out_imag], axis=-1).astype(jnp.bfloat16)
    return joined.reshape(row_count * SHIFTS, 2 * coeffs)


def combine_mass(first, second):
    top_score = jnp.maximum(first[0], second[0])
    return (
        top_score,
        first[1] * jnp.exp(first[0] - top_score) + second[1] * jnp.exp(second[0] - top_score),
    )


def per_device(images, offsets, slices, seg_map, interp):
    inv_noise = 100.0 / K
    orient_count = lax.axis_size("orient")
    group_count = lax.axis_size("img") * lax.axis_size("brick")
    group_index = lax.axis_index("img") * lax.axis_size("brick") + lax.axis_index("brick")
    flat_index = lax.axis_index("orient") * group_count + group_index
    brick_count = orient_count * group_count
    per_shard = images.shape[0]
    orient_local = slices.shape[0]
    group_offsets = lax.dynamic_index_in_dim(
        offsets.reshape(orient_count, group_count, per_shard, 2), group_index, 1, keepdims=False
    )
    group_offsets = group_offsets.reshape(orient_count * per_shard, 2)
    shifted = shift_images(lax.all_gather(images, "orient", axis=0, tiled=True), group_offsets)
    half_norm = 0.5 * jnp.sum(jnp.square(slices.astype(jnp.float32)), axis=1)
    intersections = lax.dot_general(
        shifted, slices, (((1,), (1,)), ((), ())), preferred_element_type=jnp.float32
    )
    score = inv_noise * (intersections - half_norm[None, :])
    per_image = score.reshape(-1, SHIFTS * orient_local)
    local_top = jnp.max(per_image, axis=1)
    local_terms = jnp.exp(per_image - local_top[:, None])
    local_mass = jnp.sum(local_terms, axis=1)
    top_score, mass_total = combined_all((local_top, local_mass), "orient", combine_mass)
    exp_terms = local_terms * jnp.exp(local_top - top_score)[:, None]
    posterior = (exp_terms / mass_total[:, None]).astype(jnp.bfloat16).reshape(-1, orient_local)
    weighted = lax.dot_general(
        posterior, shifted, (((0,), (0,)), ((), ())), preferred_element_type=jnp.float32
    )
    post_mass = jnp.sum(posterior.astype(jnp.float32), axis=0)
    own_rows = orient_local // group_count
    own_slices, own_mass = (
        lax.psum_scatter(
            weighted.astype(jnp.bfloat16), ("img", "brick"), scatter_dimension=0, tiled=True
        ).astype(jnp.float32),
        lax.psum_scatter(
            post_mass.astype(jnp.bfloat16), ("img", "brick"), scatter_dimension=0, tiled=True
        ).astype(jnp.float32),
    )
    seg_count = K // SEG
    seg_rows = own_rows * seg_count
    capacity = 2 * ((seg_rows + brick_count - 1) // brick_count)
    brick_table = seg_map[:, 0].reshape(brick_count, seg_rows)
    own_dest = lax.dynamic_index_in_dim(brick_table, flat_index, 0, keepdims=False)
    brick_ids = jnp.arange(brick_count, dtype=jnp.int32)
    brick_hits = (own_dest[:, None] == brick_ids[None, :]).astype(jnp.int32)
    slot_rank = jnp.sum((jnp.cumsum(brick_hits, axis=0) - 1) * brick_hits, axis=1)
    target = own_dest * capacity + slot_rank
    select = (
        jnp.arange(brick_count * capacity, dtype=jnp.int32)[:, None] == target[None, :]
    ).astype(jnp.float32)
    select = select.reshape(brick_count * capacity, own_rows, seg_count)
    pieces = own_slices.reshape(own_rows, 2, seg_count, SEG)
    outgoing = jnp.einsum("qtj,tpjs->qps", select, pieces, precision=lax.Precision.HIGHEST)
    outgoing = outgoing.reshape(brick_count, capacity, 2, SEG)
    outgoing_mass = jnp.einsum(
        "qtj,t->q", select, own_mass, precision=lax.Precision.HIGHEST
    ).reshape(brick_count, capacity)
    arrived, arrived_mass = (
        lax.all_to_all(
            outgoing.astype(jnp.bfloat16),
            ("orient", "img", "brick"),
            split_axis=0,
            concat_axis=0,
            tiled=True,
        ).astype(outgoing.dtype),
        lax.all_to_all(
            outgoing_mass.astype(jnp.bfloat16),
            ("orient", "img", "brick"),
            split_axis=0,
            concat_axis=0,
            tiled=True,
        ).astype(outgoing_mass.dtype),
    )
    arrivals = brick_table == flat_index
    arrival_slot = jnp.cumsum(arrivals.astype(jnp.int32), axis=1) - 1
    slot_place = jnp.where(arrivals, arrival_slot, -1)
    slot_pick = (
        slot_place[:, :, None] == jnp.arange(capacity, dtype=jnp.int32)[None, None, :]
    ).astype(jnp.float32)
    segment_of = jnp.arange(seg_rows, dtype=jnp.int32) % seg_count
    segment_pick = (segment_of[:, None] == jnp.arange(seg_count, dtype=jnp.int32)[None, :]).astype(
        jnp.float32
    )
    routing = jnp.einsum("src,rj->scj", slot_pick, segment_pick, precision=lax.Precision.HIGHEST)
    seg_total = jnp.einsum("scj,scpv->jpv", routing, arrived, precision=lax.Precision.HIGHEST)
    seg_mass = jnp.einsum("scj,sc->j", routing, arrived_mass, precision=lax.Precision.HIGHEST)
    weights = interp[0].astype(jnp.float32) * interp_scale
    brick_values = jnp.einsum("jps,jsv->pv", seg_total, weights, precision=lax.Precision.HIGHEST)
    coverage = jnp.sum(weights, axis=1)
    brick_weight = jnp.einsum("j,jv->v", seg_mass, coverage, precision=lax.Precision.HIGHEST)
    return (brick_values[None], brick_weight[None])


def solution(mesh):
    placed = (
        P(("groups", "orient", "img", "brick"), None),
        P("groups", None),
        P(("groups", "orient"), None),
        P(),
        P(("orient", "img", "brick"), None, None, None),
    )
    return jax.shard_map(
        per_device,
        mesh=mesh,
        in_specs=placed,
        out_specs=(
            P(("groups", "orient", "img", "brick"), None, None),
            P(("groups", "orient", "img", "brick"), None),
        ),
        check_vma=False,
    )
```

profile of v0, /device:TPU:0, one launch (start us, length us, event | category | flops | bytes accessed | tf_op | source)
XLA Modules:
  0.0 226.4 jit_solution(8136047674621850956)
XLA Ops:
  7.2 0.7 all-gather.6.cloned.1.call-update
  8.0 0.8 reshape.244
  8.8 0.1 reshape.245
  8.8 0.1 broadcast_add_fusion.1
  9.0 0.1 broadcast_add_fusion
  9.1 0.1 add.205
  9.2 2.1 multiply_reduce_fusion
  11.3 29.0 %all-gather.6.cloned.1.call-done = bf16[128,4096]{1,0:T(8,128)(2,1)} async-done(((bf16[32,4096]{1,0:T(8,128)(2,1)}), bf16[128,4096]{1,0:T(8,128)(2,1)}) %all-gather.6.cloned.1.call-update) | async-done | bytes 1048592 | tf_op jit(solution)/shard_map/all_gather | solution.py:71
  40.3 1.4 slice_convert_fusion.1
  41.7 72.2 %fusion.6 = (bf16[2048,2048]{1,0:T(8,128)(2,1)S(1)}, bf16[2048,2048]{1,0:T(8,128)(2,1)S(1)}) fusion(f32[128,2048]{1,0:T(8,128)S(1)} %get-tuple-element.154, s32[2048]{0:T(1024)S(1)} %get-tuple-element.161, s32[2048]{0:T(1024)S(1)} %add.205, s32[2048]{0:T(1024)S(1)} %get-tuple-element.162, s32[2048]{0:T(1024)S(1)} %add.200, f32[128,2048]{1,0:T(8,128)S(1)} %get-tuple-element.153), kind=kLoop, calls=%fused_computation.17 | loop fusion | flops 100663296 | bytes 18907136 | tf_op jit(solution)/shard_map/convert.2
  114.0 8.9 %fusion.60 = (f32[2048]{0:T(1024)S(1)}, f32[2048,256]{0,1:T(8,128)}) fusion(f32[256]{0:T(256)S(1)} %broadcast_multiply_fusion, bf16[256,4096]{1,0:T(8,128)(2,1)} %param.9, bf16[2048,2048]{1,0:T(8,128)(2,1)S(1)} %get-tuple-element.152, bf16[2048,2048]{1,0:T(8,128)(2,1)S(1)} %get-tuple-element.151), kind=kOutput, calls=%fused_computation.115 | convolution fusion | flops 4330092544 | bytes 20980736 | tf_op jit(solution)/shard_map/dot_general | solution.py:73
  123.0 0.1 reduce_max.18
  123.2 0.1 sub.97
  123.3 1.9 fusion.25
  125.3 0.1 reduce_sum.71
  125.4 9.4 %all-gather.3 = f32[4,1,128]{2,1,0:T(1,128)S(1)} all-gather(f32[1,1,128]{2,1,0:T(1,128)S(1)} %bitcast.147), channel_id=3, replica_groups=mesh['groups'=2,'orient'=4,'img'=2,'brick'=2] {'orient'}, dimensions={0}, use_global_device_ids=true | all-gather | bytes 2560 | tf_op jit(solution)/shard_map/all_gather | solution.py:16
  134.8 7.8 %all-gather.2 = f32[4,1,128]{2,1,0:T(1,128)S(1)} all-gather(f32[1,1,128]{2,1,0:T(1,128)S(1)} %bitcast.146), channel_id=2, replica_groups=mesh['groups'=2,'orient'=4,'img'=2,'brick'=2] {'orient'}, dimensions={0}, use_global_device_ids=true | all-gather | bytes 2560 | tf_op jit(solution)/shard_map/all_gather | solution.py:16
  142.5 0.1 while.17
  142.7 0.1 mul.174
  142.9 0.1 div.34
  143.0 2.2 fusion.59
  145.2 10.1 %fusion.13 = bf16[256,4096]{1,0:T(8,128)(2,1)} fusion(bf16[2048,256]{0,1:T(8,128)(2,1)S(1)} %get-tuple-element.150, bf16[2048,2048]{1,0:T(8,128)(2,1)} %copy-done.1, bf16[2048,2048]{1,0:T(8,128)(2,1)} %copy-done), kind=kOutput, calls=%fused_computation.25 | convolution fusion | flops 4329570304 | bytes 19922944 | tf_op jit(solution)/shard_map/dot_general | solution.py:84
  155.4 0.5 broadcast.343
  155.9 0.8 reduce.21
  156.8 1.2 reduce-window.16
  157.9 0.2 slice_reduce_fusion
  158.2 0.1 fusion.37
  158.3 0.1 eq.136
  158.4 0.7 convert_reduce_fusion
  159.1 0.2 copy.39
  159.3 0.6 dynamic-slice
  160.6 5.9 %all-reduce = bf16[256]{0:T(256)(128)(2,1)S(1)} all-reduce(bf16[256]{0:T(256)(128)(2,1)S(1)} %get-tuple-element.149), channel_id=5, replica_groups=mesh['groups'=2,'orient'=4,'img'=2,'brick'=2] {'img','brick'}, use_global_device_ids=true, to_apply=%region_15.16.clone | all-reduce | flops 256 | bytes 1024
  166.4 0.7 fusion.55
  167.2 0.6 copy.32
  167.8 4.3 %all-to-all-start.1 = ((bf16[16,1,64]{2,1,0:T(2,128)(2,1)}), bf16[16,1,64]{2,1,0:T(2,128)(2,1)S(1)}, u32[]{:S(2)}, u32[]{:S(2)}) async-start(bf16[16,1,64]{2,1,0:T(2,128)(2,1)} %copy.32), calls=%async_computation.2 | async-start | bytes 16384 | tf_op jit(solution)/shard_map/all_to_all | solution.py:124
  172.1 14.1 %reduce-scatter.2.cloned.1.call-done = bf16[64,4096]{1,0:T(8,128)(2,1)} async-done(((bf16[256,4096]{1,0:T(8,128)(2,1)}), bf16[64,4096]{1,0:T(8,128)(2,1)}) %reduce-scatter.2.cloned.1.call-update) | async-done | bytes 524304 | tf_op jit(solution)/shard_map/reduce_scatter | solution.py:90
  186.2 1.1 copy.42
  187.3 2.5 %bitcast_convert_fusion = bf16[16,64,2,256]{3,1,2,0:T(8,128)(2,1)} fusion(s32[8,64]{0,1:T(8,128)S(1)} %bitcast.138, s32[16,64]{1,0:T(8,128)S(1)} %multiply_add_fusion, bf16[64,2,8,256]{3,2,1,0:T(8,128)(2,1)S(1)} %bitcast.137), kind=kOutput, calls=%fused_computation.34 | convolution fusion | flops 537919488 | bytes 1579008 | tf_op jit(solution)/shard_map/qtj,tpjs->qps/dot_general | solution.py:111
  189.8 4.7 %all-to-all-start = ((bf16[16,64,2,256]{3,1,2,0:T(8,128)(2,1)}), bf16[16,64,2,256]{3,1,2,0:T(8,128)(2,1)S(1)}, u32[]{:S(2)}, u32[]{:S(2)}) async-start(bf16[16,64,2,256]{3,1,2,0:T(8,128)(2,1)} %bitcast_convert_fusion), calls=%async_computation.1 | async-start | bytes 2097152 | tf_op jit(solution)/shard_map/all_to_all | solution.py:117
  194.6 1.2 reduce-window.14
  195.7 0.2 slice_reduce_fusion.1
  196.0 0.2 fusion.24
  196.3 0.5 fusion.23
  196.8 0.1 convolution_bitcast_fusion.1
  197.0 0.8 fusion.61
  197.7 19.7 %all-to-all-done = bf16[16,64,2,256]{3,1,2,0:T(8,128)(2,1)S(1)} async-done(((bf16[16,64,2,256]{3,1,2,0:T(8,128)(2,1)}), bf16[16,64,2,256]{3,1,2,0:T(8,128)(2,1)S(1)}, u32[]{:S(2)}, u32[]{:S(2)}) %all-to-all-start) | async-done | bytes 1048608 | tf_op jit(solution)/shard_map/all_to_all | solution.py:117
  217.4 0.5 convolution_bitcast_fusion
  218.0 1.6 fusion.28
  (45 shorter events, 1.0 us)
Async XLA Ops:
  7.2 33.1 %all-gather.6.cloned.1.call-start = ((), (), s32[]{:S(2)}) async-start(), calls=%async_computation.3 | async-start | bytes 1310720 | tf_op jit(solution)/shard_map/all_gather | solution.py:71
  7.9 178.3 %reduce-scatter.2.cloned.1.call-start = ((), (), s32[]{:S(2)}) async-start(), calls=%async_computation.4 | async-start | bytes 2621440 | tf_op jit(solution)/shard_map/reduce_scatter | solution.py:90
  114.0 9.0 %copy-start = (bf16[2048,2048]{1,0:T(8,128)(2,1)}, bf16[2048,2048]{1,0:T(8,128)(2,1)S(1)}, u32[]{:S(2)}) copy-start(bf16[2048,2048]{1,0:T(8,128)(2,1)S(1)} %get-tuple-element.151) | copy-start | bytes 25165828
  114.0 9.0 %copy-start.1 = (bf16[2048,2048]{1,0:T(8,128)(2,1)}, bf16[2048,2048]{1,0:T(8,128)(2,1)S(1)}, u32[]{:S(2)}) copy-start(bf16[2048,2048]{1,0:T(8,128)(2,1)S(1)} %get-tuple-element.152) | copy-start | bytes 25165828
  145.2 10.7 %copy-start.3 = (s32[8192,1]{0,1:T(1,128)S(1)}, s32[8192,1]{0,1:T(1,128)}, u32[]{:S(2)}) copy-start(s32[8192,1]{0,1:T(1,128)} %param.10) | copy-start | bytes 98308
  145.2 14.1 %copy-start.4 = (u32[32]{0:T(128)S(1)}, u32[32]{0:T(128)}, u32[]{:S(2)}) copy-start(u32[32]{0:T(128)} %constant.178) | copy-start | bytes 388
  155.4 40.6 %copy-start.2 = (s32[1,8,256,256]{3,2,1,0:T(8,128)S(1)}, s32[1,8,256,256]{3,2,1,0:T(8,128)}, u32[]{:S(2)}) copy-start(s32[1,8,256,256]{3,2,1,0:T(8,128)} %param.11) | copy-start | bytes 6291460
  167.8 22.0 %all-to-all-start.1 = ((bf16[16,1,64]{2,1,0:T(2,128)(2,1)}), bf16[16,1,64]{2,1,0:T(2,128)(2,1)S(1)}, u32[]{:S(2)}, u32[]{:S(2)}) async-start(bf16[16,1,64]{2,1,0:T(2,128)(2,1)} %copy.32), calls=%async_computation.2 | async-start | bytes 16384 | tf_op jit(solution)/shard_map/all_to_all | solution.py:124
  189.8 27.6 %all-to-all-start = ((bf16[16,64,2,256]{3,1,2,0:T(8,128)(2,1)}), bf16[16,64,2,256]{3,1,2,0:T(8,128)(2,1)S(1)}, u32[]{:S(2)}, u32[]{:S(2)}) async-start(bf16[16,64,2,256]{3,1,2,0:T(8,128)(2,1)} %bitcast_convert_fusion), calls=%async_computation.1 | async-start | bytes 2097152 | tf_op jit(solution)/shard_map/all_to_all | solution.py:117
Sparse Core Ops, SparseCore 0:
  9.5 30.6 all-gather.5
  155.5 30.6 reduce-scatter.1
where the time goes:
time: 228 us; the launch traced here: 226 us
  other arithmetic  84.7 us (37%)
  waiting for transfers between devices  63.4 us (28%)
  matrix products  25.8 us (11%)
  blocking collectives  23 us (10%)
  between operations  15 us (7%)
  starting transfers between devices  9.13 us (4%)
  local copies, waits for them, and re-layouts  5.36 us (2%)
    another operation x5, other arithmetic  74.6 us
    all_gather x1, waiting for transfers between devices, per_device(): lax.all_gather(images, 'orient', axis=0, tiled=True)  29 us
    all_to_all x1, waiting for transfers between devices, per_device(): lax.all_to_all(outgoing.astype(jnp.bfloat16), ('orient', 'img', 'brick'),...  19.7 us
    all_gather x2, blocking collectives, combined_all(): everything = jax.tree.map(lambda part: lax.all_gather(part, axis), array)  17.1 us
    reduce_scatter x1, waiting for transfers between devices, per_device(): lax.psum_scatter(weighted.astype(jnp.bfloat16), ('img', 'brick'), scatter...  14.1 us
    dot_general x1, matrix products, per_device(): lax.dot_general(posterior, shifted, (((0,), (0,)), ((), ())), preferred_e...  10.1 us
    dot_general x1, matrix products, per_device(): lax.dot_general(shifted, slices, (((1,), (1,)), ((), ())), preferred_elem...  8.94 us
    unnamed x1, blocking collectives  5.85 us
  transfers between devices with their start and end apart: 4, of which 3 were waited for; matrix products, arithmetic and copies ran while one was open for 7% of the time, Pallas kernels for 0%

commit v1 on v0

v1 whole, which is shorter than its diff:
```python
import functools

import jax
import jax.numpy as jnp
import numpy as np
from jax import lax
from jax.experimental import pallas as pl
from jax.experimental.pallas import tpu as pltpu
from jax.sharding import PartitionSpec as P

SHIFTS = 16
SEG = 256
NSEG = 8
K = SEG * NSEG
LANES = 128

frame_side = 64
interp_bits = 4
interp_scale = 1.0 / 256.0
PAIRS = SHIFTS // 2


def phase_tables():
    coef = np.arange(K)
    u = coef % frame_side - frame_side // 2
    w = coef // frame_side
    shift = np.arange(PAIRS)
    dx = 2 * (shift % 4) - 3
    dy = 2 * (shift // 4) - 3
    angle = (u[None, :] * dx[:, None] + w[None, :] * dy[:, None]) % (2 * frame_side)
    angle = angle * (2.0 * np.pi / (2 * frame_side))
    return np.cos(angle).astype(np.float32), np.sin(angle).astype(np.float32)


def cos_sin(steps):
    centred = jnp.bitwise_and(steps + frame_side, 2 * frame_side - 1) - frame_side
    x = centred.astype(jnp.float32) * (np.pi / frame_side)
    x2 = x * x
    c = jnp.full_like(x, (-1.0) ** 10 / float(np.prod(np.arange(1.0, 21.0))))
    s = jnp.full_like(x, (-1.0) ** 10 / float(np.prod(np.arange(1.0, 22.0))))
    for k in range(9, -1, -1):
        c = c * x2 + (-1.0) ** k / float(np.prod(np.arange(1.0, 2 * k + 1.0)))
        s = s * x2 + (-1.0) ** k / float(np.prod(np.arange(1.0, 2 * k + 2.0)))
    return c, s * x


def norm_kernel(slices_ref, out_ref):
    orient = slices_ref.shape[0]
    total = jnp.zeros((orient, LANES), jnp.float32)
    for k in range(2 * K // LANES):
        piece = slices_ref[:, k * LANES : (k + 1) * LANES].astype(jnp.float32)
        total = total + piece * piece
    ones = jnp.ones((8, LANES), jnp.float32)
    out_ref[...] = 0.5 * lax.dot_general(
        ones,
        total,
        (((1,), (1,)), ((), ())),
        precision=lax.Precision.HIGHEST,
        preferred_element_type=jnp.float32,
    )


def interp_kernel(interp_ref, weight_ref, cover_ref):
    raw = interp_ref[0, 0]
    high = jnp.right_shift(raw, interp_bits)
    low = jnp.bitwise_and(raw, (1 << interp_bits) - 1)
    vox = raw.shape[1]
    weight_ref[:, :vox] = high.astype(jnp.float32).astype(jnp.bfloat16)
    weight_ref[:, vox:] = low.astype(jnp.float32).astype(jnp.bfloat16)
    total = jnp.sum(raw.astype(jnp.float32), axis=0, keepdims=True)
    cover_ref[0] = total * interp_scale


def score_kernel(
    first, where_ref, images_ref, offsets_ref, slices_ref, norm_ref, cos_ref, sin_ref, *rest
):
    if first:
        terms_ref, based_ref, stats_ref, left_ref = rest
    else:
        _, _, stats_in_ref, terms_ref, based_ref, stats_ref, left_ref = rest
    inv_noise = 100.0 / K
    rows = images_ref.shape[0]
    off = 2 * offsets_ref[...] - 1
    off_x, off_y = off[:, 0:1], off[:, 1:2]
    lane = lax.broadcasted_iota(jnp.int32, (rows, LANES), 1)
    u = jnp.bitwise_and(lane, frame_side - 1) - frame_side // 2
    half = jnp.right_shift(lane, 6)
    c1, s1 = cos_sin(u * off_x + half * off_y)
    c2, s2 = cos_sin(2 * lane * off_y)
    for k in range(K // LANES):
        re_at = slice(k * LANES, (k + 1) * LANES)
        im_at = slice(K + k * LANES, K + (k + 1) * LANES)
        x_re = images_ref[:, re_at].astype(jnp.float32)
        x_im = images_ref[:, im_at].astype(jnp.float32)
        ck, sk = c2[:, k : k + 1], s2[:, k : k + 1]
        cb = c1 * ck - s1 * sk
        sb = s1 * ck + c1 * sk
        y_re = x_re * cb + x_im * sb
        y_im = x_im * cb - x_re * sb
        based_ref[:, re_at] = y_re.astype(jnp.bfloat16)
        based_ref[:, im_at] = y_im.astype(jnp.bfloat16)
        re_rows, im_rows = [], []
        for t in range(PAIRS):
            cos_t = cos_ref[t : t + 1, re_at]
            sin_t = sin_ref[t : t + 1, re_at]
            re_rows += [y_re * cos_t, y_im * sin_t]
            im_rows += [y_im * cos_t, -(y_re * sin_t)]
        left_ref[:, re_at] = jnp.concatenate(re_rows, axis=0).astype(jnp.bfloat16)
        left_ref[:, im_at] = jnp.concatenate(im_rows, axis=0).astype(jnp.bfloat16)
    both = lax.dot_general(
        left_ref[...],
        slices_ref[...],
        (((1,), (1,)), ((), ())),
        preferred_element_type=jnp.float32,
    )
    norm = norm_ref[0:1, :]
    scores = []
    for t in range(PAIRS):
        even = both[2 * t * rows : (2 * t + 1) * rows] - norm
        odd = both[(2 * t + 1) * rows : (2 * t + 2) * rows]
        scores += [inv_noise * (even + odd), inv_noise * (even - odd)]
    top = scores[0]
    for s in scores[1:]:
        top = jnp.maximum(top, s)
    top = jnp.max(top, axis=1, keepdims=True)
    mass = jnp.zeros_like(scores[0])
    for i, s in enumerate(scores):
        term = jnp.exp(s - top)
        mass = mass + term
        terms_ref[i] = term.astype(jnp.bfloat16)
    mass = jnp.sum(mass, axis=1, keepdims=True)
    count = stats_ref.shape[1]
    row = lax.broadcasted_iota(jnp.int32, (rows, count), 0)
    col = lax.broadcasted_iota(jnp.int32, (rows, count), 1)
    mine = col == row + where_ref[0] * rows
    top_row = jnp.sum(jnp.where(mine, top, 0.0), axis=0, keepdims=True)
    mass_row = jnp.sum(jnp.where(mine, mass, 0.0), axis=0, keepdims=True)
    which = lax.broadcasted_iota(jnp.int32, (8, count), 0)
    part = jnp.where(which == 0, top_row, jnp.where(which == 1, mass_row, 0.0))
    stats_ref[...] = part if first else part + stats_in_ref[...]


def brick_kernel(others, bricks, terms_ref, based_ref, seg_ref, cos_ref, sin_ref, *rest):
    stats_refs, (out_ref, pairs_ref) = rest[:others], rest[others:]
    count = based_ref.shape[0]
    orient = terms_ref.shape[2]
    own_top = stats_refs[0][0:1, :]
    top = own_top
    for ref in stats_refs[1:]:
        top = jnp.maximum(top, ref[0:1, :])
    mass = jnp.zeros_like(top)
    for ref in stats_refs:
        mass = mass + ref[1:2, :] * jnp.exp(ref[0:1, :] - top)
    factor = jnp.exp(own_top - top) / mass
    brick = lax.broadcasted_iota(jnp.int32, (bricks, orient), 0)
    hit = jnp.concatenate(
        [(brick == seg_ref[j : j + 1, :]).astype(jnp.float32) for j in range(NSEG)], axis=0
    ).astype(jnp.bfloat16)
    mass_sum = jnp.zeros((NSEG * bricks, count), jnp.float32)
    for t in range(PAIRS):
        plus, minus = (
            lax.dot_general(
                hit,
                terms_ref[2 * t + i],
                (((1,), (1,)), ((), ())),
                preferred_element_type=jnp.float32,
            )
            for i in range(2)
        )
        even = (plus + minus) * factor
        odd = (plus - minus) * factor
        mass_sum = mass_sum + even
        for j in range(NSEG):
            at = slice(j * bricks, (j + 1) * bricks)
            pairs_ref[j, t * bricks : (t + 1) * bricks, :] = even[at].astype(jnp.bfloat16)
            pairs_ref[j, (PAIRS + t) * bricks : (PAIRS + t + 1) * bricks, :] = odd[at].astype(
                jnp.bfloat16
            )
    mass_sum = jnp.sum(mass_sum, axis=1, keepdims=True)
    mass_high = mass_sum.astype(jnp.bfloat16).astype(jnp.float32)
    mass_low = mass_sum - mass_high
    lane = lax.broadcasted_iota(jnp.int32, (bricks, LANES), 1)
    tail = jnp.zeros((bricks, LANES), jnp.float32)
    for j in range(NSEG):
        at = slice(j * bricks, (j + 1) * bricks)
        tail = jnp.where(lane == j, mass_high[at], tail)
        tail = jnp.where(lane == NSEG + j, mass_low[at], tail)
        re_at = slice(j * SEG, (j + 1) * SEG)
        im_at = slice(K + j * SEG, K + (j + 1) * SEG)
        left = pairs_ref[j]
        with_re = jnp.dot(left, based_ref[:, re_at], preferred_element_type=jnp.float32)
        with_im = jnp.dot(left, based_ref[:, im_at], preferred_element_type=jnp.float32)
        sum_re = jnp.zeros((bricks, SEG), jnp.float32)
        sum_im = jnp.zeros((bricks, SEG), jnp.float32)
        for t in range(PAIRS):
            cos_t = cos_ref[t : t + 1, re_at]
            sin_t = sin_ref[t : t + 1, re_at]
            even = slice(t * bricks, (t + 1) * bricks)
            odd = slice((PAIRS + t) * bricks, (PAIRS + t + 1) * bricks)
            sum_re = sum_re + cos_t * with_re[even] + sin_t * with_im[odd]
            sum_im = sum_im + cos_t * with_im[even] - sin_t * with_re[odd]
        out_ref[:, re_at] = sum_re.astype(jnp.bfloat16)
        out_ref[:, im_at] = sum_im.astype(jnp.bfloat16)
    out_ref[:, 2 * K :] = tail.astype(jnp.bfloat16)


def final_kernel(arrived_ref, weight_ref, cover_ref, values_ref, mass_ref):
    vox = cover_ref.shape[2]
    total = jnp.sum(arrived_ref[...].astype(jnp.float32), axis=0, keepdims=True)
    re, im = total[:, :K], total[:, K : 2 * K]
    seg_mass = total[:, 2 * K :]
    parts = []
    for _ in range(3):
        high = [x.astype(jnp.bfloat16).astype(jnp.float32) for x in (re, im)]
        parts += high
        re, im = re - high[0], im - high[1]
    left = jnp.concatenate(parts + [jnp.zeros_like(re)] * 2, axis=0).astype(jnp.bfloat16)
    product = jnp.dot(left, weight_ref[...], preferred_element_type=jnp.float32)
    product = product[0:2] + product[2:4] + product[4:6]
    values_ref[0] = (product[:, :vox] * float(1 << interp_bits) + product[:, vox:]) * interp_scale
    weight = jnp.zeros((1, vox), jnp.float32)
    for j in range(NSEG):
        mass_j = seg_mass[:, j : j + 1] + seg_mass[:, NSEG + j : NSEG + j + 1]
        weight = weight + mass_j * cover_ref[j]
    mass_ref[0] = weight


def per_device(images, offsets, slices, seg_map, interp):
    orient_count = lax.axis_size("orient")
    group_count = lax.axis_size("img") * lax.axis_size("brick")
    group_index = lax.axis_index("img") * lax.axis_size("brick") + lax.axis_index("brick")
    plane = lax.axis_index("orient")
    bricks = orient_count * group_count
    rows = images.shape[0]
    orient = slices.shape[0]
    count = rows * orient_count
    vox = interp.shape[3]
    cos_table, sin_table = (jnp.asarray(t) for t in phase_tables())

    arrived = [images] + [
        lax.ppermute(
            images, "orient", [(i, (i + k) % orient_count) for i in range(orient_count)]
        )
        for k in range(1, orient_count)
    ]

    norm = pl.pallas_call(
        norm_kernel,
        out_shape=jax.ShapeDtypeStruct((8, orient), jnp.float32),
        name="norms",
    )(slices)
    weights, cover = pl.pallas_call(
        interp_kernel,
        grid=(NSEG,),
        in_specs=[pl.BlockSpec((1, 1, SEG, vox), lambda j: (0, j, 0, 0))],
        out_specs=[
            pl.BlockSpec((SEG, 2 * vox), lambda j: (j, 0)),
            pl.BlockSpec((1, 1, vox), lambda j: (j, 0, 0)),
        ],
        out_shape=[
            jax.ShapeDtypeStruct((NSEG * SEG, 2 * vox), jnp.bfloat16),
            jax.ShapeDtypeStruct((NSEG, 1, vox), jnp.float32),
        ],
        name="weights",
    )(interp)

    def whole(shape):
        return pl.BlockSpec(shape, lambda i, where: (0,) * len(shape))

    state = ()
    for k in range(orient_count):
        source = (plane - k) % orient_count
        where = jnp.stack([source, source * group_count + group_index]).astype(jnp.int32)
        first = k == 0
        state_shapes = [
            jax.ShapeDtypeStruct((SHIFTS, count, orient), jnp.bfloat16),
            jax.ShapeDtypeStruct((count, 2 * K), jnp.bfloat16),
            jax.ShapeDtypeStruct((8, count), jnp.float32),
        ]
        state = pl.pallas_call(
            functools.partial(score_kernel, first),
            grid_spec=pltpu.PrefetchScalarGridSpec(
                num_scalar_prefetch=1,
                grid=(1,),
                in_specs=[
                    whole((rows, 2 * K)),
                    pl.BlockSpec((rows, 2), lambda i, where: (where[1], 0)),
                    whole((orient, 2 * K)),
                    whole((8, orient)),
                    whole((PAIRS, K)),
                    whole((PAIRS, K)),
                ]
                + (
                    []
                    if first
                    else [
                        pl.BlockSpec(memory_space=pl.ANY),
                        pl.BlockSpec(memory_space=pl.ANY),
                        whole((8, count)),
                    ]
                ),
                out_specs=[
                    pl.BlockSpec((SHIFTS, rows, orient), lambda i, where: (0, where[0], 0)),
                    pl.BlockSpec((rows, 2 * K), lambda i, where: (where[0], 0)),
                    whole((8, count)),
                ],
                scratch_shapes=[pltpu.VMEM((SHIFTS * rows, 2 * K), jnp.bfloat16)],
            ),
            out_shape=state_shapes,
            input_output_aliases={} if first else {7: 0, 8: 1, 9: 2},
            name="scores",
        )(where, arrived[k], offsets, slices, norm, cos_table, sin_table, *state)
    terms, based, stats = state

    everyone = [stats] + [
        lax.ppermute(stats, "orient", [(i, (i + k) % orient_count) for i in range(orient_count)])
        for k in range(1, orient_count)
    ]
    own_map = lax.dynamic_slice_in_dim(
        seg_map.reshape(orient_count * orient, NSEG), plane * orient, orient, 0
    ).T
    outgoing = pl.pallas_call(
        functools.partial(brick_kernel, orient_count, bricks),
        out_shape=jax.ShapeDtypeStruct((bricks, 2 * K + LANES), jnp.bfloat16),
        scratch_shapes=[pltpu.VMEM((NSEG, SHIFTS * bricks, count), jnp.bfloat16)],
        name="bricks",
    )(terms, based, own_map, cos_table, sin_table, *everyone)
    received = lax.all_to_all(
        outgoing, ("orient", "img", "brick"), split_axis=0, concat_axis=0, tiled=True
    )
    return pl.pallas_call(
        final_kernel,
        out_shape=[
            jax.ShapeDtypeStruct((1, 2, vox), jnp.float32),
            jax.ShapeDtypeStruct((1, 1, vox), jnp.float32),
        ],
        name="insert",
    )(received, weights, cover)


def solution(mesh):
    placed = (
        P(("groups", "orient", "img", "brick"), None),
        P("groups", None),
        P(("groups", "orient"), None),
        P(),
        P(("orient", "img", "brick"), None, None, None),
    )

    def device(*args):
        values, weight = per_device(*args)
        return values, weight.reshape(1, -1)

    return jax.shard_map(
        device,
        mesh=mesh,
        in_specs=placed,
        out_specs=(
            P(("groups", "orient", "img", "brick"), None, None),
            P(("groups", "orient", "img", "brick"), None),
        ),
        check_vma=False,
    )
```

time: 228 us -> 72.7 us (0.32)
  other arithmetic: 84.7 us -> 4.68 us
  waiting for transfers between devices: 63.4 us -> 3.04 us
  Pallas kernels: 0 us -> 35.1 us
  matrix products: 25.8 us -> 0 us
  blocking collectives: 23 us -> 0 us
  between operations: 15 us -> 0.71 us
  starting transfers between devices: 9.13 us -> 20.7 us
  local copies, waits for them, and re-layouts: 5.36 us -> 7.84 us
    another operation x5 -> x4, other arithmetic: 74.6 us -> 2.46 us  [per_device(): jnp.stack([source, source * group_count + group_index]).astype(jnp.int32)]
    pallas_call x0 -> x8, Pallas kernels: none -> 35.1 us  [the longest x4 20.6 us: per_device(): pl.pallas_call(functools.partial(score_kernel, first), grid_spec=pltpu.Pr...]
    all_gather x1 -> x0, waiting for transfers between devices: 29 us -> none  [per_device(): lax.all_gather(images, 'orient', axis=0, tiled=True)]
    dot_general x9 -> x0, matrix products: 25.8 us -> none  [the longest x1 10.1 us: per_device(): lax.dot_general(posterior, shifted, (((0,), (0,)), ((), ())), preferred_e...]
    all_to_all x2 -> x1, waiting for transfers between devices: 19.7 us -> 2.18 us  [per_device(): lax.all_to_all(outgoing, ('orient', 'img', 'brick'), split_axis=0, concat...]
    all_gather x2 -> x0, blocking collectives: 17.1 us -> none  [combined_all(): everything = jax.tree.map(lambda part: lax.all_gather(part, axis), array)]
    ppermute x0 -> x6, starting transfers between devices: none -> 14.3 us  [the longest x3 7.23 us: per_device(): lax.ppermute(stats, 'orient', [(i, (i + k) % orient_count) for i in range...]
    reduce_scatter x1 -> x0, waiting for transfers between devices: 14.1 us -> none  [per_device(): lax.psum_scatter(weighted.astype(jnp.bfloat16), ('img', 'brick'), scatter...]
  transfers between devices with their start and end apart: 4 -> 7, of which waited for: 3 -> 2; matrix products, arithmetic and copies ran while one was open for 7% -> 8% of each run, Pallas kernels for 0% -> 33%
where the time goes in v1:
time: 72.7 us; the launch traced here: 72.1 us
  Pallas kernels  35.1 us (48%)
  starting transfers between devices  20.7 us (28%)
  local copies, waits for them, and re-layouts  7.84 us (11%)
  other arithmetic  4.68 us (6%)
  waiting for transfers between devices  3.04 us (4%)
    pallas_call x4, Pallas kernels, per_device(): pl.pallas_call(functools.partial(score_kernel, first), grid_spec=pltpu.Pr...  20.6 us
    ppermute x3, starting transfers between devices, per_device(): lax.ppermute(stats, 'orient', [(i, (i + k) % orient_count) for i in range...  7.23 us
    ppermute x3, starting transfers between devices, per_device(): lax.ppermute(images, 'orient', [(i, (i + k) % orient_count) for i in rang...  7.04 us
    unnamed x20, local copies, waits for them, and re-layouts  7.02 us
    all_to_all x1, starting transfers between devices, per_device(): lax.all_to_all(outgoing, ('orient', 'img', 'brick'), split_axis=0, concat...  6.39 us
    pallas_call x1, Pallas kernels, per_device(): pl.pallas_call(interp_kernel, grid=(NSEG,), in_specs=[pl.BlockSpec((1, 1,...  5.85 us
    pallas_call x1, Pallas kernels, per_device(): pl.pallas_call(functools.partial(brick_kernel, orient_count, bricks), out...  3.3 us
    pallas_call x1, Pallas kernels, per_device(): pl.pallas_call(norm_kernel, out_shape=jax.ShapeDtypeStruct((8, orient), j...  2.79 us
  transfers between devices with their start and end apart: 7, of which 2 were waited for; matrix products, arithmetic and copies ran while one was open for 8% of the time, Pallas kernels for 33%

profile of v1, /device:TPU:0, one launch (start us, length us, event | category | flops | bytes accessed | tf_op | source)
XLA Modules:
  0.0 72.1 jit_solution(6770751167031878295)
XLA Ops:
  0.6 0.0 copy-start.3
  0.6 3.1 %collective-permute-start.2 = (bf16[32,4096]{1,0:T(8,128)(2,1)}, bf16[32,4096]{1,0:T(8,128)(2,1)S(1)}, u32[]{:S(2)}, u32[]{:S(2)}) collective-permute-start(bf16[32,4096]{1,0:T(8,128)(2,1)} %images_ref.1), channel_id=1, source_target_pairs={{0,4},{4,8},{8,12},{12,0},{1,5},{5,9},{9,13},{13,1},{2,6},{6,10},{... | collective-permute-start | bytes 786440 | tf_op jit(solution)/shard_map/ppermute | solution.py:241
  3.7 2.6 %collective-permute-start.1 = (bf16[32,4096]{1,0:T(8,128)(2,1)}, bf16[32,4096]{1,0:T(8,128)(2,1)S(1)}, u32[]{:S(2)}, u32[]{:S(2)}) collective-permute-start(bf16[32,4096]{1,0:T(8,128)(2,1)} %images_ref.1), channel_id=1, source_target_pairs={{0,8},{4,12},{8,0},{12,4},{1,9},{5,13},{9,1},{13,5},{2,10},{6,14},... | collective-permute-start | bytes 786440 | tf_op jit(solution)/shard_map/ppermute | solution.py:241
  6.3 1.3 %collective-permute-start = (bf16[32,4096]{1,0:T(8,128)(2,1)}, bf16[32,4096]{1,0:T(8,128)(2,1)S(1)}, u32[]{:S(2)}, u32[]{:S(2)}) collective-permute-start(bf16[32,4096]{1,0:T(8,128)(2,1)} %images_ref.1), channel_id=1, source_target_pairs={{0,12},{4,0},{8,4},{12,8},{1,13},{5,1},{9,5},{13,9},{2,14},{6,2},{... | collective-permute-start | bytes 786440 | tf_op jit(solution)/shard_map/ppermute | solution.py:241
  7.7 0.6 pad_add_fusion.3.where_ref
  8.3 0.6 pad_add_fusion.2.where_ref
  8.9 1.5 %copy.36.offsets_ref = s32[512,2]{1,0:T(8,128)} copy(s32[512,2]{0,1:T(2,128)} %param.8) | data formatting | bytes 8192 | tf_op args[1]
  10.5 2.8 %norms.1.norm_ref = f32[8,256]{1,0:T(8,128)} custom-call(bf16[256,4096]{1,0:T(8,128)(2,1)} %slices_ref.9), custom_call_target="tpu_custom_call" | custom-call | tf_op jit(solution)/shard_map/norms/pallas_call | solution.py:247
  13.3 0.5 broadcast.7
  13.8 0.0 copy-done.3
  13.8 0.6 reduce.3
  14.4 0.3 reshape.12
  14.7 5.1 %scores.4 = (bf16[16,128,256]{2,1,0:T(8,128)(2,1)}, bf16[128,4096]{1,0:T(8,128)(2,1)}, f32[8,128]{1,0:T(8,128)}) custom-call(s32[2]{0:T(128)} %pad_add_fusion.3.where_ref, bf16[32,4096]{1,0:T(8,128)(2,1)} %images_ref.1, s32[512,2]{1,0:T(8,128)} %copy.36.offsets_ref, bf16[256,4096]{1,0:T(8,128)(2,1)} %slices_ref.9, f32[8,256]{1,0:T(8,128)} %norms.1.norm_ref, ...), custom_call_target="tpu_custom_call" | custom-call | tf_op jit(solution)/shard_map/scores/pallas_call | solution.py:280
  19.8 0.6 pad_add_fusion.1.where_ref
  20.4 0.6 pad_add_fusion.where_ref
  21.1 0.0 collective-permute-done.2.images_ref
  21.1 0.0 copy-start.2
  21.1 0.7 copy-done.2
  21.8 5.2 %scores.5 = (bf16[16,128,256]{2,1,0:T(8,128)(2,1)}, bf16[128,4096]{1,0:T(8,128)(2,1)}, f32[8,128]{1,0:T(8,128)}) custom-call(s32[2]{0:T(128)} %pad_add_fusion.2.where_ref, bf16[32,4096]{1,0:T(8,128)(2,1)} %copy-done.2, s32[512,2]{1,0:T(8,128)} %copy.36.offsets_ref, ...), custom_call_target="tpu_custom_call", output_to_operand_aliasing={{0}: (7, {}), {1}: (8, {}), {2}: (9, {})} | custom-call | tf_op jit(solution)/shard_map/scores/pallas_call | solution.py:280
  26.9 0.0 collective-permute-done.1.images_ref
  26.9 0.0 copy-start.1
  26.9 0.7 copy-done.1
  27.6 5.2 %scores.6 = (bf16[16,128,256]{2,1,0:T(8,128)(2,1)}, bf16[128,4096]{1,0:T(8,128)(2,1)}, f32[8,128]{1,0:T(8,128)}) custom-call(s32[2]{0:T(128)} %pad_add_fusion.1.where_ref, bf16[32,4096]{1,0:T(8,128)(2,1)} %copy-done.1, s32[512,2]{1,0:T(8,128)} %copy.36.offsets_ref, ...), custom_call_target="tpu_custom_call", output_to_operand_aliasing={{0}: (7, {}), {1}: (8, {}), {2}: (9, {})} | custom-call | tf_op jit(solution)/shard_map/scores/pallas_call | solution.py:280
  32.8 0.0 collective-permute-done.images_ref
  32.8 0.0 copy-start
  32.8 0.7 copy-done
  33.5 5.2 %scores.7 = (bf16[16,128,256]{2,1,0:T(8,128)(2,1)}, bf16[128,4096]{1,0:T(8,128)(2,1)}, f32[8,128]{1,0:T(8,128)}) custom-call(s32[2]{0:T(128)} %pad_add_fusion.where_ref, bf16[32,4096]{1,0:T(8,128)(2,1)} %copy-done, s32[512,2]{1,0:T(8,128)} %copy.36.offsets_ref, ...), custom_call_target="tpu_custom_call", output_to_operand_aliasing={{0}: (7, {}), {1}: (8, {}), {2}: (9, {})} | custom-call | tf_op jit(solution)/shard_map/scores/pallas_call | solution.py:280
  38.7 2.5 %collective-permute-start.3 = (f32[8,128]{1,0:T(8,128)}, f32[8,128]{1,0:T(8,128)S(1)}, u32[]{:S(2)}, u32[]{:S(2)}) collective-permute-start(f32[8,128]{1,0:T(8,128)} %get-tuple-element.29.rest_0_), channel_id=1, source_target_pairs={{0,4},{4,8},{8,12},{12,0},{1,5},{5,9},{9,13},{13,1},{2,6},{6,10},{... | collective-permute-start | bytes 12296 | tf_op jit(solution)/shard_map/ppermute | solution.py:316
  41.2 1.9 %collective-permute-start.4 = (f32[8,128]{1,0:T(8,128)}, f32[8,128]{1,0:T(8,128)S(1)}, u32[]{:S(2)}, u32[]{:S(2)}) collective-permute-start(f32[8,128]{1,0:T(8,128)} %get-tuple-element.29.rest_0_), channel_id=1, source_target_pairs={{0,8},{4,12},{8,0},{12,4},{1,9},{5,13},{9,1},{13,5},{2,10},{6,14},... | collective-permute-start | bytes 12296 | tf_op jit(solution)/shard_map/ppermute | solution.py:316
  43.1 2.8 %collective-permute-start.5 = (f32[8,128]{1,0:T(8,128)}, f32[8,128]{1,0:T(8,128)S(1)}, u32[]{:S(2)}, u32[]{:S(2)}) collective-permute-start(f32[8,128]{1,0:T(8,128)} %get-tuple-element.29.rest_0_), channel_id=1, source_target_pairs={{0,12},{4,0},{8,4},{12,8},{1,13},{5,1},{9,5},{13,9},{2,14},{6,2},{... | collective-permute-start | bytes 12296 | tf_op jit(solution)/shard_map/ppermute | solution.py:316
  45.9 0.7 copy.40
  46.6 0.0 collective-permute-done.3.rest_1_
  46.6 0.0 collective-permute-done.4.rest_2_
  46.6 0.0 copy-start.5
  46.6 0.8 %collective-permute-done.5.rest_3_ = f32[8,128]{1,0:T(8,128)S(1)} collective-permute-done((f32[8,128]{1,0:T(8,128)}, f32[8,128]{1,0:T(8,128)S(1)}, u32[]{:S(2)}, u32[]{:S(2)}) %collective-permute-start.5) | collective-permute-done | bytes 4128 | tf_op jit(solution)/shard_map/ppermute | solution.py:316
  47.4 0.0 copy-done.4
  47.4 0.0 copy-done.5
  47.4 0.6 copy-done.6
  48.0 3.3 %bricks.1 = bf16[16,4224]{1,0:T(8,128)(2,1)} custom-call(bf16[16,128,256]{2,1,0:T(8,128)(2,1)} %get-tuple-element.27.terms_ref, bf16[128,4096]{1,0:T(8,128)(2,1)} %get-tuple-element.28.based_ref, s32[8,256]{1,0:T(8,128)} %bitcast.17, f32[8,2048]{1,0:T(8,128)} %constant.55.clone.cos_ref, f32[8,2048]{1,0:T(8,128)} %constant.56.clone.sin_ref, ...), custom_call_target="tpu_custom_call" | custom-call | tf_op jit(solution)/shard_map/bricks/pallas_call | solution.py:322
  51.3 0.5 broadcast.8
  51.8 1.6 %reduce.4 = bf16[16,4224]{1,0:T(8,128)(2,1)S(1)} reduce(bf16[16,1,4224]{2,0,1:T(8,128)(2,1)} %bitcast.16, bf16[]{:T(256)} %broadcast.8), dimensions={1}, to_apply=%copy.38.reduce_sub_computation | reduce | bytes 270338 | tf_op jit(solution)/shard_map/all_to_all | solution.py:328
  53.4 0.8 %reshape.23 = bf16[16,2,2112]{2,1,0:T(2,128)(2,1)} reshape(bf16[16,4224]{1,0:T(8,128)(2,1)S(1)} %reduce.4) | data formatting | bytes 270336
  54.2 6.4 %all-to-all-start = ((bf16[16,2,2112]{2,1,0:T(2,128)(2,1)}), bf16[16,2,2112]{2,1,0:T(2,128)(2,1)S(1)}, u32[]{:S(2)}, u32[]{:S(2)}) async-start(bf16[16,2,2112]{2,1,0:T(2,128)(2,1)} %reshape.23), calls=%async_computation | async-start | bytes 278528 | tf_op jit(solution)/shard_map/all_to_all | solution.py:328
  60.6 5.9 %weights.1 = (bf16[2048,512]{1,0:T(8,128)(2,1)}, f32[8,1,256]{2,1,0:T(1,128)}) custom-call(s32[1,8,256,256]{3,2,1,0:T(8,128)} %interp_ref.1), custom_call_target="tpu_custom_call" | custom-call | tf_op jit(solution)/shard_map/weights/pallas_call | solution.py:252
  66.5 2.2 %all-to-all-done = bf16[16,2,2112]{2,1,0:T(2,128)(2,1)S(1)} async-done(((bf16[16,2,2112]{2,1,0:T(2,128)(2,1)}), bf16[16,2,2112]{2,1,0:T(2,128)(2,1)S(1)}, u32[]{:S(2)}, u32[]{:S(2)}) %all-to-all-start) | async-done | bytes 135200 | tf_op jit(solution)/shard_map/all_to_all | solution.py:328
  68.7 0.1 reshape.24
  68.8 0.7 copy.42
  69.5 2.6 %insert.1 = (f32[1,2,256]{2,1,0:T(2,128)}, f32[1,1,256]{2,1,0:T(1,128)}) custom-call(bf16[16,4224]{1,0:T(8,128)(2,1)} %bitcast.15, bf16[2048,512]{1,0:T(8,128)(2,1)} %get-tuple-element.30.weight_ref, f32[8,1,256]{2,1,0:T(1,128)} %get-tuple-element.31.cover_ref), custom_call_target="tpu_custom_call" | custom-call | tf_op jit(solution)/shard_map/insert/pallas_call | solution.py:331
  (3 shorter events, 0.0 us)
Async XLA Ops:
  0.6 13.1 %copy-start.3 = (s32[8192,1]{0,1:T(1,128)S(1)}, s32[8192,1]{0,1:T(1,128)}, u32[]{:S(2)}) copy-start(s32[8192,1]{0,1:T(1,128)} %param.10) | copy-start | bytes 98308
  0.6 20.4 %collective-permute-start.2 = (bf16[32,4096]{1,0:T(8,128)(2,1)}, bf16[32,4096]{1,0:T(8,128)(2,1)S(1)}, u32[]{:S(2)}, u32[]{:S(2)}) collective-permute-start(bf16[32,4096]{1,0:T(8,128)(2,1)} %images_ref.1), channel_id=1, source_target_pairs={{0,4},{4,8},{8,12},{12,0},{1,5},{5,9},{9,13},{13,1},{2,6},{6,10},{... | collective-permute-start | bytes 786440 | tf_op jit(solution)/shard_map/ppermute | solution.py:241
  3.7 23.2 %collective-permute-start.1 = (bf16[32,4096]{1,0:T(8,128)(2,1)}, bf16[32,4096]{1,0:T(8,128)(2,1)S(1)}, u32[]{:S(2)}, u32[]{:S(2)}) collective-permute-start(bf16[32,4096]{1,0:T(8,128)(2,1)} %images_ref.1), channel_id=1, source_target_pairs={{0,8},{4,12},{8,0},{12,4},{1,9},{5,13},{9,1},{13,5},{2,10},{6,14},... | collective-permute-start | bytes 786440 | tf_op jit(solution)/shard_map/ppermute | solution.py:241
  6.3 26.5 %collective-permute-start = (bf16[32,4096]{1,0:T(8,128)(2,1)}, bf16[32,4096]{1,0:T(8,128)(2,1)S(1)}, u32[]{:S(2)}, u32[]{:S(2)}) collective-permute-start(bf16[32,4096]{1,0:T(8,128)(2,1)} %images_ref.1), channel_id=1, source_target_pairs={{0,12},{4,0},{8,4},{12,8},{1,13},{5,1},{9,5},{13,9},{2,14},{6,2},{... | collective-permute-start | bytes 786440 | tf_op jit(solution)/shard_map/ppermute | solution.py:241
  21.1 0.7 copy-start.2
  26.9 0.7 copy-start.1
  32.8 0.7 copy-start
  38.7 7.9 %collective-permute-start.3 = (f32[8,128]{1,0:T(8,128)}, f32[8,128]{1,0:T(8,128)S(1)}, u32[]{:S(2)}, u32[]{:S(2)}) collective-permute-start(f32[8,128]{1,0:T(8,128)} %get-tuple-element.29.rest_0_), channel_id=1, source_target_pairs={{0,4},{4,8},{8,12},{12,0},{1,5},{5,9},{9,13},{13,1},{2,6},{6,10},{... | collective-permute-start | bytes 12296 | tf_op jit(solution)/shard_map/ppermute | solution.py:316
  41.2 5.4 %collective-permute-start.4 = (f32[8,128]{1,0:T(8,128)}, f32[8,128]{1,0:T(8,128)S(1)}, u32[]{:S(2)}, u32[]{:S(2)}) collective-permute-start(f32[8,128]{1,0:T(8,128)} %get-tuple-element.29.rest_0_), channel_id=1, source_target_pairs={{0,8},{4,12},{8,0},{12,4},{1,9},{5,13},{9,1},{13,5},{2,10},{6,14},... | collective-permute-start | bytes 12296 | tf_op jit(solution)/shard_map/ppermute | solution.py:316
  43.1 4.4 %collective-permute-start.5 = (f32[8,128]{1,0:T(8,128)}, f32[8,128]{1,0:T(8,128)S(1)}, u32[]{:S(2)}, u32[]{:S(2)}) collective-permute-start(f32[8,128]{1,0:T(8,128)} %get-tuple-element.29.rest_0_), channel_id=1, source_target_pairs={{0,12},{4,0},{8,4},{12,8},{1,13},{5,1},{9,5},{13,9},{2,14},{6,2},{... | collective-permute-start | bytes 12296 | tf_op jit(solution)/shard_map/ppermute | solution.py:316
  46.6 0.9 %copy-start.4 = (f32[8,128]{1,0:T(8,128)}, f32[8,128]{1,0:T(8,128)S(1)}, u32[]{:S(2)}) copy-start(f32[8,128]{1,0:T(8,128)S(1)} %collective-permute-done.3.rest_1_) | copy-start | bytes 12292
  46.6 0.9 %copy-start.5 = (f32[8,128]{1,0:T(8,128)}, f32[8,128]{1,0:T(8,128)S(1)}, u32[]{:S(2)}) copy-start(f32[8,128]{1,0:T(8,128)S(1)} %collective-permute-done.4.rest_2_) | copy-start | bytes 12292
  47.4 0.6 copy-start.6
  54.2 14.4 %all-to-all-start = ((bf16[16,2,2112]{2,1,0:T(2,128)(2,1)}), bf16[16,2,2112]{2,1,0:T(2,128)(2,1)S(1)}, u32[]{:S(2)}, u32[]{:S(2)}) async-start(bf16[16,2,2112]{2,1,0:T(2,128)(2,1)} %reshape.23), calls=%async_computation | async-start | bytes 278528 | tf_op jit(solution)/shard_map/all_to_all | solution.py:328

commit v2 on v1

v2 whole, which is shorter than its diff:
```python
import functools

import jax
import jax.numpy as jnp
import numpy as np
from jax import lax
from jax.experimental import pallas as pl
from jax.experimental.pallas import tpu as pltpu
from jax.sharding import PartitionSpec as P

SHIFTS = 16
SEG = 256
NSEG = 8
K = SEG * NSEG
LANES = 128

frame_side = 64
interp_bits = 4
interp_scale = 1.0 / 256.0
PAIRS = SHIFTS // 2


def phase_tables():
    coef = np.arange(K)
    u = coef % frame_side - frame_side // 2
    w = coef // frame_side
    shift = np.arange(PAIRS)
    dx = 2 * (shift % 4) - 3
    dy = 2 * (shift // 4) - 3
    angle = (u[None, :] * dx[:, None] + w[None, :] * dy[:, None]) % (2 * frame_side)
    angle = angle * (2.0 * np.pi / (2 * frame_side))
    return np.cos(angle).astype(np.float32), np.sin(angle).astype(np.float32)


def cos_sin(steps):
    centred = jnp.bitwise_and(steps + frame_side, 2 * frame_side - 1) - frame_side
    x = centred.astype(jnp.float32) * (np.pi / frame_side)
    x2 = x * x
    c = jnp.full_like(x, (-1.0) ** 10 / float(np.prod(np.arange(1.0, 21.0))))
    s = jnp.full_like(x, (-1.0) ** 10 / float(np.prod(np.arange(1.0, 22.0))))
    for k in range(9, -1, -1):
        c = c * x2 + (-1.0) ** k / float(np.prod(np.arange(1.0, 2 * k + 1.0)))
        s = s * x2 + (-1.0) ** k / float(np.prod(np.arange(1.0, 2 * k + 2.0)))
    return c, s * x


def setup_kernel(bricks, interp_ref, map_ref, weight_ref, cover_ref, hit_ref):
    vox = interp_ref.shape[3]
    covers = []
    for j in range(NSEG):
        raw = interp_ref[0, j]
        high = jnp.right_shift(raw, interp_bits).astype(jnp.float32)
        low = jnp.bitwise_and(raw, (1 << interp_bits) - 1).astype(jnp.float32)
        weight_ref[:, 2 * j * vox : (2 * j + 1) * vox] = high.astype(jnp.bfloat16)
        weight_ref[:, (2 * j + 1) * vox : (2 * j + 2) * vox] = low.astype(jnp.bfloat16)
        covers.append(jnp.sum(raw.astype(jnp.float32), axis=0, keepdims=True) * interp_scale)
    cover_ref[...] = jnp.concatenate(covers, axis=0)
    orient = hit_ref.shape[1]
    rows = orient * NSEG // LANES
    per_row = LANES // NSEG
    start = pl.multiple_of(lax.axis_index("orient") * rows, rows)
    entries = map_ref[pl.ds(start, rows), :].astype(jnp.float32)
    lane = lax.broadcasted_iota(jnp.int32, (rows, LANES), 1)
    masked = jnp.concatenate(
        [jnp.where(lane % NSEG == j, entries, 0.0) for j in range(NSEG)], axis=0
    )
    source = lax.broadcasted_iota(jnp.int32, (LANES, orient), 0) // NSEG
    target = lax.broadcasted_iota(jnp.int32, (LANES, orient), 1) % per_row
    spread = jnp.dot(
        masked,
        (source == target).astype(jnp.float32),
        precision=lax.Precision.HIGHEST,
        preferred_element_type=jnp.float32,
    )
    row = lax.broadcasted_iota(jnp.int32, (rows, orient), 0)
    own = lax.broadcasted_iota(jnp.int32, (rows, orient), 1) // per_row == row
    brick = lax.broadcasted_iota(jnp.int32, (bricks, orient), 0).astype(jnp.float32)
    hits = []
    for j in range(NSEG):
        named = jnp.where(own, spread[j * rows : (j + 1) * rows], 0.0)
        named = jnp.sum(named, axis=0, keepdims=True)
        hits.append((brick == named).astype(jnp.float32))
    hit_ref[...] = jnp.concatenate(hits, axis=0).astype(jnp.bfloat16)


def source_plane(source):
    kind, amount = source
    plane = lax.axis_index("orient")
    if kind == "xor":
        return jnp.bitwise_xor(plane, amount)
    count = lax.axis_size("orient")
    return lax.rem(plane + count - amount, count)


def score_kernel(first, source, choices, *refs):
    images_refs, refs = refs[:choices], refs[choices:]
    offsets_ref, slices_ref, cos_ref, sin_ref = refs[:4]
    if first:
        terms_ref, based_ref, stats_ref, norm_ref, left_ref = refs[4:]
    else:
        norm_ref, _, _, stats_in_ref, _ = refs[4:9]
        terms_ref, based_ref, stats_ref, left_ref = refs[9:]
    inv_noise = 100.0 / K
    rows = images_refs[0].shape[0]
    plane = source_plane(source)
    group = lax.axis_index("img") * lax.axis_size("brick") + lax.axis_index("brick")
    groups = lax.axis_size("img") * lax.axis_size("brick")
    count = offsets_ref.shape[1]
    row = lax.broadcasted_iota(jnp.int32, (rows, count), 0)
    col = lax.broadcasted_iota(jnp.int32, (rows, count), 1)
    mine = col == row + (plane * groups + group) * rows
    off = 2.0 * offsets_ref[...].astype(jnp.float32) - 1.0
    off_x, off_y = (
        jnp.sum(jnp.where(mine, off[i : i + 1, :], 0.0), axis=1, keepdims=True).astype(jnp.int32)
        for i in range(2)
    )
    if first:
        orient = slices_ref.shape[0]
        total = jnp.zeros((orient, LANES), jnp.float32)
        for k in range(2 * K // LANES):
            piece = slices_ref[:, k * LANES : (k + 1) * LANES].astype(jnp.float32)
            total = total + piece * piece
        norm_ref[...] = 0.5 * lax.dot_general(
            jnp.ones((8, LANES), jnp.float32),
            total,
            (((1,), (1,)), ((), ())),
            precision=lax.Precision.HIGHEST,
            preferred_element_type=jnp.float32,
        )
    lane = lax.broadcasted_iota(jnp.int32, (rows, LANES), 1)
    u = jnp.bitwise_and(lane, frame_side - 1) - frame_side // 2
    half = jnp.right_shift(lane, 6)
    c1, s1 = cos_sin(u * off_x + half * off_y)
    c2, s2 = cos_sin(2 * lane * off_y)
    at_end = (lax.axis_index("orient") == 0) | (
        lax.axis_index("orient") == lax.axis_size("orient") - 1
    )

    def pixels(at):
        if choices == 1:
            return images_refs[0][:, at].astype(jnp.float32)
        return jnp.where(at_end, images_refs[0][:, at], images_refs[1][:, at]).astype(jnp.float32)

    for k in range(K // LANES):
        re_at = slice(k * LANES, (k + 1) * LANES)
        im_at = slice(K + k * LANES, K + (k + 1) * LANES)
        x_re, x_im = pixels(re_at), pixels(im_at)
        ck, sk = c2[:, k : k + 1], s2[:, k : k + 1]
        cb = c1 * ck - s1 * sk
        sb = s1 * ck + c1 * sk
        y_re = x_re * cb + x_im * sb
        y_im = x_im * cb - x_re * sb
        where = pl.ds(pl.multiple_of(plane * rows, rows), rows)
        based_ref[where, re_at] = y_re.astype(jnp.bfloat16)
        based_ref[where, im_at] = y_im.astype(jnp.bfloat16)
        re_rows, im_rows = [], []
        for t in range(PAIRS):
            cos_t = cos_ref[t : t + 1, re_at]
            sin_t = sin_ref[t : t + 1, re_at]
            re_rows += [y_re * cos_t, y_im * sin_t]
            im_rows += [y_im * cos_t, -(y_re * sin_t)]
        left_ref[:, re_at] = jnp.concatenate(re_rows, axis=0).astype(jnp.bfloat16)
        left_ref[:, im_at] = jnp.concatenate(im_rows, axis=0).astype(jnp.bfloat16)
    both = lax.dot_general(
        left_ref[...],
        slices_ref[...],
        (((1,), (1,)), ((), ())),
        preferred_element_type=jnp.float32,
    )
    norm = norm_ref[0:1, :]
    scores = []
    for t in range(PAIRS):
        even = both[2 * t * rows : (2 * t + 1) * rows] - norm
        odd = both[(2 * t + 1) * rows : (2 * t + 2) * rows]
        scores += [inv_noise * (even + odd), inv_noise * (even - odd)]
    top = scores[0]
    for s in scores[1:]:
        top = jnp.maximum(top, s)
    top = jnp.max(top, axis=1, keepdims=True)
    mass = jnp.zeros_like(scores[0])
    for i, s in enumerate(scores):
        term = jnp.exp(s - top)
        mass = mass + term
        terms_ref[i, where, :] = term.astype(jnp.bfloat16)
    mass = jnp.sum(mass, axis=1, keepdims=True)
    count = stats_ref.shape[1]
    row = lax.broadcasted_iota(jnp.int32, (rows, count), 0)
    col = lax.broadcasted_iota(jnp.int32, (rows, count), 1)
    mine = col == row + plane * rows
    top_row = jnp.sum(jnp.where(mine, top, 0.0), axis=0, keepdims=True)
    mass_row = jnp.sum(jnp.where(mine, mass, 0.0), axis=0, keepdims=True)
    which = lax.broadcasted_iota(jnp.int32, (8, count), 0)
    part = jnp.where(which == 0, top_row, jnp.where(which == 1, mass_row, 0.0))
    stats_ref[...] = part if first else part + stats_in_ref[...]


def brick_kernel(others, terms_ref, based_ref, hit_ref, cos_ref, sin_ref, *rest):
    stats_refs, (out_ref, pairs_ref, sums_ref) = rest[:others], rest[others:]
    bricks = hit_ref.shape[0] // NSEG
    count = based_ref.shape[0]
    own_top = stats_refs[0][0:1, :]
    top = own_top
    for ref in stats_refs[1:]:
        top = jnp.maximum(top, ref[0:1, :])
    mass = jnp.zeros_like(top)
    for ref in stats_refs:
        mass = mass + ref[1:2, :] * jnp.exp(ref[0:1, :] - top)
    factor = jnp.exp(own_top - top) / mass
    mass_sum = jnp.zeros((NSEG * bricks, count), jnp.float32)
    for t in range(PAIRS):
        plus, minus = (
            lax.dot_general(
                hit_ref[...],
                terms_ref[2 * t + i],
                (((1,), (1,)), ((), ())),
                preferred_element_type=jnp.float32,
            )
            for i in range(2)
        )
        even = (plus + minus) * factor
        odd = (plus - minus) * factor
        mass_sum = mass_sum + even
        for j in range(NSEG):
            at = slice(j * bricks, (j + 1) * bricks)
            pairs_ref[j, t * bricks : (t + 1) * bricks, :] = even[at].astype(jnp.bfloat16)
            pairs_ref[j, (PAIRS + t) * bricks : (PAIRS + t + 1) * bricks, :] = odd[at].astype(
                jnp.bfloat16
            )
    mass_sum = jnp.sum(mass_sum, axis=1, keepdims=True)
    mass_high = mass_sum.astype(jnp.bfloat16).astype(jnp.float32)
    mass_low = mass_sum - mass_high
    lane = lax.broadcasted_iota(jnp.int32, (bricks, LANES), 1)
    for j in range(NSEG):
        at = slice(j * bricks, (j + 1) * bricks)
        re_at = slice(j * SEG, (j + 1) * SEG)
        im_at = slice(K + j * SEG, K + (j + 1) * SEG)
        left = pairs_ref[j]
        with_re = jnp.dot(left, based_ref[:, re_at], preferred_element_type=jnp.float32)
        with_im = jnp.dot(left, based_ref[:, im_at], preferred_element_type=jnp.float32)
        sum_re = jnp.zeros((bricks, SEG), jnp.float32)
        sum_im = jnp.zeros((bricks, SEG), jnp.float32)
        for t in range(PAIRS):
            cos_t = cos_ref[t : t + 1, re_at]
            sin_t = sin_ref[t : t + 1, re_at]
            even = slice(t * bricks, (t + 1) * bricks)
            odd = slice((PAIRS + t) * bricks, (PAIRS + t + 1) * bricks)
            sum_re = sum_re + cos_t * with_re[even] + sin_t * with_im[odd]
            sum_im = sum_im + cos_t * with_im[even] - sin_t * with_re[odd]
        sums_ref[:, j, :SEG] = sum_re
        sums_ref[:, j, SEG : 2 * SEG] = sum_im
        sums_ref[:, j, 2 * SEG :] = jnp.where(
            lane == 0, mass_high[at], jnp.where(lane == 1, mass_low[at], 0.0)
        )
    out_ref[...] = sums_ref[...].astype(jnp.bfloat16)


def final_kernel(arrived_ref, weight_ref, cover_ref, values_ref, mass_ref):
    vox = cover_ref.shape[1]
    total = jnp.sum(arrived_ref[...].astype(jnp.float32), axis=0)
    re, im = total[:, :SEG], total[:, SEG : 2 * SEG]
    seg_mass = total[:, 2 * SEG : 2 * SEG + 1] + total[:, 2 * SEG + 1 : 2 * SEG + 2]
    parts = []
    for _ in range(3):
        high = [x.astype(jnp.bfloat16).astype(jnp.float32) for x in (re, im)]
        parts += high
        re, im = re - high[0], im - high[1]
    left = jnp.concatenate(parts, axis=0).astype(jnp.bfloat16)
    row = lax.broadcasted_iota(jnp.int32, (left.shape[0], 2 * vox), 0) % NSEG
    product = jnp.zeros((left.shape[0], 2 * vox), jnp.float32)
    for j in range(NSEG):
        full = jnp.dot(
            left,
            weight_ref[:, 2 * j * vox : 2 * (j + 1) * vox],
            preferred_element_type=jnp.float32,
        )
        product = jnp.where(row == j, full, product)
    step = 2 * NSEG
    product = product[:step] + product[step : 2 * step] + product[2 * step :]
    for p in range(2):
        line = jnp.sum(product[p * NSEG : (p + 1) * NSEG], axis=0, keepdims=True)
        values_ref[0, p : p + 1, :] = (
            line[:, :vox] * float(1 << interp_bits) + line[:, vox:]
        ) * interp_scale
    mass_ref[0] = jnp.sum(seg_mass * cover_ref[...], axis=0, keepdims=True)


def on_chip(*arrays):
    return [pltpu.with_memory_space_constraint(x, pltpu.VMEM) for x in arrays]


def call(kernel, name, out_shape, inputs, scratch=(), aliases=None, chip_out=True):
    spec = pl.BlockSpec(memory_space=pltpu.VMEM)
    single = not isinstance(out_shape, list)
    shapes = [out_shape] if single else out_shape
    if chip_out:
        shapes = [pltpu.VMEM(x.shape, x.dtype) for x in shapes]
    out = pl.pallas_call(
        kernel,
        in_specs=[spec] * len(inputs),
        out_specs=[spec] * len(shapes),
        out_shape=shapes,
        scratch_shapes=list(scratch),
        input_output_aliases=aliases or {},
        compiler_params=pltpu.CompilerParams(vmem_limit_bytes=VMEM_LIMIT),
        name=name,
    )(*inputs)
    return out[0] if single else out


VMEM_LIMIT = 24 * 2**20


def swap(array, amount):
    count = lax.axis_size("orient")
    return lax.ppermute(array, "orient", [(i, i ^ amount) for i in range(count)])


def shift(array, amount):
    count = lax.axis_size("orient")
    return lax.ppermute(array, "orient", [(i, (i + amount) % count) for i in range(count)])


def image_rounds(images):
    count = lax.axis_size("orient")
    rounds = [(("shift", 0), [images])]
    if count != 4:
        return rounds + [(("shift", k), [shift(images, k)]) for k in range(1, count)]
    far = swap(images, 2)
    near = swap(images, 1)
    relayed = lax.ppermute(far, "orient", [(1, 0), (2, 3)])
    middle = lax.ppermute(images, "orient", [(1, 2), (2, 1)])
    return rounds + [
        (("xor", 1), [near]),
        (("xor", 2), [far]),
        (("xor", 3), [relayed, middle]),
    ]


def everyone(array):
    count = lax.axis_size("orient")
    if count != 4:
        return [array] + [shift(array, k) for k in range(1, count)]
    return [array] + [swap(array, k) for k in (3, 2, 1)]


def per_device(images, offsets, slices, seg_map, interp):
    orient_count = lax.axis_size("orient")
    group_count = lax.axis_size("img") * lax.axis_size("brick")
    bricks = orient_count * group_count
    rows = images.shape[0]
    orient = slices.shape[0]
    count = rows * orient_count
    vox = interp.shape[3]
    cos_table, sin_table = on_chip(*(jnp.asarray(t) for t in phase_tables()))
    f32, bf16 = jnp.float32, jnp.bfloat16

    rounds = image_rounds(images)
    weights, cover, hit = call(
        functools.partial(setup_kernel, bricks),
        "setup",
        [
            jax.ShapeDtypeStruct((SEG, 2 * NSEG * vox), bf16),
            jax.ShapeDtypeStruct((NSEG, vox), f32),
            jax.ShapeDtypeStruct((NSEG * bricks, orient), bf16),
        ],
        [interp, seg_map.reshape(-1, LANES)],
    )
    slices_v, offsets_v = on_chip(slices, offsets.T)
    state_shapes = [
        jax.ShapeDtypeStruct((SHIFTS, count, orient), bf16),
        jax.ShapeDtypeStruct((count, 2 * K), bf16),
        jax.ShapeDtypeStruct((8, count), f32),
    ]
    for k, (source, arrays) in enumerate(rounds):
        first = k == 0
        inputs = on_chip(*arrays) + [offsets_v, slices_v, cos_table, sin_table]
        if not first:
            inputs += on_chip(norm, *state, cover)
        at = len(arrays) + 5
        out = call(
            functools.partial(score_kernel, first, source, len(arrays)),
            "scores",
            state_shapes + ([jax.ShapeDtypeStruct((8, orient), f32)] if first else []),
            inputs,
            scratch=[pltpu.VMEM((SHIFTS * rows, 2 * K), bf16)],
            aliases={} if first else {at + i: i for i in range(3)},
        )
        if first:
            norm = out[3]
        state = out[:3]
    terms, based, stats = state
    outgoing = call(
        functools.partial(brick_kernel, orient_count),
        "bricks",
        jax.ShapeDtypeStruct((bricks, NSEG, 2 * SEG + LANES), bf16),
        on_chip(terms, based, hit) + [cos_table, sin_table] + on_chip(*everyone(stats)),
        scratch=[
            pltpu.VMEM((NSEG, SHIFTS * bricks, count), bf16),
            pltpu.VMEM((bricks, NSEG, 2 * SEG + LANES), f32),
        ],
    )
    received = lax.all_to_all(
        outgoing, ("orient", "img", "brick"), split_axis=0, concat_axis=0, tiled=True
    )
    return call(
        final_kernel,
        "insert",
        [
            jax.ShapeDtypeStruct((1, 2, vox), f32),
            jax.ShapeDtypeStruct((1, 1, vox), f32),
        ],
        on_chip(received, weights, cover),
        chip_out=False,
    )


def solution(mesh):
    placed = (
        P(("groups", "orient", "img", "brick"), None),
        P("groups", None),
        P(("groups", "orient"), None),
        P(),
        P(("orient", "img", "brick"), None, None, None),
    )

    def device(*args):
        values, weight = per_device(*args)
        return values, weight.reshape(1, -1)

    return jax.shard_map(
        device,
        mesh=mesh,
        in_specs=placed,
        out_specs=(
            P(("groups", "orient", "img", "brick"), None, None),
            P(("groups", "orient", "img", "brick"), None),
        ),
        check_vma=False,
    )
```

time: 72.7 us -> 57.5 us (0.79)
  Pallas kernels: 35.1 us -> 11.9 us
  blocking collectives: 0 us -> 13.3 us
  waiting for transfers between devices: 3.04 us -> 14 us
  starting transfers between devices: 20.7 us -> 12.2 us
  other arithmetic: 4.68 us -> 0 us
  local copies, waits for them, and re-layouts: 7.84 us -> 4.98 us
    pallas_call x8 -> x7, Pallas kernels: 35.1 us -> 11.9 us  [call(): pl.pallas_call(kernel, in_specs=[spec] * len(inputs), out_specs=[spec] *...]
    all_to_all x0 -> x1, blocking collectives: none -> 13.3 us  [per_device(): lax.all_to_all(outgoing, ('orient', 'img', 'brick'), split_axis=0, concat...]
    ppermute x6 -> x7, waiting for transfers between devices: 0.86 us -> 14 us  [the longest x5 14 us: swap(): lax.ppermute(array, 'orient', [(i, i ^ amount) for i in range(count)])]
    all_to_all x1 -> x0, starting transfers between devices: 6.39 us -> none  [per_device(): lax.all_to_all(outgoing, ('orient', 'img', 'brick'), split_axis=0, concat...]
    another operation x4 -> x0, other arithmetic: 2.46 us -> none  [per_device(): jnp.stack([source, source * group_count + group_index]).astype(jnp.int32)]
    all_to_all x1 -> x0, waiting for transfers between devices: 2.18 us -> none  [per_device(): lax.all_to_all(outgoing, ('orient', 'img', 'brick'), split_axis=0, concat...]
    ppermute x6 -> x7, starting transfers between devices: 14.3 us -> 12.2 us  [the longest x5 10.2 us: swap(): lax.ppermute(array, 'orient', [(i, i ^ amount) for i in range(count)])]
    unnamed x20 -> x18, local copies, waits for them, and re-layouts: 7.02 us -> 4.98 us
  transfers between devices with their start and end apart: 7 -> 7, of which waited for: 2 -> 4; matrix products, arithmetic and copies ran while one was open for 8% -> 0% of each run, Pallas kernels for 33% -> 13%
where the time goes in v2:
time: 57.5 us; the launch traced here: 57.1 us
  waiting for transfers between devices  14 us (24%)
  blocking collectives  13.3 us (23%)
  starting transfers between devices  12.2 us (21%)
  Pallas kernels  11.9 us (21%)
  local copies, waits for them, and re-layouts  4.98 us (9%)
  between operations  0.74 us (1%)
    ppermute x5, waiting for transfers between devices, swap(): lax.ppermute(array, 'orient', [(i, i ^ amount) for i in range(count)])  14 us
    all_to_all x1, blocking collectives, per_device(): lax.all_to_all(outgoing, ('orient', 'img', 'brick'), split_axis=0, concat...  13.3 us
    pallas_call x7, Pallas kernels, call(): pl.pallas_call(kernel, in_specs=[spec] * len(inputs), out_specs=[spec] *...  11.9 us
    ppermute x5, starting transfers between devices, swap(): lax.ppermute(array, 'orient', [(i, i ^ amount) for i in range(count)])  10.2 us
    unnamed x18, local copies, waits for them, and re-layouts  4.98 us
    ppermute x1, starting transfers between devices, image_rounds(): relayed = lax.ppermute(far, 'orient', [(1, 0), (2, 3)])  1.28 us
  transfers between devices with their start and end apart: 7, of which 4 were waited for; matrix products, arithmetic and copies ran while one was open for 0% of the time, Pallas kernels for 13%

profile of v2, /device:TPU:0, one launch (start us, length us, event | category | flops | bytes accessed | tf_op | source)
XLA Modules:
  0.0 57.1 jit_solution(14439129518555946439)
XLA Ops:
  0.6 0.0 copy-start
  0.6 4.1 %collective-permute-start = (bf16[32,4096]{1,0:T(8,128)(2,1)}, bf16[32,4096]{1,0:T(8,128)(2,1)S(1)}, u32[]{:S(2)}, u32[]{:S(2)}) collective-permute-start(bf16[32,4096]{1,0:T(8,128)(2,1)} %refs_0_.1), channel_id=1, source_target_pairs={{0,8},{4,12},{8,0},{12,4},{1,9},{5,13},{9,1},{13,5},{2,10},{6,14},... | collective-permute-start | bytes 786440 | tf_op jit(solution)/shard_map/ppermute | solution.py:315
  4.8 1.6 %collective-permute-start.3 = (bf16[32,4096]{1,0:T(8,128)(2,1)}, bf16[32,4096]{1,0:T(8,128)(2,1)S(1)}, u32[]{:S(2)}, u32[]{:S(2)}) collective-permute-start(bf16[32,4096]{1,0:T(8,128)(2,1)} %refs_0_.1), channel_id=1, source_target_pairs={{0,4},{4,0},{8,12},{12,8},{1,5},{5,1},{9,13},{13,9},{2,6},{6,2},{1... | collective-permute-start | bytes 786440 | tf_op jit(solution)/shard_map/ppermute | solution.py:315
  6.3 0.7 %collective-permute-start.2 = (bf16[32,4096]{1,0:T(8,128)(2,1)}, bf16[32,4096]{1,0:T(8,128)(2,1)S(1)}, u32[]{:S(2)}, u32[]{:S(2)}) collective-permute-start(bf16[32,4096]{1,0:T(8,128)(2,1)} %refs_0_.1), channel_id=1, source_target_pairs={{4,8},{8,4},{5,9},{9,5},{6,10},{10,6},{7,11},{11,7},{20,24},{24,20... | collective-permute-start | bytes 786440 | tf_op jit(solution)/shard_map/ppermute | solution.py:331
  7.0 10.8 %collective-permute-done.refs_0_ = bf16[32,4096]{1,0:T(8,128)(2,1)S(1)} collective-permute-done((bf16[32,4096]{1,0:T(8,128)(2,1)}, bf16[32,4096]{1,0:T(8,128)(2,1)S(1)}, u32[]{:S(2)}, u32[]{:S(2)}) %collective-permute-start) | collective-permute-done | bytes 262176 | tf_op jit(solution)/shard_map/ppermute | solution.py:315
  17.8 1.3 %collective-permute-start.1 = (bf16[32,4096]{1,0:T(8,128)(2,1)S(1)}, bf16[32,4096]{1,0:T(8,128)(2,1)S(1)}, u32[]{:S(2)}, u32[]{:S(2)}) collective-permute-start(bf16[32,4096]{1,0:T(8,128)(2,1)S(1)} %collective-permute-done.refs_0_), channel_id=1, source_target_pairs={{4,0},{8,12},{5,1},{9,13},{6,2},{10,14},{7,3},{11,15},{20,16},{24,... | collective-permute-start | bytes 786440 | tf_op jit(solution)/shard_map/ppermute | solution.py:330
  19.1 0.0 copy-start.1
  19.1 1.6 %copy-done.1 = s32[1,8,256,256]{3,2,1,0:T(8,128)S(1)} copy-done((s32[1,8,256,256]{3,2,1,0:T(8,128)S(1)}, s32[1,8,256,256]{3,2,1,0:T(8,128)}, u32[]{:S(2)}) %copy-start.1) | copy-done | bytes 2097176
  20.7 0.0 copy-start.8
  20.7 0.8 %copy-done.8 = s32[8192,1]{0,1:T(1,128)S(1)} copy-done((s32[8192,1]{0,1:T(1,128)S(1)}, s32[8192,1]{0,1:T(1,128)}, u32[]{:S(2)}) %copy-start.8) | copy-done | bytes 32792
  21.4 0.0 copy-start.7
  21.4 1.1 %setup.1 = (bf16[256,4096]{1,0:T(8,128)(2,1)S(1)}, f32[8,256]{1,0:T(8,128)S(1)}, bf16[128,256]{1,0:T(8,128)(2,1)S(1)}) custom-call(s32[1,8,256,256]{3,2,1,0:T(8,128)S(1)} %copy-done.1, s32[64,128]{1,0:T(8,128)S(1)} %bitcast.7), custom_call_target="tpu_custom_call" | custom-call | tf_op jit(solution)/shard_map/setup/pallas_call | solution.py:297
  22.6 0.0 copy-done
  22.6 0.0 copy-done.7
  22.6 0.0 copy-start.2
  22.6 0.8 %copy-done.2 = f32[8,2048]{1,0:T(8,128)S(1)} copy-done((f32[8,2048]{1,0:T(8,128)S(1)}, f32[8,2048]{1,0:T(8,128)}, u32[]{:S(2)}) %copy-start.2) | copy-done | bytes 65560
  23.4 0.0 copy-start.4
  23.4 0.8 %copy-done.4 = f32[8,2048]{1,0:T(8,128)S(1)} copy-done((f32[8,2048]{1,0:T(8,128)S(1)}, f32[8,2048]{1,0:T(8,128)}, u32[]{:S(2)}) %copy-start.4) | copy-done | bytes 65560
  24.3 0.0 copy-start.6
  24.3 0.9 %copy-done.6 = bf16[32,4096]{1,0:T(8,128)(2,1)S(1)} copy-done((bf16[32,4096]{1,0:T(8,128)(2,1)S(1)}, bf16[32,4096]{1,0:T(8,128)(2,1)}, u32[]{:S(2)}) %copy-start.6) | copy-done | bytes 262168
  25.2 0.0 copy-start.3
  25.2 2.5 %scores.4 = (bf16[16,128,256]{2,1,0:T(8,128)(2,1)S(1)}, bf16[128,4096]{1,0:T(8,128)(2,1)S(1)}, f32[8,128]{1,0:T(8,128)S(1)}, f32[8,256]{1,0:T(8,128)S(1)}) custom-call(bf16[32,4096]{1,0:T(8,128)(2,1)S(1)} %copy-done.6, s32[2,512]{1,0:T(2,128)S(1)} %bitcast.3, bf16[256,4096]{1,0:T(8,128)(2,1)S(1)} %copy-done, f32[8,2048]{1,0:T(8,128)S(1)} %copy-done.2, ...), custom_call_target="tpu_custom_call" | custom-call | tf_op jit(solution)/shard_map/scores/pallas_call | solution.py:297
  27.7 0.0 collective-permute-done.3.refs_0_
  27.7 0.0 copy-done.3
  27.7 2.0 %scores.5 = (bf16[16,128,256]{2,1,0:T(8,128)(2,1)S(1)}, bf16[128,4096]{1,0:T(8,128)(2,1)S(1)}, f32[8,128]{1,0:T(8,128)S(1)}) custom-call(bf16[32,4096]{1,0:T(8,128)(2,1)S(1)} %collective-permute-done.3.refs_0_, s32[2,512]{1,0:T(2,128)S(1)} %bitcast.4, bf16[256,4096]{1,0:T(8,128)(2,1)S(1)} %copy-done, ...), custom_call_target="tpu_custom_call", output_to_operand_aliasing={{0}: (6, {}), {1}: (7, {}), {2}: (8, {})} | custom-call | tf_op jit(solution)/shard_map/scores/pallas_call | solution.py:297
  29.7 0.0 copy-start.5
  29.7 2.0 %scores.6 = (bf16[16,128,256]{2,1,0:T(8,128)(2,1)S(1)}, bf16[128,4096]{1,0:T(8,128)(2,1)S(1)}, f32[8,128]{1,0:T(8,128)S(1)}) custom-call(bf16[32,4096]{1,0:T(8,128)(2,1)S(1)} %collective-permute-done.refs_0_, s32[2,512]{1,0:T(2,128)S(1)} %bitcast.5, bf16[256,4096]{1,0:T(8,128)(2,1)S(1)} %copy-done, ...), custom_call_target="tpu_custom_call", output_to_operand_aliasing={{0}: (6, {}), {1}: (7, {}), {2}: (8, {})} | custom-call | tf_op jit(solution)/shard_map/scores/pallas_call | solution.py:297
  31.7 0.0 collective-permute-done.2.refs_1_
  31.8 0.0 collective-permute-done.1.refs_0_
  31.8 0.0 copy-done.5
  31.8 2.0 %scores.7 = (bf16[16,128,256]{2,1,0:T(8,128)(2,1)S(1)}, bf16[128,4096]{1,0:T(8,128)(2,1)S(1)}, f32[8,128]{1,0:T(8,128)S(1)}) custom-call(bf16[32,4096]{1,0:T(8,128)(2,1)S(1)} %collective-permute-done.1.refs_0_, bf16[32,4096]{1,0:T(8,128)(2,1)S(1)} %collective-permute-done.2.refs_1_, ...), custom_call_target="tpu_custom_call", output_to_operand_aliasing={{0}: (7, {}), {1}: (8, {}), {2}: (9, {})} | custom-call | tf_op jit(solution)/shard_map/scores/pallas_call | solution.py:297
  33.8 2.8 %collective-permute-start.4 = (f32[8,128]{1,0:T(8,128)S(1)}, f32[8,128]{1,0:T(8,128)S(1)}, u32[]{:S(2)}, u32[]{:S(2)}) collective-permute-start(f32[8,128]{1,0:T(8,128)S(1)} %get-tuple-element.34.rest_0_), channel_id=1, source_target_pairs={{0,12},{4,8},{8,4},{12,0},{1,13},{5,9},{9,5},{13,1},{2,14},{6,10},... | collective-permute-start | bytes 12296 | tf_op jit(solution)/shard_map/ppermute | solution.py:315
  36.6 1.4 %collective-permute-start.5 = (f32[8,128]{1,0:T(8,128)S(1)}, f32[8,128]{1,0:T(8,128)S(1)}, u32[]{:S(2)}, u32[]{:S(2)}) collective-permute-start(f32[8,128]{1,0:T(8,128)S(1)} %get-tuple-element.34.rest_0_), channel_id=1, source_target_pairs={{0,8},{4,12},{8,0},{12,4},{1,9},{5,13},{9,1},{13,5},{2,10},{6,14},... | collective-permute-start | bytes 12296 | tf_op jit(solution)/shard_map/ppermute | solution.py:315
  38.0 0.4 collective-permute-start.6
  38.3 0.9 %collective-permute-done.4.rest_1_ = f32[8,128]{1,0:T(8,128)S(1)} collective-permute-done((f32[8,128]{1,0:T(8,128)S(1)}, f32[8,128]{1,0:T(8,128)S(1)}, u32[]{:S(2)}, u32[]{:S(2)}) %collective-permute-start.4) | collective-permute-done | bytes 4128 | tf_op jit(solution)/shard_map/ppermute | solution.py:315
  39.3 1.8 %collective-permute-done.5.rest_2_ = f32[8,128]{1,0:T(8,128)S(1)} collective-permute-done((f32[8,128]{1,0:T(8,128)S(1)}, f32[8,128]{1,0:T(8,128)S(1)}, u32[]{:S(2)}, u32[]{:S(2)}) %collective-permute-start.5) | collective-permute-done | bytes 4128 | tf_op jit(solution)/shard_map/ppermute | solution.py:315
  41.1 0.5 collective-permute-done.6.rest_3_
  41.6 1.1 %bricks.1 = bf16[16,8,640]{2,1,0:T(8,128)(2,1)S(1)} custom-call(bf16[16,128,256]{2,1,0:T(8,128)(2,1)S(1)} %get-tuple-element.31.terms_ref, bf16[128,4096]{1,0:T(8,128)(2,1)S(1)} %get-tuple-element.32.based_ref, bf16[128,256]{1,0:T(8,128)(2,1)S(1)} %get-tuple-element.33.hit_ref, f32[8,2048]{1,0:T(8,128)S(1)} %copy-done.3, f32[8,2048]{1,0:T(8,128)S(1)} %copy-done.5, ...), custom_call_target="tpu_custom_call" | custom-call | tf_op jit(solution)/shard_map/bricks/pallas_call | solution.py:297
  42.7 13.3 %all_to_all.5.arrived_ref = bf16[16,8,640]{2,1,0:T(8,128)(2,1)S(1)} all-to-all(bf16[16,8,640]{2,1,0:T(8,128)(2,1)S(1)} %bricks.1), channel_id=1, replica_groups=mesh['groups'=2,'orient'=4,'img'=2,'brick'=2] {'orient','img','brick'}, dimensions={0} | all-to-all | bytes 327680 | tf_op jit(solution)/shard_map/all_to_all | solution.py:402
  56.0 1.1 %insert.1 = (f32[1,2,256]{2,1,0:T(2,128)}, f32[1,1,256]{2,1,0:T(1,128)}) custom-call(bf16[16,8,640]{2,1,0:T(8,128)(2,1)S(1)} %all_to_all.5.arrived_ref, bf16[256,4096]{1,0:T(8,128)(2,1)S(1)} %get-tuple-element.35.weight_ref, f32[8,256]{1,0:T(8,128)S(1)} %get-tuple-element.24.refs_9_.refs_10_.cover_ref), custom_call_target="tpu_custom_call" | custom-call | tf_op jit(solution)/shard_map/insert/pallas_call | solution.py:297
Async XLA Ops:
  0.6 21.9 %copy-start = (bf16[256,4096]{1,0:T(8,128)(2,1)S(1)}, bf16[256,4096]{1,0:T(8,128)(2,1)}, u32[]{:S(2)}) copy-start(bf16[256,4096]{1,0:T(8,128)(2,1)} %refs_3_.4) | copy-start | bytes 6291460
  0.6 17.2 %collective-permute-start = (bf16[32,4096]{1,0:T(8,128)(2,1)}, bf16[32,4096]{1,0:T(8,128)(2,1)S(1)}, u32[]{:S(2)}, u32[]{:S(2)}) collective-permute-start(bf16[32,4096]{1,0:T(8,128)(2,1)} %refs_0_.1), channel_id=1, source_target_pairs={{0,8},{4,12},{8,0},{12,4},{1,9},{5,13},{9,1},{13,5},{2,10},{6,14},... | collective-permute-start | bytes 786440 | tf_op jit(solution)/shard_map/ppermute | solution.py:315
  4.8 22.9 %collective-permute-start.3 = (bf16[32,4096]{1,0:T(8,128)(2,1)}, bf16[32,4096]{1,0:T(8,128)(2,1)S(1)}, u32[]{:S(2)}, u32[]{:S(2)}) collective-permute-start(bf16[32,4096]{1,0:T(8,128)(2,1)} %refs_0_.1), channel_id=1, source_target_pairs={{0,4},{4,0},{8,12},{12,8},{1,5},{5,1},{9,13},{13,9},{2,6},{6,2},{1... | collective-permute-start | bytes 786440 | tf_op jit(solution)/shard_map/ppermute | solution.py:315
  6.3 25.4 %collective-permute-start.2 = (bf16[32,4096]{1,0:T(8,128)(2,1)}, bf16[32,4096]{1,0:T(8,128)(2,1)S(1)}, u32[]{:S(2)}, u32[]{:S(2)}) collective-permute-start(bf16[32,4096]{1,0:T(8,128)(2,1)} %refs_0_.1), channel_id=1, source_target_pairs={{4,8},{8,4},{5,9},{9,5},{6,10},{10,6},{7,11},{11,7},{20,24},{24,20... | collective-permute-start | bytes 786440 | tf_op jit(solution)/shard_map/ppermute | solution.py:331
  17.8 14.0 %collective-permute-start.1 = (bf16[32,4096]{1,0:T(8,128)(2,1)S(1)}, bf16[32,4096]{1,0:T(8,128)(2,1)S(1)}, u32[]{:S(2)}, u32[]{:S(2)}) collective-permute-start(bf16[32,4096]{1,0:T(8,128)(2,1)S(1)} %collective-permute-done.refs_0_), channel_id=1, source_target_pairs={{4,0},{8,12},{5,1},{9,13},{6,2},{10,14},{7,3},{11,15},{20,16},{24,... | collective-permute-start | bytes 786440 | tf_op jit(solution)/shard_map/ppermute | solution.py:330
  19.1 1.6 %copy-start.1 = (s32[1,8,256,256]{3,2,1,0:T(8,128)S(1)}, s32[1,8,256,256]{3,2,1,0:T(8,128)}, u32[]{:S(2)}) copy-start(s32[1,8,256,256]{3,2,1,0:T(8,128)} %interp_ref.1) | copy-start | bytes 6291460
  20.7 0.8 %copy-start.8 = (s32[8192,1]{0,1:T(1,128)S(1)}, s32[8192,1]{0,1:T(1,128)}, u32[]{:S(2)}) copy-start(s32[8192,1]{0,1:T(1,128)} %param.10) | copy-start | bytes 98308
  21.4 1.1 %copy-start.7 = (s32[512,2]{0,1:T(2,128)S(1)}, s32[512,2]{0,1:T(2,128)}, u32[]{:S(2)}) copy-start(s32[512,2]{0,1:T(2,128)} %param.8) | copy-start | bytes 12292
  22.6 0.8 %copy-start.2 = (f32[8,2048]{1,0:T(8,128)S(1)}, f32[8,2048]{1,0:T(8,128)}, u32[]{:S(2)}) copy-start(f32[8,2048]{1,0:T(8,128)} %constant.4.clone.refs_3_.refs_4_.cos_ref) | copy-start | bytes 196612
  23.4 0.8 %copy-start.4 = (f32[8,2048]{1,0:T(8,128)S(1)}, f32[8,2048]{1,0:T(8,128)}, u32[]{:S(2)}) copy-start(f32[8,2048]{1,0:T(8,128)} %constant.5.clone.refs_4_.refs_5_.sin_ref) | copy-start | bytes 196612
  24.3 0.9 %copy-start.6 = (bf16[32,4096]{1,0:T(8,128)(2,1)S(1)}, bf16[32,4096]{1,0:T(8,128)(2,1)}, u32[]{:S(2)}) copy-start(bf16[32,4096]{1,0:T(8,128)(2,1)} %refs_0_.1) | copy-start | bytes 786436
  25.2 2.5 %copy-start.3 = (f32[8,2048]{1,0:T(8,128)S(1)}, f32[8,2048]{1,0:T(8,128)}, u32[]{:S(2)}) copy-start(f32[8,2048]{1,0:T(8,128)} %constant.4.clone.refs_3_.refs_4_.cos_ref) | copy-start | bytes 196612
  29.7 2.1 %copy-start.5 = (f32[8,2048]{1,0:T(8,128)S(1)}, f32[8,2048]{1,0:T(8,128)}, u32[]{:S(2)}) copy-start(f32[8,2048]{1,0:T(8,128)} %constant.5.clone.refs_4_.refs_5_.sin_ref) | copy-start | bytes 196612
  33.8 5.4 %collective-permute-start.4 = (f32[8,128]{1,0:T(8,128)S(1)}, f32[8,128]{1,0:T(8,128)S(1)}, u32[]{:S(2)}, u32[]{:S(2)}) collective-permute-start(f32[8,128]{1,0:T(8,128)S(1)} %get-tuple-element.34.rest_0_), channel_id=1, source_target_pairs={{0,12},{4,8},{8,4},{12,0},{1,13},{5,9},{9,5},{13,1},{2,14},{6,10},... | collective-permute-start | bytes 12296 | tf_op jit(solution)/shard_map/ppermute | solution.py:315
  36.6 4.5 %collective-permute-start.5 = (f32[8,128]{1,0:T(8,128)S(1)}, f32[8,128]{1,0:T(8,128)S(1)}, u32[]{:S(2)}, u32[]{:S(2)}) collective-permute-start(f32[8,128]{1,0:T(8,128)S(1)} %get-tuple-element.34.rest_0_), channel_id=1, source_target_pairs={{0,8},{4,12},{8,0},{12,4},{1,9},{5,13},{9,1},{13,5},{2,10},{6,14},... | collective-permute-start | bytes 12296 | tf_op jit(solution)/shard_map/ppermute | solution.py:315
  38.0 3.6 %collective-permute-start.6 = (f32[8,128]{1,0:T(8,128)S(1)}, f32[8,128]{1,0:T(8,128)S(1)}, u32[]{:S(2)}, u32[]{:S(2)}) collective-permute-start(f32[8,128]{1,0:T(8,128)S(1)} %get-tuple-element.34.rest_0_), channel_id=1, source_target_pairs={{0,4},{4,0},{8,12},{12,8},{1,5},{5,1},{9,13},{13,9},{2,6},{6,2},{1... | collective-permute-start | bytes 12296 | tf_op jit(solution)/shard_map/ppermute | solution.py:315

commit v3 on v2

--- a/solution.py
+++ b/solution.py
@@ -18,18 +18,6 @@
 interp_bits = 4
 interp_scale = 1.0 / 256.0
 PAIRS = SHIFTS // 2
-
-
-def phase_tables():
-    coef = np.arange(K)
-    u = coef % frame_side - frame_side // 2
-    w = coef // frame_side
-    shift = np.arange(PAIRS)
-    dx = 2 * (shift % 4) - 3
-    dy = 2 * (shift // 4) - 3
-    angle = (u[None, :] * dx[:, None] + w[None, :] * dy[:, None]) % (2 * frame_side)
-    angle = angle * (2.0 * np.pi / (2 * frame_side))
-    return np.cos(angle).astype(np.float32), np.sin(angle).astype(np.float32)
 
 
 def cos_sin(steps):
@@ -44,11 +32,49 @@
     return c, s * x
 
 
-def setup_kernel(bricks, interp_ref, map_ref, weight_ref, cover_ref, hit_ref):
-    vox = interp_ref.shape[3]
+def setup_kernel(
+    bricks,
+    interp_hbm,
+    map_hbm,
+    images_hbm,
+    offsets_hbm,
+    weight_ref,
+    cover_ref,
+    hit_ref,
+    cos_ref,
+    sin_ref,
+    images_ref,
+    offsets_ref,
+    interp_ref,
+    map_ref,
+    sems,
+):
+    small = [
+        pltpu.make_async_copy(source, target, sems.at[NSEG + i])
+        for i, (source, target) in enumerate(
+            [(images_hbm, images_ref), (offsets_hbm, offsets_ref), (map_hbm, map_ref)]
+        )
+    ]
+    large = [
+        pltpu.make_async_copy(interp_hbm.at[0, j], interp_ref.at[j], sems.at[j])
+        for j in range(NSEG)
+    ]
+    for copy in small + large:
+        copy.start()
+    coef = lax.broadcasted_iota(jnp.int32, (PAIRS, K), 1)
+    pair = lax.broadcasted_iota(jnp.int32, (PAIRS, K), 0)
+    u = jnp.bitwise_and(coef, frame_side - 1) - frame_side // 2
+    w = coef // frame_side
+    dx = 2 * jnp.bitwise_and(pair, 3) - 3
+    dy = 2 * (pair // 4) - 3
+    cos_ref[...], sin_ref[...] = cos_sin(u * dx + w * dy)
+    for copy in small:
+        copy.wait()
+    vox = interp_ref.shape[2]
     covers = []
     for j in range(NSEG):
-        raw = interp_ref[0, j]
+        large[j].wait()
+        raw = interp_ref[j]
         high = jnp.right_shift(raw, interp_bits).astype(jnp.float32)
         low = jnp.bitwise_and(raw, (1 << interp_bits) - 1).astype(jnp.float32)
         weight_ref[:, 2 * j * vox : (2 * j + 1) * vox] = high.astype(jnp.bfloat16)
@@ -98,8 +124,8 @@
     if first:
         terms_ref, based_ref, stats_ref, norm_ref, left_ref = refs[4:]
     else:
-        norm_ref, _, _, stats_in_ref, _ = refs[4:9]
-        terms_ref, based_ref, stats_ref, left_ref = refs[9:]
+        norm_ref, _, _, stats_in_ref = refs[4:8]
+        terms_ref, based_ref, stats_ref, left_ref = refs[8:]
     inv_noise = 100.0 / K
     rows = images_refs[0].shape[0]
     plane = source_plane(source)
@@ -288,15 +314,16 @@
     return [pltpu.with_memory_space_constraint(x, pltpu.VMEM) for x in arrays]
 
 
-def call(kernel, name, out_shape, inputs, scratch=(), aliases=None, chip_out=True):
+def call(kernel, name, out_shape, inputs, scratch=(), aliases=None, chip_out=True, hbm_in=False):
     spec = pl.BlockSpec(memory_space=pltpu.VMEM)
+    in_spec = pl.BlockSpec(memory_space=pltpu.HBM) if hbm_in else spec
     single = not isinstance(out_shape, list)
     shapes = [out_shape] if single else out_shape
     if chip_out:
         shapes = [pltpu.VMEM(x.shape, x.dtype) for x in shapes]
     out = pl.pallas_call(
         kernel,
-        in_specs=[spec] * len(inputs),
+        in_specs=[in_spec] * len(inputs),
         out_specs=[spec] * len(shapes),
         out_shape=shapes,
         scratch_shapes=list(scratch),
@@ -320,22 +347,6 @@
     return lax.ppermute(array, "orient", [(i, (i + amount) % count) for i in range(count)])
 
 
-def image_rounds(images):
-    count = lax.axis_size("orient")
-    rounds = [(("shift", 0), [images])]
-    if count != 4:
-        return rounds + [(("shift", k), [shift(images, k)]) for k in range(1, count)]
-    far = swap(images, 2)
-    near = swap(images, 1)
-    relayed = lax.ppermute(far, "orient", [(1, 0), (2, 3)])
-    middle = lax.ppermute(images, "orient", [(1, 2), (2, 1)])
-    return rounds + [
-        (("xor", 1), [near]),
-        (("xor", 2), [far]),
-        (("xor", 3), [relayed, middle]),
-    ]
-
-
 def everyone(array):
     count = lax.axis_size("orient")
     if count != 4:
@@ -351,33 +362,52 @@
     orient = slices.shape[0]
     count = rows * orient_count
     vox = interp.shape[3]
-    cos_table, sin_table = on_chip(*(jnp.asarray(t) for t in phase_tables()))
     f32, bf16 = jnp.float32, jnp.bfloat16
-
-    rounds = image_rounds(images)
-    weights, cover, hit = call(
+    relay = orient_count == 4
+    if relay:
+        far = swap(images, 2)
+        near = swap(images, 1)
+        waiting = [(("xor", 1), [near])]
+    else:
+        waiting = [(("shift", k), [shift(images, k)]) for k in range(1, orient_count)]
+
+    weights, cover, hit, cos_table, sin_table, own, offsets_v = call(
         functools.partial(setup_kernel, bricks),
         "setup",
         [
             jax.ShapeDtypeStruct((SEG, 2 * NSEG * vox), bf16),
             jax.ShapeDtypeStruct((NSEG, vox), f32),
             jax.ShapeDtypeStruct((NSEG * bricks, orient), bf16),
+            jax.ShapeDtypeStruct((PAIRS, K), f32),
+            jax.ShapeDtypeStruct((PAIRS, K), f32),
+            jax.ShapeDtypeStruct(images.shape, bf16),
+            jax.ShapeDtypeStruct(offsets.shape[::-1], jnp.int32),
         ],
-        [interp, seg_map.reshape(-1, LANES)],
-    )
-    slices_v, offsets_v = on_chip(slices, offsets.T)
+        [
+            pltpu.with_memory_space_constraint(x, pltpu.HBM)
+            for x in (interp, seg_map.reshape(-1, LANES), images, offsets.T)
+        ],
+        scratch=[
+            pltpu.VMEM(interp.shape[1:], jnp.int32),
+            pltpu.VMEM((seg_map.shape[0] // LANES, LANES), jnp.int32),
+            pltpu.SemaphoreType.DMA((NSEG + 3,)),
+        ],
+        hbm_in=True,
+    )
+    constant = on_chip(offsets_v, slices, cos_table, sin_table)
     state_shapes = [
         jax.ShapeDtypeStruct((SHIFTS, count, orient), bf16),
         jax.ShapeDtypeStruct((count, 2 * K), bf16),
         jax.ShapeDtypeStruct((8, count), f32),
     ]
-    for k, (source, arrays) in enumerate(rounds):
-        first = k == 0
-        inputs = on_chip(*arrays) + [offsets_v, slices_v, cos_table, sin_table]
+
+    def scored(source, arrays, earlier):
+        first = earlier is None
+        inputs = on_chip(*arrays) + constant
         if not first:
-            inputs += on_chip(norm, *state, cover)
+            inputs += on_chip(*earlier)
         at = len(arrays) + 5
-        out = call(
+        return call(
             functools.partial(score_kernel, first, source, len(arrays)),
             "scores",
             state_shapes + ([jax.ShapeDtypeStruct((8, orient), f32)] if first else []),
@@ -385,9 +415,18 @@
             scratch=[pltpu.VMEM((SHIFTS * rows, 2 * K), bf16)],
             aliases={} if first else {at + i: i for i in range(3)},
         )
-        if first:
-            norm = out[3]
-        state = out[:3]
+
+    *state, norm = scored(("shift", 0), [own], None)
+    for source, arrays in waiting:
+        state = scored(source, arrays, [norm, *state])
+    if relay:
+        terms, based, stats = state
+        stats, far, again = lax.optimization_barrier((stats, far, images))
+        state = [terms, based, stats]
+        relayed = lax.ppermute(far, "orient", [(1, 0), (2, 3)])
+        middle = lax.ppermute(again, "orient", [(1, 2), (2, 1)])
+        state = scored(("xor", 2), [far], [norm, *state])
+        state = scored(("xor", 3), [relayed, middle], [norm, *state])
     terms, based, stats = state
     outgoing = call(
         functools.partial(brick_kernel, orient_count),

time: 57.5 us -> 52.6 us (0.915)
  local copies, waits for them, and re-layouts: 4.98 us -> 0.01 us
  blocking collectives: 13.3 us -> 11.9 us
  Pallas kernels: 11.9 us -> 12.9 us
  waiting for transfers between devices: 14 us -> 14.9 us
    ppermute x2, waiting for transfers between devices: 0.01 us -> 5.53 us  [the longest x1 5.52 us: per_device(): relayed = lax.ppermute(far, 'orient', [(1, 0), (2, 3)])]
    unnamed x18 -> x4, local copies, waits for them, and re-layouts: 4.98 us -> 0.01 us
    ppermute x5, waiting for transfers between devices: 14 us -> 9.33 us  [swap(): lax.ppermute(array, 'orient', [(i, i ^ amount) for i in range(count)])]
    all_to_all x1, blocking collectives: 13.3 us -> 11.9 us  [per_device(): lax.all_to_all(outgoing, ('orient', 'img', 'brick'), split_axis=0, concat...]
    pallas_call x7, Pallas kernels: 11.9 us -> 12.9 us  [call(): pl.pallas_call(kernel, in_specs=[in_spec] * len(inputs), out_specs=[spec]...]
  transfers between devices with their start and end apart: 7 -> 7, of which waited for: 4 -> 5; matrix products, arithmetic and copies ran while one was open for 0% -> 0% of each run, Pallas kernels for 13% -> 16%
where the time goes in v3:
time: 52.6 us; the launch traced here: 52.4 us
  waiting for transfers between devices  14.9 us (28%)
  Pallas kernels  12.9 us (25%)
  starting transfers between devices  12.1 us (23%)
  blocking collectives  11.9 us (23%)
  between operations  0.7 us (1%)
    pallas_call x7, Pallas kernels, call(): pl.pallas_call(kernel, in_specs=[in_spec] * len(inputs), out_specs=[spec]...  12.9 us
    all_to_all x1, blocking collectives, per_device(): lax.all_to_all(outgoing, ('orient', 'img', 'brick'), split_axis=0, concat...  11.9 us
    ppermute x5, starting transfers between devices, swap(): lax.ppermute(array, 'orient', [(i, i ^ amount) for i in range(count)])  10.1 us
    ppermute x5, waiting for transfers between devices, swap(): lax.ppermute(array, 'orient', [(i, i ^ amount) for i in range(count)])  9.33 us
    ppermute x1, waiting for transfers between devices, per_device(): relayed = lax.ppermute(far, 'orient', [(1, 0), (2, 3)])  5.52 us
    ppermute x1, starting transfers between devices, per_device(): relayed = lax.ppermute(far, 'orient', [(1, 0), (2, 3)])  1.29 us
  transfers between devices with their start and end apart: 7, of which 5 were waited for; matrix products, arithmetic and copies ran while one was open for 0% of the time, Pallas kernels for 16%

profile of v3, /device:TPU:0, one launch (start us, length us, event | category | flops | bytes accessed | tf_op | source)
XLA Modules:
  0.0 52.4 jit_solution(10950953738139315348)
XLA Ops:
  0.6 0.0 copy-start
  0.6 3.1 %collective-permute-start = (bf16[32,4096]{1,0:T(8,128)(2,1)}, bf16[32,4096]{1,0:T(8,128)(2,1)S(1)}, u32[]{:S(2)}, u32[]{:S(2)}) collective-permute-start(bf16[32,4096]{1,0:T(8,128)(2,1)} %images_hbm.1), channel_id=1, source_target_pairs={{0,4},{4,0},{8,12},{12,8},{1,5},{5,1},{9,13},{13,9},{2,6},{6,2},{1... | collective-permute-start | bytes 786440 | tf_op jit(solution)/shard_map/ppermute | solution.py:342
  3.8 2.6 %collective-permute-start.1 = (bf16[32,4096]{1,0:T(8,128)(2,1)}, bf16[32,4096]{1,0:T(8,128)(2,1)S(1)}, u32[]{:S(2)}, u32[]{:S(2)}) collective-permute-start(bf16[32,4096]{1,0:T(8,128)(2,1)} %images_hbm.1), channel_id=1, source_target_pairs={{0,8},{4,12},{8,0},{12,4},{1,9},{5,13},{9,1},{13,5},{2,10},{6,14},... | collective-permute-start | bytes 786440 | tf_op jit(solution)/shard_map/ppermute | solution.py:342
  6.3 2.1 %setup.1 = (bf16[256,4096]{1,0:T(8,128)(2,1)S(1)}, f32[8,256]{1,0:T(8,128)S(1)}, bf16[128,256]{1,0:T(8,128)(2,1)S(1)}, f32[8,2048]{1,0:T(8,128)S(1)}, f32[8,2048...) custom-call(s32[1,8,256,256]{3,2,1,0:T(8,128)} %interp_hbm.1, s32[64,128]{1,0:T(8,128)} %bitcast.3, ...), custom_call_target="tpu_custom_call" | custom-call | tf_op jit(solution)/shard_map/setup/pallas_call | solution.py:324
  8.5 0.0 copy-done
  8.5 2.5 %scores.4 = (bf16[16,128,256]{2,1,0:T(8,128)(2,1)S(1)}, bf16[128,4096]{1,0:T(8,128)(2,1)S(1)}, f32[8,128]{1,0:T(8,128)S(1)}, f32[8,256]{1,0:T(8,128)S(1)}) custom-call(bf16[32,4096]{1,0:T(8,128)(2,1)S(1)} %get-tuple-element.30.refs_0_, s32[2,512]{1,0:T(2,128)S(1)} %get-tuple-element.27.refs_1_.refs_2_, bf16[256,4096]{1,0:T(8,128)(2,1)S(1)} %copy-done, ...), custom_call_target="tpu_custom_call" | custom-call | tf_op jit(solution)/shard_map/scores/pallas_call | solution.py:324
  10.9 4.8 %collective-permute-done.refs_0_ = bf16[32,4096]{1,0:T(8,128)(2,1)S(1)} collective-permute-done((bf16[32,4096]{1,0:T(8,128)(2,1)}, bf16[32,4096]{1,0:T(8,128)(2,1)S(1)}, u32[]{:S(2)}, u32[]{:S(2)}) %collective-permute-start) | collective-permute-done | bytes 262176 | tf_op jit(solution)/shard_map/ppermute | solution.py:342
  15.8 0.0 copy-start.1
  15.8 2.0 %scores.5 = (bf16[16,128,256]{2,1,0:T(8,128)(2,1)S(1)}, bf16[128,4096]{1,0:T(8,128)(2,1)S(1)}, f32[8,128]{1,0:T(8,128)S(1)}) custom-call(bf16[32,4096]{1,0:T(8,128)(2,1)S(1)} %collective-permute-done.refs_0_, s32[2,512]{1,0:T(2,128)S(1)} %get-tuple-element.27.refs_1_.refs_2_, ...), custom_call_target="tpu_custom_call", output_to_operand_aliasing={{0}: (6, {}), {1}: (7, {}), {2}: (8, {})} | custom-call | tf_op jit(solution)/shard_map/scores/pallas_call | solution.py:324
  17.8 0.5 collective-permute-done.1.refs_0_
  18.3 0.0 copy-done.1
  18.3 0.7 %collective-permute-start.3 = (bf16[32,4096]{1,0:T(8,128)(2,1)S(1)}, bf16[32,4096]{1,0:T(8,128)(2,1)S(1)}, u32[]{:S(2)}, u32[]{:S(2)}) collective-permute-start(bf16[32,4096]{1,0:T(8,128)(2,1)S(1)} %copy-done.1), channel_id=1, source_target_pairs={{4,8},{8,4},{5,9},{9,5},{6,10},{10,6},{7,11},{11,7},{20,24},{24,20... | collective-permute-start | bytes 786440 | tf_op jit(solution)/shard_map/ppermute | solution.py:427
  19.0 1.3 %collective-permute-start.2 = (bf16[32,4096]{1,0:T(8,128)(2,1)S(1)}, bf16[32,4096]{1,0:T(8,128)(2,1)S(1)}, u32[]{:S(2)}, u32[]{:S(2)}) collective-permute-start(bf16[32,4096]{1,0:T(8,128)(2,1)S(1)} %collective-permute-done.1.refs_0_), channel_id=1, source_target_pairs={{4,0},{8,12},{5,1},{9,13},{6,2},{10,14},{7,3},{11,15},{20,16},{24,... | collective-permute-start | bytes 786440 | tf_op jit(solution)/shard_map/ppermute | solution.py:426
  20.3 2.0 %scores.6 = (bf16[16,128,256]{2,1,0:T(8,128)(2,1)S(1)}, bf16[128,4096]{1,0:T(8,128)(2,1)S(1)}, f32[8,128]{1,0:T(8,128)S(1)}) custom-call(bf16[32,4096]{1,0:T(8,128)(2,1)S(1)} %collective-permute-done.1.refs_0_, s32[2,512]{1,0:T(2,128)S(1)} %get-tuple-element.27.refs_1_.refs_2_, ...), custom_call_target="tpu_custom_call", output_to_operand_aliasing={{0}: (6, {}), {1}: (7, {}), {2}: (8, {})} | custom-call | tf_op jit(solution)/shard_map/scores/pallas_call | solution.py:324
  22.3 0.0 collective-permute-done.3.refs_1_
  22.3 5.5 %collective-permute-done.2.refs_0_ = bf16[32,4096]{1,0:T(8,128)(2,1)S(1)} collective-permute-done((bf16[32,4096]{1,0:T(8,128)(2,1)S(1)}, bf16[32,4096]{1,0:T(8,128)(2,1)S(1)}, u32[]{:S(2)}, u32[]{:S(2)}) %collective-permute-start.2) | collective-permute-done | bytes 262176 | tf_op jit(solution)/shard_map/ppermute | solution.py:426
  27.9 2.0 %scores.7 = (bf16[16,128,256]{2,1,0:T(8,128)(2,1)S(1)}, bf16[128,4096]{1,0:T(8,128)(2,1)S(1)}, f32[8,128]{1,0:T(8,128)S(1)}) custom-call(bf16[32,4096]{1,0:T(8,128)(2,1)S(1)} %collective-permute-done.2.refs_0_, bf16[32,4096]{1,0:T(8,128)(2,1)S(1)} %collective-permute-done.3.refs_1_, ...), custom_call_target="tpu_custom_call", output_to_operand_aliasing={{0}: (7, {}), {1}: (8, {}), {2}: (9, {})} | custom-call | tf_op jit(solution)/shard_map/scores/pallas_call | solution.py:324
  29.9 0.0 collective-permute-start.6
  29.9 2.9 %collective-permute-start.5 = (f32[8,128]{1,0:T(8,128)S(1)}, f32[8,128]{1,0:T(8,128)S(1)}, u32[]{:S(2)}, u32[]{:S(2)}) collective-permute-start(f32[8,128]{1,0:T(8,128)S(1)} %get-tuple-element.47.rest_0_), channel_id=1, source_target_pairs={{0,8},{4,12},{8,0},{12,4},{1,9},{5,13},{9,1},{13,5},{2,10},{6,14},... | collective-permute-start | bytes 12296 | tf_op jit(solution)/shard_map/ppermute | solution.py:342
  32.9 1.4 %collective-permute-start.4 = (f32[8,128]{1,0:T(8,128)S(1)}, f32[8,128]{1,0:T(8,128)S(1)}, u32[]{:S(2)}, u32[]{:S(2)}) collective-permute-start(f32[8,128]{1,0:T(8,128)S(1)} %get-tuple-element.47.rest_0_), channel_id=1, source_target_pairs={{0,12},{4,8},{8,4},{12,0},{1,13},{5,9},{9,5},{13,1},{2,14},{6,10},... | collective-permute-start | bytes 12296 | tf_op jit(solution)/shard_map/ppermute | solution.py:342
  34.3 0.0 collective-permute-done.6.rest_3_
  34.3 0.2 collective-permute-done.5.rest_2_
  34.5 3.8 %collective-permute-done.4.rest_1_ = f32[8,128]{1,0:T(8,128)S(1)} collective-permute-done((f32[8,128]{1,0:T(8,128)S(1)}, f32[8,128]{1,0:T(8,128)S(1)}, u32[]{:S(2)}, u32[]{:S(2)}) %collective-permute-start.4) | collective-permute-done | bytes 4128 | tf_op jit(solution)/shard_map/ppermute | solution.py:342
  38.3 1.1 %bricks.1 = bf16[16,8,640]{2,1,0:T(8,128)(2,1)S(1)} custom-call(bf16[16,128,256]{2,1,0:T(8,128)(2,1)S(1)} %get-tuple-element.44.terms_ref, bf16[128,4096]{1,0:T(8,128)(2,1)S(1)} %get-tuple-element.45.based_ref, bf16[128,256]{1,0:T(8,128)(2,1)S(1)} %get-tuple-element.46.hit_ref, f32[8,2048]{1,0:T(8,128)S(1)} %get-tuple-element.28.refs_3_.refs_4_.cos_ref, ...), custom_call_target="tpu_custom_call" | custom-call | tf_op jit(solution)/shard_map/bricks/pallas_call | solution.py:324
  39.4 11.9 %all_to_all.5.arrived_ref = bf16[16,8,640]{2,1,0:T(8,128)(2,1)S(1)} all-to-all(bf16[16,8,640]{2,1,0:T(8,128)(2,1)S(1)} %bricks.1), channel_id=1, replica_groups=mesh['groups'=2,'orient'=4,'img'=2,'brick'=2] {'orient','img','brick'}, dimensions={0} | all-to-all | bytes 327680 | tf_op jit(solution)/shard_map/all_to_all | solution.py:441
  51.3 1.1 %insert.1 = (f32[1,2,256]{2,1,0:T(2,128)}, f32[1,1,256]{2,1,0:T(1,128)}) custom-call(bf16[16,8,640]{2,1,0:T(8,128)(2,1)S(1)} %all_to_all.5.arrived_ref, bf16[256,4096]{1,0:T(8,128)(2,1)S(1)} %get-tuple-element.48.weight_ref, f32[8,256]{1,0:T(8,128)S(1)} %get-tuple-element.49.cover_ref), custom_call_target="tpu_custom_call" | custom-call | tf_op jit(solution)/shard_map/insert/pallas_call | solution.py:324
Async XLA Ops:
  0.6 7.8 %copy-start = (bf16[256,4096]{1,0:T(8,128)(2,1)S(1)}, bf16[256,4096]{1,0:T(8,128)(2,1)}, u32[]{:S(2)}) copy-start(bf16[256,4096]{1,0:T(8,128)(2,1)} %refs_3_.1) | copy-start | bytes 6291460
  0.6 15.1 %collective-permute-start = (bf16[32,4096]{1,0:T(8,128)(2,1)}, bf16[32,4096]{1,0:T(8,128)(2,1)S(1)}, u32[]{:S(2)}, u32[]{:S(2)}) collective-permute-start(bf16[32,4096]{1,0:T(8,128)(2,1)} %images_hbm.1), channel_id=1, source_target_pairs={{0,4},{4,0},{8,12},{12,8},{1,5},{5,1},{9,13},{13,9},{2,6},{6,2},{1... | collective-permute-start | bytes 786440 | tf_op jit(solution)/shard_map/ppermute | solution.py:342
  3.8 14.6 %collective-permute-start.1 = (bf16[32,4096]{1,0:T(8,128)(2,1)}, bf16[32,4096]{1,0:T(8,128)(2,1)S(1)}, u32[]{:S(2)}, u32[]{:S(2)}) collective-permute-start(bf16[32,4096]{1,0:T(8,128)(2,1)} %images_hbm.1), channel_id=1, source_target_pairs={{0,8},{4,12},{8,0},{12,4},{1,9},{5,13},{9,1},{13,5},{2,10},{6,14},... | collective-permute-start | bytes 786440 | tf_op jit(solution)/shard_map/ppermute | solution.py:342
  15.8 2.6 %copy-start.1 = (bf16[32,4096]{1,0:T(8,128)(2,1)S(1)}, bf16[32,4096]{1,0:T(8,128)(2,1)}, u32[]{:S(2)}) copy-start(bf16[32,4096]{1,0:T(8,128)(2,1)} %images_hbm.1) | copy-start | bytes 786436
  18.3 4.0 %collective-permute-start.3 = (bf16[32,4096]{1,0:T(8,128)(2,1)S(1)}, bf16[32,4096]{1,0:T(8,128)(2,1)S(1)}, u32[]{:S(2)}, u32[]{:S(2)}) collective-permute-start(bf16[32,4096]{1,0:T(8,128)(2,1)S(1)} %copy-done.1), channel_id=1, source_target_pairs={{4,8},{8,4},{5,9},{9,5},{6,10},{10,6},{7,11},{11,7},{20,24},{24,20... | collective-permute-start | bytes 786440 | tf_op jit(solution)/shard_map/ppermute | solution.py:427
  19.0 8.9 %collective-permute-start.2 = (bf16[32,4096]{1,0:T(8,128)(2,1)S(1)}, bf16[32,4096]{1,0:T(8,128)(2,1)S(1)}, u32[]{:S(2)}, u32[]{:S(2)}) collective-permute-start(bf16[32,4096]{1,0:T(8,128)(2,1)S(1)} %collective-permute-done.1.refs_0_), channel_id=1, source_target_pairs={{4,0},{8,12},{5,1},{9,13},{6,2},{10,14},{7,3},{11,15},{20,16},{24,... | collective-permute-start | bytes 786440 | tf_op jit(solution)/shard_map/ppermute | solution.py:426
  29.9 4.4 %collective-permute-start.6 = (f32[8,128]{1,0:T(8,128)S(1)}, f32[8,128]{1,0:T(8,128)S(1)}, u32[]{:S(2)}, u32[]{:S(2)}) collective-permute-start(f32[8,128]{1,0:T(8,128)S(1)} %get-tuple-element.47.rest_0_), channel_id=1, source_target_pairs={{0,4},{4,0},{8,12},{12,8},{1,5},{5,1},{9,13},{13,9},{2,6},{6,2},{1... | collective-permute-start | bytes 12296 | tf_op jit(solution)/shard_map/ppermute | solution.py:342
  29.9 4.6 %collective-permute-start.5 = (f32[8,128]{1,0:T(8,128)S(1)}, f32[8,128]{1,0:T(8,128)S(1)}, u32[]{:S(2)}, u32[]{:S(2)}) collective-permute-start(f32[8,128]{1,0:T(8,128)S(1)} %get-tuple-element.47.rest_0_), channel_id=1, source_target_pairs={{0,8},{4,12},{8,0},{12,4},{1,9},{5,13},{9,1},{13,5},{2,10},{6,14},... | collective-permute-start | bytes 12296 | tf_op jit(solution)/shard_map/ppermute | solution.py:342
  32.9 5.4 %collective-permute-start.4 = (f32[8,128]{1,0:T(8,128)S(1)}, f32[8,128]{1,0:T(8,128)S(1)}, u32[]{:S(2)}, u32[]{:S(2)}) collective-permute-start(f32[8,128]{1,0:T(8,128)S(1)} %get-tuple-element.47.rest_0_), channel_id=1, source_target_pairs={{0,12},{4,8},{8,4},{12,0},{1,13},{5,9},{9,5},{13,1},{2,14},{6,10},... | collective-permute-start | bytes 12296 | tf_op jit(solution)/shard_map/ppermute | solution.py:342

commit v4 on v3

--- a/solution.py
+++ b/solution.py
@@ -110,12 +110,8 @@
 
 
 def source_plane(source):
-    kind, amount = source
-    plane = lax.axis_index("orient")
-    if kind == "xor":
-        return jnp.bitwise_xor(plane, amount)
-    count = lax.axis_size("orient")
-    return lax.rem(plane + count - amount, count)
+    factor, offset, modulus = source
+    return lax.rem(factor * lax.axis_index("orient") + offset, modulus)
 
 
 def score_kernel(first, source, choices, *refs):
@@ -220,9 +216,24 @@
     stats_ref[...] = part if first else part + stats_in_ref[...]
 
 
-def brick_kernel(others, terms_ref, based_ref, hit_ref, cos_ref, sin_ref, *rest):
+def share_kernel(terms_ref, hit_ref, share_ref):
+    for t in range(PAIRS):
+        plus, minus = (
+            lax.dot_general(
+                hit_ref[...],
+                terms_ref[2 * t + i],
+                (((1,), (1,)), ((), ())),
+                preferred_element_type=jnp.float32,
+            )
+            for i in range(2)
+        )
+        share_ref[2 * t] = plus + minus
+        share_ref[2 * t + 1] = plus - minus
+
+
+def brick_kernel(others, share_ref, based_ref, cos_ref, sin_ref, *rest):
     stats_refs, (out_ref, pairs_ref, sums_ref) = rest[:others], rest[others:]
-    bricks = hit_ref.shape[0] // NSEG
+    bricks = share_ref.shape[1] // NSEG
     count = based_ref.shape[0]
     own_top = stats_refs[0][0:1, :]
     top = own_top
@@ -234,17 +245,8 @@
     factor = jnp.exp(own_top - top) / mass
     mass_sum = jnp.zeros((NSEG * bricks, count), jnp.float32)
     for t in range(PAIRS):
-        plus, minus = (
-            lax.dot_general(
-                hit_ref[...],
-                terms_ref[2 * t + i],
-                (((1,), (1,)), ((), ())),
-                preferred_element_type=jnp.float32,
-            )
-            for i in range(2)
-        )
-        even = (plus + minus) * factor
-        odd = (plus - minus) * factor
+        even = share_ref[2 * t] * factor
+        odd = share_ref[2 * t + 1] * factor
         mass_sum = mass_sum + even
         for j in range(NSEG):
             at = slice(j * bricks, (j + 1) * bricks)
@@ -354,6 +356,12 @@
     return [array] + [swap(array, k) for k in (3, 2, 1)]
 
 
+def after(state, images):
+    terms, based, stats = state
+    stats, images = lax.optimization_barrier((stats, images))
+    return [terms, based, stats], images
+
+
 def per_device(images, offsets, slices, seg_map, interp):
     orient_count = lax.axis_size("orient")
     group_count = lax.axis_size("img") * lax.axis_size("brick")
@@ -365,11 +373,12 @@
     f32, bf16 = jnp.float32, jnp.bfloat16
     relay = orient_count == 4
     if relay:
-        far = swap(images, 2)
-        near = swap(images, 1)
-        waiting = [(("xor", 1), [near])]
+        first = lax.ppermute(images, "orient", [(0, 2), (3, 1), (2, 3), (1, 0)])
     else:
-        waiting = [(("shift", k), [shift(images, k)]) for k in range(1, orient_count)]
+        waiting = [
+            ((1, orient_count - k, orient_count), shift(images, k))
+            for k in range(1, orient_count)
+        ]
 
     weights, cover, hit, cos_table, sin_table, own, offsets_v = call(
         functools.partial(setup_kernel, bricks),
@@ -416,23 +425,32 @@
             aliases={} if first else {at + i: i for i in range(3)},
         )
 
-    *state, norm = scored(("shift", 0), [own], None)
-    for source, arrays in waiting:
-        state = scored(source, arrays, [norm, *state])
+    *state, norm = scored((1, 0, orient_count), [own], None)
     if relay:
-        terms, based, stats = state
-        stats, far, again = lax.optimization_barrier((stats, far, images))
-        state = [terms, based, stats]
-        relayed = lax.ppermute(far, "orient", [(1, 0), (2, 3)])
+        state, again = after(state, images)
+        second = lax.ppermute(again, "orient", [(0, 1), (3, 2), (1, 3), (2, 0)])
+        first, again = lax.optimization_barrier((first, again))
+        relayed = lax.ppermute(first, "orient", [(2, 3), (1, 0)])
         middle = lax.ppermute(again, "orient", [(1, 2), (2, 1)])
-        state = scored(("xor", 2), [far], [norm, *state])
-        state = scored(("xor", 3), [relayed, middle], [norm, *state])
+        state = scored((2, 1, 5), [first], [norm, *state])
+        state = scored((3, 2, 5), [second], [norm, *state])
+        state = scored((4, 3, 5), [relayed, middle], [norm, *state])
+    else:
+        for source, array in waiting:
+            state = scored(source, [array], [norm, *state])
     terms, based, stats = state
+    gathered = everyone(stats)
+    shares = call(
+        share_kernel,
+        "shares",
+        jax.ShapeDtypeStruct((SHIFTS, NSEG * bricks, count), f32),
+        on_chip(terms, hit),
+    )
     outgoing = call(
         functools.partial(brick_kernel, orient_count),
         "bricks",
         jax.ShapeDtypeStruct((bricks, NSEG, 2 * SEG + LANES), bf16),
-        on_chip(terms, based, hit) + [cos_table, sin_table] + on_chip(*everyone(stats)),
+        on_chip(shares, based, cos_table, sin_table, *gathered),
         scratch=[
             pltpu.VMEM((NSEG, SHIFTS * bricks, count), bf16),
             pltpu.VMEM((bricks, NSEG, 2 * SEG + LANES), f32),

time: 52.6 us -> 47.5 us (0.903)
  waiting for transfers between devices: 14.9 us -> 10.4 us
  starting transfers between devices: 12.1 us -> 10.5 us
  blocking collectives: 11.9 us -> 12.5 us
    ppermute x5 -> x3, waiting for transfers between devices: 9.33 us -> 2.13 us  [swap(): lax.ppermute(array, 'orient', [(i, i ^ amount) for i in range(count)])]
    ppermute x5 -> x3, starting transfers between devices: 10.1 us -> 4.42 us  [swap(): lax.ppermute(array, 'orient', [(i, i ^ amount) for i in range(count)])]
    ppermute x1 -> x3, starting transfers between devices: 1.29 us -> 5.45 us  [the longest x1 4.12 us: per_device(): first = lax.ppermute(images, 'orient', [(0, 2), (3, 1), (2, 3), (1, 0)])]
    ppermute x1 -> x3, waiting for transfers between devices: 5.52 us -> 8.24 us  [the longest x1 3.37 us: per_device(): relayed = lax.ppermute(first, 'orient', [(2, 3), (1, 0)])]
    all_to_all x1, blocking collectives: 11.9 us -> 12.5 us  [per_device(): lax.all_to_all(outgoing, ('orient', 'img', 'brick'), split_axis=0, concat...]
    pallas_call x7 -> x8, Pallas kernels: 12.9 us -> 13.1 us  [call(): pl.pallas_call(kernel, in_specs=[in_spec] * len(inputs), out_specs=[spec]...]
  transfers between devices with their start and end apart: 7 -> 7, of which waited for: 5 -> 5; matrix products, arithmetic and copies ran while one was open for 0% -> 0% of each run, Pallas kernels for 16% -> 19%
where the time goes in v4:
time: 47.5 us; the launch traced here: 47.3 us
  Pallas kernels  13.1 us (28%)
  blocking collectives  12.5 us (26%)
  starting transfers between devices  10.5 us (22%)
  waiting for transfers between devices  10.4 us (22%)
  between operations  0.7 us (1%)
    pallas_call x8, Pallas kernels, call(): pl.pallas_call(kernel, in_specs=[in_spec] * len(inputs), out_specs=[spec]...  13.1 us
    all_to_all x1, blocking collectives, per_device(): lax.all_to_all(outgoing, ('orient', 'img', 'brick'), split_axis=0, concat...  12.5 us
    ppermute x3, starting transfers between devices, swap(): lax.ppermute(array, 'orient', [(i, i ^ amount) for i in range(count)])  4.42 us
    ppermute x1, starting transfers between devices, per_device(): first = lax.ppermute(images, 'orient', [(0, 2), (3, 1), (2, 3), (1, 0)])  4.12 us
    ppermute x1, waiting for transfers between devices, per_device(): relayed = lax.ppermute(first, 'orient', [(2, 3), (1, 0)])  3.37 us
    ppermute x1, waiting for transfers between devices, per_device(): second = lax.ppermute(again, 'orient', [(0, 1), (3, 2), (1, 3), (2, 0)])  2.54 us
    ppermute x1, waiting for transfers between devices, per_device(): first = lax.ppermute(images, 'orient', [(0, 2), (3, 1), (2, 3), (1, 0)])  2.33 us
    ppermute x3, waiting for transfers between devices, swap(): lax.ppermute(array, 'orient', [(i, i ^ amount) for i in range(count)])  2.13 us
  transfers between devices with their start and end apart: 7, of which 5 were waited for; matrix products, arithmetic and copies ran while one was open for 0% of the time, Pallas kernels for 19%

profile of v4, /device:TPU:0, one launch (start us, length us, event | category | flops | bytes accessed | tf_op | source)
XLA Modules:
  0.0 47.3 jit_solution(1022114406167737923)
XLA Ops:
  0.6 0.0 copy-start
  0.6 4.1 %collective-permute-start = (bf16[32,4096]{1,0:T(8,128)(2,1)}, bf16[32,4096]{1,0:T(8,128)(2,1)S(1)}, u32[]{:S(2)}, u32[]{:S(2)}) collective-permute-start(bf16[32,4096]{1,0:T(8,128)(2,1)} %images_hbm.1), channel_id=1, source_target_pairs={{0,8},{12,4},{8,12},{4,0},{1,9},{13,5},{9,13},{5,1},{2,10},{14,6},... | collective-permute-start | bytes 786440 | tf_op jit(solution)/shard_map/ppermute | solution.py:376
  4.8 0.0 copy-start.1
  4.8 2.1 %setup.1 = (bf16[256,4096]{1,0:T(8,128)(2,1)S(1)}, f32[8,256]{1,0:T(8,128)S(1)}, bf16[128,256]{1,0:T(8,128)(2,1)S(1)}, f32[8,2048]{1,0:T(8,128)S(1)}, f32[8,2048...) custom-call(s32[1,8,256,256]{3,2,1,0:T(8,128)} %interp_hbm.1, s32[64,128]{1,0:T(8,128)} %bitcast.3, ...), custom_call_target="tpu_custom_call" | custom-call | tf_op jit(solution)/shard_map/setup/pallas_call | solution.py:326
  6.9 0.0 copy-done
  6.9 2.5 %scores.4 = (bf16[16,128,256]{2,1,0:T(8,128)(2,1)S(1)}, bf16[128,4096]{1,0:T(8,128)(2,1)S(1)}, f32[8,128]{1,0:T(8,128)S(1)}, f32[8,256]{1,0:T(8,128)S(1)}) custom-call(bf16[32,4096]{1,0:T(8,128)(2,1)S(1)} %get-tuple-element.28.refs_0_, s32[2,512]{1,0:T(2,128)S(1)} %get-tuple-element.29.refs_1_.refs_2_, bf16[256,4096]{1,0:T(8,128)(2,1)S(1)} %copy-done, ...), custom_call_target="tpu_custom_call" | custom-call | tf_op jit(solution)/shard_map/scores/pallas_call | solution.py:326
  9.4 0.0 copy-done.1
  9.4 0.1 collective-permute-start.3
  9.4 2.3 %collective-permute-done.refs_0_ = bf16[32,4096]{1,0:T(8,128)(2,1)S(1)} collective-permute-done((bf16[32,4096]{1,0:T(8,128)(2,1)}, bf16[32,4096]{1,0:T(8,128)(2,1)S(1)}, u32[]{:S(2)}, u32[]{:S(2)}) %collective-permute-start) | collective-permute-done | bytes 262176 | tf_op jit(solution)/shard_map/ppermute | solution.py:376
  11.8 1.3 %collective-permute-start.1 = (bf16[32,4096]{1,0:T(8,128)(2,1)S(1)}, bf16[32,4096]{1,0:T(8,128)(2,1)S(1)}, u32[]{:S(2)}, u32[]{:S(2)}) collective-permute-start(bf16[32,4096]{1,0:T(8,128)(2,1)S(1)} %collective-permute-done.refs_0_), channel_id=1, source_target_pairs={{8,12},{4,0},{9,13},{5,1},{10,14},{6,2},{11,15},{7,3},{24,28},{20,... | collective-permute-start | bytes 786440 | tf_op jit(solution)/shard_map/ppermute | solution.py:433
  13.1 0.7 %collective-permute-start.2 = (bf16[32,4096]{1,0:T(8,128)(2,1)S(1)}, bf16[32,4096]{1,0:T(8,128)(2,1)S(1)}, u32[]{:S(2)}, u32[]{:S(2)}) collective-permute-start(bf16[32,4096]{1,0:T(8,128)(2,1)S(1)} %copy-done.1), channel_id=1, source_target_pairs={{4,8},{8,4},{5,9},{9,5},{6,10},{10,6},{7,11},{11,7},{20,24},{24,20... | collective-permute-start | bytes 786440 | tf_op jit(solution)/shard_map/ppermute | solution.py:434
  13.7 2.0 %scores.5 = (bf16[16,128,256]{2,1,0:T(8,128)(2,1)S(1)}, bf16[128,4096]{1,0:T(8,128)(2,1)S(1)}, f32[8,128]{1,0:T(8,128)S(1)}) custom-call(bf16[32,4096]{1,0:T(8,128)(2,1)S(1)} %collective-permute-done.refs_0_, s32[2,512]{1,0:T(2,128)S(1)} %get-tuple-element.29.refs_1_.refs_2_, ...), custom_call_target="tpu_custom_call", output_to_operand_aliasing={{0}: (6, {}), {1}: (7, {}), {2}: (8, {})} | custom-call | tf_op jit(solution)/shard_map/scores/pallas_call | solution.py:326
  15.8 2.5 %collective-permute-done.3.refs_0_ = bf16[32,4096]{1,0:T(8,128)(2,1)S(1)} collective-permute-done((bf16[32,4096]{1,0:T(8,128)(2,1)S(1)}, bf16[32,4096]{1,0:T(8,128)(2,1)S(1)}, u32[]{:S(2)}, u32[]{:S(2)}) %collective-permute-start.3) | collective-permute-done | bytes 262176 | tf_op jit(solution)/shard_map/ppermute | solution.py:431
  18.3 2.0 %scores.6 = (bf16[16,128,256]{2,1,0:T(8,128)(2,1)S(1)}, bf16[128,4096]{1,0:T(8,128)(2,1)S(1)}, f32[8,128]{1,0:T(8,128)S(1)}) custom-call(bf16[32,4096]{1,0:T(8,128)(2,1)S(1)} %collective-permute-done.3.refs_0_, s32[2,512]{1,0:T(2,128)S(1)} %get-tuple-element.29.refs_1_.refs_2_, ...), custom_call_target="tpu_custom_call", output_to_operand_aliasing={{0}: (6, {}), {1}: (7, {}), {2}: (8, {})} | custom-call | tf_op jit(solution)/shard_map/scores/pallas_call | solution.py:326
  20.3 3.4 %collective-permute-done.1.refs_0_ = bf16[32,4096]{1,0:T(8,128)(2,1)S(1)} collective-permute-done((bf16[32,4096]{1,0:T(8,128)(2,1)S(1)}, bf16[32,4096]{1,0:T(8,128)(2,1)S(1)}, u32[]{:S(2)}, u32[]{:S(2)}) %collective-permute-start.1) | collective-permute-done | bytes 262176 | tf_op jit(solution)/shard_map/ppermute | solution.py:433
  23.7 0.0 collective-permute-done.2.refs_1_
  23.7 2.1 %scores.7 = (bf16[16,128,256]{2,1,0:T(8,128)(2,1)S(1)}, bf16[128,4096]{1,0:T(8,128)(2,1)S(1)}, f32[8,128]{1,0:T(8,128)S(1)}) custom-call(bf16[32,4096]{1,0:T(8,128)(2,1)S(1)} %collective-permute-done.1.refs_0_, bf16[32,4096]{1,0:T(8,128)(2,1)S(1)} %collective-permute-done.2.refs_1_, ...), custom_call_target="tpu_custom_call", output_to_operand_aliasing={{0}: (7, {}), {1}: (8, {}), {2}: (9, {})} | custom-call | tf_op jit(solution)/shard_map/scores/pallas_call | solution.py:326
  25.8 2.5 %collective-permute-start.4 = (f32[8,128]{1,0:T(8,128)S(1)}, f32[8,128]{1,0:T(8,128)S(1)}, u32[]{:S(2)}, u32[]{:S(2)}) collective-permute-start(f32[8,128]{1,0:T(8,128)S(1)} %get-tuple-element.49.rest_0_), channel_id=1, source_target_pairs={{0,12},{4,8},{8,4},{12,0},{1,13},{5,9},{9,5},{13,1},{2,14},{6,10},... | collective-permute-start | bytes 12296 | tf_op jit(solution)/shard_map/ppermute | solution.py:344
  28.3 0.0 collective-permute-start.5
  28.3 1.9 %collective-permute-start.6 = (f32[8,128]{1,0:T(8,128)S(1)}, f32[8,128]{1,0:T(8,128)S(1)}, u32[]{:S(2)}, u32[]{:S(2)}) collective-permute-start(f32[8,128]{1,0:T(8,128)S(1)} %get-tuple-element.49.rest_0_), channel_id=1, source_target_pairs={{0,4},{4,0},{8,12},{12,8},{1,5},{5,1},{9,13},{13,9},{2,6},{6,2},{1... | collective-permute-start | bytes 12296 | tf_op jit(solution)/shard_map/ppermute | solution.py:344
  30.2 0.4 shares.1.share_ref
  30.6 0.6 %collective-permute-done.4.rest_1_ = f32[8,128]{1,0:T(8,128)S(1)} collective-permute-done((f32[8,128]{1,0:T(8,128)S(1)}, f32[8,128]{1,0:T(8,128)S(1)}, u32[]{:S(2)}, u32[]{:S(2)}) %collective-permute-start.4) | collective-permute-done | bytes 4128 | tf_op jit(solution)/shard_map/ppermute | solution.py:344
  31.2 1.6 %collective-permute-done.5.rest_2_ = f32[8,128]{1,0:T(8,128)S(1)} collective-permute-done((f32[8,128]{1,0:T(8,128)S(1)}, f32[8,128]{1,0:T(8,128)S(1)}, u32[]{:S(2)}, u32[]{:S(2)}) %collective-permute-start.5) | collective-permute-done | bytes 4128 | tf_op jit(solution)/shard_map/ppermute | solution.py:344
  32.8 0.0 collective-permute-done.6.rest_3_
  32.8 0.8 %bricks.1 = bf16[16,8,640]{2,1,0:T(8,128)(2,1)S(1)} custom-call(f32[16,128,128]{2,1,0:T(8,128)S(1)} %shares.1.share_ref, bf16[128,4096]{1,0:T(8,128)(2,1)S(1)} %get-tuple-element.48.based_ref, f32[8,2048]{1,0:T(8,128)S(1)} %get-tuple-element.30.refs_3_.refs_4_.cos_ref, f32[8,2048]{1,0:T(8,128)S(1)} %get-tuple-element.31.refs_4_.refs_5_.sin_ref, ...), custom_call_target="tpu_custom_call" | custom-call | tf_op jit(solution)/shard_map/bricks/pallas_call | solution.py:326
  33.6 12.5 %all_to_all.5.arrived_ref = bf16[16,8,640]{2,1,0:T(8,128)(2,1)S(1)} all-to-all(bf16[16,8,640]{2,1,0:T(8,128)(2,1)S(1)} %bricks.1), channel_id=1, replica_groups=mesh['groups'=2,'orient'=4,'img'=2,'brick'=2] {'orient','img','brick'}, dimensions={0} | all-to-all | bytes 327680 | tf_op jit(solution)/shard_map/all_to_all | solution.py:459
  46.2 1.1 %insert.1 = (f32[1,2,256]{2,1,0:T(2,128)}, f32[1,1,256]{2,1,0:T(1,128)}) custom-call(bf16[16,8,640]{2,1,0:T(8,128)(2,1)S(1)} %all_to_all.5.arrived_ref, bf16[256,4096]{1,0:T(8,128)(2,1)S(1)} %get-tuple-element.50.weight_ref, f32[8,256]{1,0:T(8,128)S(1)} %get-tuple-element.51.cover_ref), custom_call_target="tpu_custom_call" | custom-call | tf_op jit(solution)/shard_map/insert/pallas_call | solution.py:326
Async XLA Ops:
  0.6 6.3 %copy-start = (bf16[256,4096]{1,0:T(8,128)(2,1)S(1)}, bf16[256,4096]{1,0:T(8,128)(2,1)}, u32[]{:S(2)}) copy-start(bf16[256,4096]{1,0:T(8,128)(2,1)} %refs_3_.1) | copy-start | bytes 6291460
  0.6 11.1 %collective-permute-start = (bf16[32,4096]{1,0:T(8,128)(2,1)}, bf16[32,4096]{1,0:T(8,128)(2,1)S(1)}, u32[]{:S(2)}, u32[]{:S(2)}) collective-permute-start(bf16[32,4096]{1,0:T(8,128)(2,1)} %images_hbm.1), channel_id=1, source_target_pairs={{0,8},{12,4},{8,12},{4,0},{1,9},{13,5},{9,13},{5,1},{2,10},{14,6},... | collective-permute-start | bytes 786440 | tf_op jit(solution)/shard_map/ppermute | solution.py:376
  4.8 4.6 %copy-start.1 = (bf16[32,4096]{1,0:T(8,128)(2,1)S(1)}, bf16[32,4096]{1,0:T(8,128)(2,1)}, u32[]{:S(2)}) copy-start(bf16[32,4096]{1,0:T(8,128)(2,1)} %images_hbm.1) | copy-start | bytes 786436
  9.4 8.9 %collective-permute-start.3 = (bf16[32,4096]{1,0:T(8,128)(2,1)S(1)}, bf16[32,4096]{1,0:T(8,128)(2,1)S(1)}, u32[]{:S(2)}, u32[]{:S(2)}) collective-permute-start(bf16[32,4096]{1,0:T(8,128)(2,1)S(1)} %copy-done.1), channel_id=1, source_target_pairs={{0,4},{12,8},{4,12},{8,0},{1,5},{13,9},{5,13},{9,1},{2,6},{14,10},... | collective-permute-start | bytes 786440 | tf_op jit(solution)/shard_map/ppermute | solution.py:431
  11.8 11.9 %collective-permute-start.1 = (bf16[32,4096]{1,0:T(8,128)(2,1)S(1)}, bf16[32,4096]{1,0:T(8,128)(2,1)S(1)}, u32[]{:S(2)}, u32[]{:S(2)}) collective-permute-start(bf16[32,4096]{1,0:T(8,128)(2,1)S(1)} %collective-permute-done.refs_0_), channel_id=1, source_target_pairs={{8,12},{4,0},{9,13},{5,1},{10,14},{6,2},{11,15},{7,3},{24,28},{20,... | collective-permute-start | bytes 786440 | tf_op jit(solution)/shard_map/ppermute | solution.py:433
  13.1 10.7 %collective-permute-start.2 = (bf16[32,4096]{1,0:T(8,128)(2,1)S(1)}, bf16[32,4096]{1,0:T(8,128)(2,1)S(1)}, u32[]{:S(2)}, u32[]{:S(2)}) collective-permute-start(bf16[32,4096]{1,0:T(8,128)(2,1)S(1)} %copy-done.1), channel_id=1, source_target_pairs={{4,8},{8,4},{5,9},{9,5},{6,10},{10,6},{7,11},{11,7},{20,24},{24,20... | collective-permute-start | bytes 786440 | tf_op jit(solution)/shard_map/ppermute | solution.py:434
  25.8 5.4 %collective-permute-start.4 = (f32[8,128]{1,0:T(8,128)S(1)}, f32[8,128]{1,0:T(8,128)S(1)}, u32[]{:S(2)}, u32[]{:S(2)}) collective-permute-start(f32[8,128]{1,0:T(8,128)S(1)} %get-tuple-element.49.rest_0_), channel_id=1, source_target_pairs={{0,12},{4,8},{8,4},{12,0},{1,13},{5,9},{9,5},{13,1},{2,14},{6,10},... | collective-permute-start | bytes 12296 | tf_op jit(solution)/shard_map/ppermute | solution.py:344
  28.3 4.5 %collective-permute-start.5 = (f32[8,128]{1,0:T(8,128)S(1)}, f32[8,128]{1,0:T(8,128)S(1)}, u32[]{:S(2)}, u32[]{:S(2)}) collective-permute-start(f32[8,128]{1,0:T(8,128)S(1)} %get-tuple-element.49.rest_0_), channel_id=1, source_target_pairs={{0,8},{4,12},{8,0},{12,4},{1,9},{5,13},{9,1},{13,5},{2,10},{6,14},... | collective-permute-start | bytes 12296 | tf_op jit(solution)/shard_map/ppermute | solution.py:344
  28.3 4.5 %collective-permute-start.6 = (f32[8,128]{1,0:T(8,128)S(1)}, f32[8,128]{1,0:T(8,128)S(1)}, u32[]{:S(2)}, u32[]{:S(2)}) collective-permute-start(f32[8,128]{1,0:T(8,128)S(1)} %get-tuple-element.49.rest_0_), channel_id=1, source_target_pairs={{0,4},{4,0},{8,12},{12,8},{1,5},{5,1},{9,13},{13,9},{2,6},{6,2},{1... | collective-permute-start | bytes 12296 | tf_op jit(solution)/shard_map/ppermute | solution.py:344

commit v5 on v4

--- a/solution.py
+++ b/solution.py
@@ -77,8 +77,8 @@
         raw = interp_ref[j]
         high = jnp.right_shift(raw, interp_bits).astype(jnp.float32)
         low = jnp.bitwise_and(raw, (1 << interp_bits) - 1).astype(jnp.float32)
-        weight_ref[:, 2 * j * vox : (2 * j + 1) * vox] = high.astype(jnp.bfloat16)
-        weight_ref[:, (2 * j + 1) * vox : (2 * j + 2) * vox] = low.astype(jnp.bfloat16)
+        weight_ref[j * SEG : (j + 1) * SEG, :vox] = high.astype(jnp.bfloat16)
+        weight_ref[j * SEG : (j + 1) * SEG, vox:] = low.astype(jnp.bfloat16)
         covers.append(jnp.sum(raw.astype(jnp.float32), axis=0, keepdims=True) * interp_scale)
     cover_ref[...] = jnp.concatenate(covers, axis=0)
     orient = hit_ref.shape[1]
@@ -258,6 +258,7 @@
     mass_high = mass_sum.astype(jnp.bfloat16).astype(jnp.float32)
     mass_low = mass_sum - mass_high
     lane = lax.broadcasted_iota(jnp.int32, (bricks, LANES), 1)
+    high = low = jnp.zeros((bricks, LANES), jnp.float32)
     for j in range(NSEG):
         at = slice(j * bricks, (j + 1) * bricks)
         re_at = slice(j * SEG, (j + 1) * SEG)
@@ -274,42 +275,33 @@
             odd = slice((PAIRS + t) * bricks, (PAIRS + t + 1) * bricks)
             sum_re = sum_re + cos_t * with_re[even] + sin_t * with_im[odd]
             sum_im = sum_im + cos_t * with_im[even] - sin_t * with_re[odd]
-        sums_ref[:, j, :SEG] = sum_re
-        sums_ref[:, j, SEG : 2 * SEG] = sum_im
-        sums_ref[:, j, 2 * SEG :] = jnp.where(
-            lane == 0, mass_high[at], jnp.where(lane == 1, mass_low[at], 0.0)
-        )
+        sums_ref[:, 0, re_at] = sum_re
+        sums_ref[:, 1, re_at] = sum_im
+        high = jnp.where(lane == j, mass_high[at], high)
+        low = jnp.where(lane == j, mass_low[at], low)
+    sums_ref[:, 0, K:] = high
+    sums_ref[:, 1, K:] = low
     out_ref[...] = sums_ref[...].astype(jnp.bfloat16)
 
 
 def final_kernel(arrived_ref, weight_ref, cover_ref, values_ref, mass_ref):
     vox = cover_ref.shape[1]
     total = jnp.sum(arrived_ref[...].astype(jnp.float32), axis=0)
-    re, im = total[:, :SEG], total[:, SEG : 2 * SEG]
-    seg_mass = total[:, 2 * SEG : 2 * SEG + 1] + total[:, 2 * SEG + 1 : 2 * SEG + 2]
+    rest = total[:, :K]
     parts = []
     for _ in range(3):
-        high = [x.astype(jnp.bfloat16).astype(jnp.float32) for x in (re, im)]
-        parts += high
-        re, im = re - high[0], im - high[1]
-    left = jnp.concatenate(parts, axis=0).astype(jnp.bfloat16)
-    row = lax.broadcasted_iota(jnp.int32, (left.shape[0], 2 * vox), 0) % NSEG
-    product = jnp.zeros((left.shape[0], 2 * vox), jnp.float32)
+        high = rest.astype(jnp.bfloat16).astype(jnp.float32)
+        parts.append(high)
+        rest = rest - high
+    left = jnp.concatenate(parts + [jnp.zeros_like(rest)], axis=0).astype(jnp.bfloat16)
+    product = jnp.dot(left, weight_ref[...], preferred_element_type=jnp.float32)
+    product = product[0:2] + product[2:4] + product[4:6]
+    values_ref[0] = (product[:, :vox] * float(1 << interp_bits) + product[:, vox:]) * interp_scale
+    seg_mass = total[0:1, K:] + total[1:2, K:]
+    weight = jnp.zeros((1, vox), jnp.float32)
     for j in range(NSEG):
-        full = jnp.dot(
-            left,
-            weight_ref[:, 2 * j * vox : 2 * (j + 1) * vox],
-            preferred_element_type=jnp.float32,
-        )
-        product = jnp.where(row == j, full, product)
-    step = 2 * NSEG
-    product = product[:step] + product[step : 2 * step] + product[2 * step :]
-    for p in range(2):
-        line = jnp.sum(product[p * NSEG : (p + 1) * NSEG], axis=0, keepdims=True)
-        values_ref[0, p : p + 1, :] = (
-            line[:, :vox] * float(1 << interp_bits) + line[:, vox:]
-        ) * interp_scale
-    mass_ref[0] = jnp.sum(seg_mass * cover_ref[...], axis=0, keepdims=True)
+        weight = weight + seg_mass[:, j : j + 1] * cover_ref[j : j + 1, :]
+    mass_ref[0] = weight
 
 
 def on_chip(*arrays):
@@ -353,7 +345,7 @@
     count = lax.axis_size("orient")
     if count != 4:
         return [array] + [shift(array, k) for k in range(1, count)]
-    return [array] + [swap(array, k) for k in (3, 2, 1)]
+    return [array] + [swap(array, k) for k in (1, 2, 3)]
 
 
 def after(state, images):
@@ -384,7 +376,7 @@
         functools.partial(setup_kernel, bricks),
         "setup",
         [
-            jax.ShapeDtypeStruct((SEG, 2 * NSEG * vox), bf16),
+            jax.ShapeDtypeStruct((K, 2 * vox), bf16),
             jax.ShapeDtypeStruct((NSEG, vox), f32),
             jax.ShapeDtypeStruct((NSEG * bricks, orient), bf16),
             jax.ShapeDtypeStruct((PAIRS, K), f32),
@@ -449,11 +441,11 @@
     outgoing = call(
         functools.partial(brick_kernel, orient_count),
         "bricks",
-        jax.ShapeDtypeStruct((bricks, NSEG, 2 * SEG + LANES), bf16),
+        jax.ShapeDtypeStruct((bricks, 2, K + LANES), bf16),
         on_chip(shares, based, cos_table, sin_table, *gathered),
         scratch=[
             pltpu.VMEM((NSEG, SHIFTS * bricks, count), bf16),
-            pltpu.VMEM((bricks, NSEG, 2 * SEG + LANES), f32),
+            pltpu.VMEM((bricks, 2, K + LANES), f32),
         ],
     )
     received = lax.all_to_all(

time: 47.5 us -> 47.9 us (level)
  waiting for transfers between devices: 10.4 us -> 11.8 us
  blocking collectives: 12.5 us -> 11.5 us
    ppermute x3, waiting for transfers between devices: 2.13 us -> 3.6 us  [swap(): lax.ppermute(array, 'orient', [(i, i ^ amount) for i in range(count)])]
    all_to_all x1, blocking collectives: 12.5 us -> 11.5 us  [per_device(): lax.all_to_all(outgoing, ('orient', 'img', 'brick'), split_axis=0, concat...]
where the time goes in v5:
time: 47.9 us; the launch traced here: 47.7 us
  Pallas kernels  13.1 us (27%)
  waiting for transfers between devices  11.8 us (25%)
  blocking collectives  11.5 us (24%)
  starting transfers between devices  10.5 us (22%)
  between operations  0.71 us (1%)
    pallas_call x8, Pallas kernels, call(): pl.pallas_call(kernel, in_specs=[in_spec] * len(inputs), out_specs=[spec]...  13.1 us
    all_to_all x1, blocking collectives, per_device(): lax.all_to_all(outgoing, ('orient', 'img', 'brick'), split_axis=0, concat...  11.5 us
    ppermute x3, starting transfers between devices, swap(): lax.ppermute(array, 'orient', [(i, i ^ amount) for i in range(count)])  4.42 us
    ppermute x1, starting transfers between devices, per_device(): first = lax.ppermute(images, 'orient', [(0, 2), (3, 1), (2, 3), (1, 0)])  4.12 us
    ppermute x3, waiting for transfers between devices, swap(): lax.ppermute(array, 'orient', [(i, i ^ amount) for i in range(count)])  3.6 us
    ppermute x1, waiting for transfers between devices, per_device(): relayed = lax.ppermute(first, 'orient', [(2, 3), (1, 0)])  3.39 us
    ppermute x1, waiting for transfers between devices, per_device(): second = lax.ppermute(again, 'orient', [(0, 1), (3, 2), (1, 3), (2, 0)])  2.49 us
    ppermute x1, waiting for transfers between devices, per_device(): first = lax.ppermute(images, 'orient', [(0, 2), (3, 1), (2, 3), (1, 0)])  2.34 us
  transfers between devices with their start and end apart: 7, of which 5 were waited for; matrix products, arithmetic and copies ran while one was open for 0% of the time, Pallas kernels for 19%

profile of v5, /device:TPU:0, one launch (start us, length us, event | category | flops | bytes accessed | tf_op | source)
XLA Modules:
  0.0 47.7 jit_solution(2204877372403074618)
XLA Ops:
  0.6 0.0 copy-start
  0.6 4.1 %collective-permute-start = (bf16[32,4096]{1,0:T(8,128)(2,1)}, bf16[32,4096]{1,0:T(8,128)(2,1)S(1)}, u32[]{:S(2)}, u32[]{:S(2)}) collective-permute-start(bf16[32,4096]{1,0:T(8,128)(2,1)} %images_hbm.1), channel_id=1, source_target_pairs={{0,8},{12,4},{8,12},{4,0},{1,9},{13,5},{9,13},{5,1},{2,10},{14,6},... | collective-permute-start | bytes 786440 | tf_op jit(solution)/shard_map/ppermute | solution.py:368
  4.8 0.0 copy-start.1
  4.8 2.1 %setup.1 = (bf16[2048,512]{1,0:T(8,128)(2,1)S(1)}, f32[8,256]{1,0:T(8,128)S(1)}, bf16[128,256]{1,0:T(8,128)(2,1)S(1)}, f32[8,2048]{1,0:T(8,128)S(1)}, f32[8,2048...) custom-call(s32[1,8,256,256]{3,2,1,0:T(8,128)} %interp_hbm.1, s32[64,128]{1,0:T(8,128)} %bitcast.3, ...), custom_call_target="tpu_custom_call" | custom-call | tf_op jit(solution)/shard_map/setup/pallas_call | solution.py:318
  6.9 0.0 copy-done
  6.9 2.5 %scores.4 = (bf16[16,128,256]{2,1,0:T(8,128)(2,1)S(1)}, bf16[128,4096]{1,0:T(8,128)(2,1)S(1)}, f32[8,128]{1,0:T(8,128)S(1)}, f32[8,256]{1,0:T(8,128)S(1)}) custom-call(bf16[32,4096]{1,0:T(8,128)(2,1)S(1)} %get-tuple-element.28.refs_0_, s32[2,512]{1,0:T(2,128)S(1)} %get-tuple-element.29.refs_1_.refs_2_, bf16[256,4096]{1,0:T(8,128)(2,1)S(1)} %copy-done, ...), custom_call_target="tpu_custom_call" | custom-call | tf_op jit(solution)/shard_map/scores/pallas_call | solution.py:318
  9.4 0.0 copy-done.1
  9.4 0.1 collective-permute-start.3
  9.4 2.3 %collective-permute-done.refs_0_ = bf16[32,4096]{1,0:T(8,128)(2,1)S(1)} collective-permute-done((bf16[32,4096]{1,0:T(8,128)(2,1)}, bf16[32,4096]{1,0:T(8,128)(2,1)S(1)}, u32[]{:S(2)}, u32[]{:S(2)}) %collective-permute-start) | collective-permute-done | bytes 262176 | tf_op jit(solution)/shard_map/ppermute | solution.py:368
  11.8 1.3 %collective-permute-start.1 = (bf16[32,4096]{1,0:T(8,128)(2,1)S(1)}, bf16[32,4096]{1,0:T(8,128)(2,1)S(1)}, u32[]{:S(2)}, u32[]{:S(2)}) collective-permute-start(bf16[32,4096]{1,0:T(8,128)(2,1)S(1)} %collective-permute-done.refs_0_), channel_id=1, source_target_pairs={{8,12},{4,0},{9,13},{5,1},{10,14},{6,2},{11,15},{7,3},{24,28},{20,... | collective-permute-start | bytes 786440 | tf_op jit(solution)/shard_map/ppermute | solution.py:425
  13.1 0.7 %collective-permute-start.2 = (bf16[32,4096]{1,0:T(8,128)(2,1)S(1)}, bf16[32,4096]{1,0:T(8,128)(2,1)S(1)}, u32[]{:S(2)}, u32[]{:S(2)}) collective-permute-start(bf16[32,4096]{1,0:T(8,128)(2,1)S(1)} %copy-done.1), channel_id=1, source_target_pairs={{4,8},{8,4},{5,9},{9,5},{6,10},{10,6},{7,11},{11,7},{20,24},{24,20... | collective-permute-start | bytes 786440 | tf_op jit(solution)/shard_map/ppermute | solution.py:426
  13.7 2.0 %scores.5 = (bf16[16,128,256]{2,1,0:T(8,128)(2,1)S(1)}, bf16[128,4096]{1,0:T(8,128)(2,1)S(1)}, f32[8,128]{1,0:T(8,128)S(1)}) custom-call(bf16[32,4096]{1,0:T(8,128)(2,1)S(1)} %collective-permute-done.refs_0_, s32[2,512]{1,0:T(2,128)S(1)} %get-tuple-element.29.refs_1_.refs_2_, ...), custom_call_target="tpu_custom_call", output_to_operand_aliasing={{0}: (6, {}), {1}: (7, {}), {2}: (8, {})} | custom-call | tf_op jit(solution)/shard_map/scores/pallas_call | solution.py:318
  15.8 2.5 %collective-permute-done.3.refs_0_ = bf16[32,4096]{1,0:T(8,128)(2,1)S(1)} collective-permute-done((bf16[32,4096]{1,0:T(8,128)(2,1)S(1)}, bf16[32,4096]{1,0:T(8,128)(2,1)S(1)}, u32[]{:S(2)}, u32[]{:S(2)}) %collective-permute-start.3) | collective-permute-done | bytes 262176 | tf_op jit(solution)/shard_map/ppermute | solution.py:423
  18.3 2.0 %scores.6 = (bf16[16,128,256]{2,1,0:T(8,128)(2,1)S(1)}, bf16[128,4096]{1,0:T(8,128)(2,1)S(1)}, f32[8,128]{1,0:T(8,128)S(1)}) custom-call(bf16[32,4096]{1,0:T(8,128)(2,1)S(1)} %collective-permute-done.3.refs_0_, s32[2,512]{1,0:T(2,128)S(1)} %get-tuple-element.29.refs_1_.refs_2_, ...), custom_call_target="tpu_custom_call", output_to_operand_aliasing={{0}: (6, {}), {1}: (7, {}), {2}: (8, {})} | custom-call | tf_op jit(solution)/shard_map/scores/pallas_call | solution.py:318
  20.3 3.4 %collective-permute-done.1.refs_0_ = bf16[32,4096]{1,0:T(8,128)(2,1)S(1)} collective-permute-done((bf16[32,4096]{1,0:T(8,128)(2,1)S(1)}, bf16[32,4096]{1,0:T(8,128)(2,1)S(1)}, u32[]{:S(2)}, u32[]{:S(2)}) %collective-permute-start.1) | collective-permute-done | bytes 262176 | tf_op jit(solution)/shard_map/ppermute | solution.py:425
  23.7 0.0 collective-permute-done.2.refs_1_
  23.7 2.1 %scores.7 = (bf16[16,128,256]{2,1,0:T(8,128)(2,1)S(1)}, bf16[128,4096]{1,0:T(8,128)(2,1)S(1)}, f32[8,128]{1,0:T(8,128)S(1)}) custom-call(bf16[32,4096]{1,0:T(8,128)(2,1)S(1)} %collective-permute-done.1.refs_0_, bf16[32,4096]{1,0:T(8,128)(2,1)S(1)} %collective-permute-done.2.refs_1_, ...), custom_call_target="tpu_custom_call", output_to_operand_aliasing={{0}: (7, {}), {1}: (8, {}), {2}: (9, {})} | custom-call | tf_op jit(solution)/shard_map/scores/pallas_call | solution.py:318
  25.8 0.6 %collective-permute-start.4 = (f32[8,128]{1,0:T(8,128)S(1)}, f32[8,128]{1,0:T(8,128)S(1)}, u32[]{:S(2)}, u32[]{:S(2)}) collective-permute-start(f32[8,128]{1,0:T(8,128)S(1)} %get-tuple-element.49.rest_0_), channel_id=1, source_target_pairs={{0,4},{4,0},{8,12},{12,8},{1,5},{5,1},{9,13},{13,9},{2,6},{6,2},{1... | collective-permute-start | bytes 12296 | tf_op jit(solution)/shard_map/ppermute | solution.py:336
  26.4 2.4 %collective-permute-start.5 = (f32[8,128]{1,0:T(8,128)S(1)}, f32[8,128]{1,0:T(8,128)S(1)}, u32[]{:S(2)}, u32[]{:S(2)}) collective-permute-start(f32[8,128]{1,0:T(8,128)S(1)} %get-tuple-element.49.rest_0_), channel_id=1, source_target_pairs={{0,8},{4,12},{8,0},{12,4},{1,9},{5,13},{9,1},{13,5},{2,10},{6,14},... | collective-permute-start | bytes 12296 | tf_op jit(solution)/shard_map/ppermute | solution.py:336
  28.8 1.4 %collective-permute-start.6 = (f32[8,128]{1,0:T(8,128)S(1)}, f32[8,128]{1,0:T(8,128)S(1)}, u32[]{:S(2)}, u32[]{:S(2)}) collective-permute-start(f32[8,128]{1,0:T(8,128)S(1)} %get-tuple-element.49.rest_0_), channel_id=1, source_target_pairs={{0,12},{4,8},{8,4},{12,0},{1,13},{5,9},{9,5},{13,1},{2,14},{6,10},... | collective-permute-start | bytes 12296 | tf_op jit(solution)/shard_map/ppermute | solution.py:336
  30.2 0.4 shares.1.share_ref
  30.6 0.0 collective-permute-done.4.rest_1_
  30.6 0.3 collective-permute-done.5.rest_2_
  30.9 3.3 %collective-permute-done.6.rest_3_ = f32[8,128]{1,0:T(8,128)S(1)} collective-permute-done((f32[8,128]{1,0:T(8,128)S(1)}, f32[8,128]{1,0:T(8,128)S(1)}, u32[]{:S(2)}, u32[]{:S(2)}) %collective-permute-start.6) | collective-permute-done | bytes 4128 | tf_op jit(solution)/shard_map/ppermute | solution.py:336
  34.2 0.9 %bricks.1 = bf16[16,2,2176]{2,1,0:T(2,128)(2,1)S(1)} custom-call(f32[16,128,128]{2,1,0:T(8,128)S(1)} %shares.1.share_ref, bf16[128,4096]{1,0:T(8,128)(2,1)S(1)} %get-tuple-element.48.based_ref, f32[8,2048]{1,0:T(8,128)S(1)} %get-tuple-element.30.refs_3_.refs_4_.cos_ref, f32[8,2048]{1,0:T(8,128)S(1)} %get-tuple-element.31.refs_4_.refs_5_.sin_ref, ...), custom_call_target="tpu_custom_call" | custom-call | tf_op jit(solution)/shard_map/bricks/pallas_call | solution.py:318
  35.2 11.5 %all_to_all.5.arrived_ref = bf16[16,2,2176]{2,1,0:T(2,128)(2,1)S(1)} all-to-all(bf16[16,2,2176]{2,1,0:T(2,128)(2,1)S(1)} %bricks.1), channel_id=1, replica_groups=mesh['groups'=2,'orient'=4,'img'=2,'brick'=2] {'orient','img','brick'}, dimensions={0} | all-to-all | bytes 278528 | tf_op jit(solution)/shard_map/all_to_all | solution.py:451
  46.7 1.0 %insert.1 = (f32[1,2,256]{2,1,0:T(2,128)}, f32[1,1,256]{2,1,0:T(1,128)}) custom-call(bf16[16,2,2176]{2,1,0:T(2,128)(2,1)S(1)} %all_to_all.5.arrived_ref, bf16[2048,512]{1,0:T(8,128)(2,1)S(1)} %get-tuple-element.50.weight_ref, f32[8,256]{1,0:T(8,128)S(1)} %get-tuple-element.51.cover_ref), custom_call_target="tpu_custom_call" | custom-call | tf_op jit(solution)/shard_map/insert/pallas_call | solution.py:318
Async XLA Ops:
  0.6 6.3 %copy-start = (bf16[256,4096]{1,0:T(8,128)(2,1)S(1)}, bf16[256,4096]{1,0:T(8,128)(2,1)}, u32[]{:S(2)}) copy-start(bf16[256,4096]{1,0:T(8,128)(2,1)} %refs_3_.1) | copy-start | bytes 6291460
  0.6 11.1 %collective-permute-start = (bf16[32,4096]{1,0:T(8,128)(2,1)}, bf16[32,4096]{1,0:T(8,128)(2,1)S(1)}, u32[]{:S(2)}, u32[]{:S(2)}) collective-permute-start(bf16[32,4096]{1,0:T(8,128)(2,1)} %images_hbm.1), channel_id=1, source_target_pairs={{0,8},{12,4},{8,12},{4,0},{1,9},{13,5},{9,13},{5,1},{2,10},{14,6},... | collective-permute-start | bytes 786440 | tf_op jit(solution)/shard_map/ppermute | solution.py:368
  4.8 4.6 %copy-start.1 = (bf16[32,4096]{1,0:T(8,128)(2,1)S(1)}, bf16[32,4096]{1,0:T(8,128)(2,1)}, u32[]{:S(2)}) copy-start(bf16[32,4096]{1,0:T(8,128)(2,1)} %images_hbm.1) | copy-start | bytes 786436
  9.4 8.9 %collective-permute-start.3 = (bf16[32,4096]{1,0:T(8,128)(2,1)S(1)}, bf16[32,4096]{1,0:T(8,128)(2,1)S(1)}, u32[]{:S(2)}, u32[]{:S(2)}) collective-permute-start(bf16[32,4096]{1,0:T(8,128)(2,1)S(1)} %copy-done.1), channel_id=1, source_target_pairs={{0,4},{12,8},{4,12},{8,0},{1,5},{13,9},{5,13},{9,1},{2,6},{14,10},... | collective-permute-start | bytes 786440 | tf_op jit(solution)/shard_map/ppermute | solution.py:423
  11.8 11.9 %collective-permute-start.1 = (bf16[32,4096]{1,0:T(8,128)(2,1)S(1)}, bf16[32,4096]{1,0:T(8,128)(2,1)S(1)}, u32[]{:S(2)}, u32[]{:S(2)}) collective-permute-start(bf16[32,4096]{1,0:T(8,128)(2,1)S(1)} %collective-permute-done.refs_0_), channel_id=1, source_target_pairs={{8,12},{4,0},{9,13},{5,1},{10,14},{6,2},{11,15},{7,3},{24,28},{20,... | collective-permute-start | bytes 786440 | tf_op jit(solution)/shard_map/ppermute | solution.py:425
  13.1 10.6 %collective-permute-start.2 = (bf16[32,4096]{1,0:T(8,128)(2,1)S(1)}, bf16[32,4096]{1,0:T(8,128)(2,1)S(1)}, u32[]{:S(2)}, u32[]{:S(2)}) collective-permute-start(bf16[32,4096]{1,0:T(8,128)(2,1)S(1)} %copy-done.1), channel_id=1, source_target_pairs={{4,8},{8,4},{5,9},{9,5},{6,10},{10,6},{7,11},{11,7},{20,24},{24,20... | collective-permute-start | bytes 786440 | tf_op jit(solution)/shard_map/ppermute | solution.py:426
  25.8 4.9 %collective-permute-start.4 = (f32[8,128]{1,0:T(8,128)S(1)}, f32[8,128]{1,0:T(8,128)S(1)}, u32[]{:S(2)}, u32[]{:S(2)}) collective-permute-start(f32[8,128]{1,0:T(8,128)S(1)} %get-tuple-element.49.rest_0_), channel_id=1, source_target_pairs={{0,4},{4,0},{8,12},{12,8},{1,5},{5,1},{9,13},{13,9},{2,6},{6,2},{1... | collective-permute-start | bytes 12296 | tf_op jit(solution)/shard_map/ppermute | solution.py:336
  26.4 4.5 %collective-permute-start.5 = (f32[8,128]{1,0:T(8,128)S(1)}, f32[8,128]{1,0:T(8,128)S(1)}, u32[]{:S(2)}, u32[]{:S(2)}) collective-permute-start(f32[8,128]{1,0:T(8,128)S(1)} %get-tuple-element.49.rest_0_), channel_id=1, source_target_pairs={{0,8},{4,12},{8,0},{12,4},{1,9},{5,13},{9,1},{13,5},{2,10},{6,14},... | collective-permute-start | bytes 12296 | tf_op jit(solution)/shard_map/ppermute | solution.py:336
  28.8 5.4 %collective-permute-start.6 = (f32[8,128]{1,0:T(8,128)S(1)}, f32[8,128]{1,0:T(8,128)S(1)}, u32[]{:S(2)}, u32[]{:S(2)}) collective-permute-start(f32[8,128]{1,0:T(8,128)S(1)} %get-tuple-element.49.rest_0_), channel_id=1, source_target_pairs={{0,12},{4,8},{8,4},{12,0},{1,13},{5,9},{9,5},{13,1},{2,14},{6,10},... | collective-permute-start | bytes 12296 | tf_op jit(solution)/shard_map/ppermute | solution.py:336

commit v6 on v5

--- a/solution.py
+++ b/solution.py
@@ -345,7 +345,7 @@
     count = lax.axis_size("orient")
     if count != 4:
         return [array] + [shift(array, k) for k in range(1, count)]
-    return [array] + [swap(array, k) for k in (1, 2, 3)]
+    return [array] + [swap(array, k) for k in (3, 2, 1)]
 
 
 def after(state, images):

time: 47.9 us -> 47.1 us (0.983)
  waiting for transfers between devices: 11.8 us -> 10.4 us
  blocking collectives: 11.5 us -> 12.2 us
    ppermute x3, waiting for transfers between devices: 3.6 us -> 2.15 us  [swap(): lax.ppermute(array, 'orient', [(i, i ^ amount) for i in range(count)])]
    all_to_all x1, blocking collectives: 11.5 us -> 12.2 us  [per_device(): lax.all_to_all(outgoing, ('orient', 'img', 'brick'), split_axis=0, concat...]
where the time goes in v6:
time: 47.1 us; the launch traced here: 46.9 us
  Pallas kernels  13.1 us (28%)
  blocking collectives  12.2 us (26%)
  starting transfers between devices  10.5 us (22%)
  waiting for transfers between devices  10.4 us (22%)
  between operations  0.7 us (1%)
    pallas_call x8, Pallas kernels, call(): pl.pallas_call(kernel, in_specs=[in_spec] * len(inputs), out_specs=[spec]...  13.1 us
    all_to_all x1, blocking collectives, per_device(): lax.all_to_all(outgoing, ('orient', 'img', 'brick'), split_axis=0, concat...  12.2 us
    ppermute x3, starting transfers between devices, swap(): lax.ppermute(array, 'orient', [(i, i ^ amount) for i in range(count)])  4.42 us
    ppermute x1, starting transfers between devices, per_device(): first = lax.ppermute(images, 'orient', [(0, 2), (3, 1), (2, 3), (1, 0)])  4.12 us
    ppermute x1, waiting for transfers between devices, per_device(): relayed = lax.ppermute(first, 'orient', [(2, 3), (1, 0)])  3.39 us
    ppermute x1, waiting for transfers between devices, per_device(): second = lax.ppermute(again, 'orient', [(0, 1), (3, 2), (1, 3), (2, 0)])  2.49 us
    ppermute x1, waiting for transfers between devices, per_device(): first = lax.ppermute(images, 'orient', [(0, 2), (3, 1), (2, 3), (1, 0)])  2.34 us
    ppermute x3, waiting for transfers between devices, swap(): lax.ppermute(array, 'orient', [(i, i ^ amount) for i in range(count)])  2.15 us
  transfers between devices with their start and end apart: 7, of which 5 were waited for; matrix products, arithmetic and copies ran while one was open for 0% of the time, Pallas kernels for 19%

profile of v6, /device:TPU:0, one launch (start us, length us, event | category | flops | bytes accessed | tf_op | source)
XLA Modules:
  0.0 46.9 jit_solution(13133192081820033462)
XLA Ops:
  0.6 0.0 copy-start
  0.6 4.1 %collective-permute-start = (bf16[32,4096]{1,0:T(8,128)(2,1)}, bf16[32,4096]{1,0:T(8,128)(2,1)S(1)}, u32[]{:S(2)}, u32[]{:S(2)}) collective-permute-start(bf16[32,4096]{1,0:T(8,128)(2,1)} %images_hbm.1), channel_id=1, source_target_pairs={{0,8},{12,4},{8,12},{4,0},{1,9},{13,5},{9,13},{5,1},{2,10},{14,6},... | collective-permute-start | bytes 786440 | tf_op jit(solution)/shard_map/ppermute | solution.py:368
  4.8 0.0 copy-start.1
  4.8 2.1 %setup.1 = (bf16[2048,512]{1,0:T(8,128)(2,1)S(1)}, f32[8,256]{1,0:T(8,128)S(1)}, bf16[128,256]{1,0:T(8,128)(2,1)S(1)}, f32[8,2048]{1,0:T(8,128)S(1)}, f32[8,2048...) custom-call(s32[1,8,256,256]{3,2,1,0:T(8,128)} %interp_hbm.1, s32[64,128]{1,0:T(8,128)} %bitcast.3, ...), custom_call_target="tpu_custom_call" | custom-call | tf_op jit(solution)/shard_map/setup/pallas_call | solution.py:318
  6.9 0.0 copy-done
  6.9 2.5 %scores.4 = (bf16[16,128,256]{2,1,0:T(8,128)(2,1)S(1)}, bf16[128,4096]{1,0:T(8,128)(2,1)S(1)}, f32[8,128]{1,0:T(8,128)S(1)}, f32[8,256]{1,0:T(8,128)S(1)}) custom-call(bf16[32,4096]{1,0:T(8,128)(2,1)S(1)} %get-tuple-element.28.refs_0_, s32[2,512]{1,0:T(2,128)S(1)} %get-tuple-element.29.refs_1_.refs_2_, bf16[256,4096]{1,0:T(8,128)(2,1)S(1)} %copy-done, ...), custom_call_target="tpu_custom_call" | custom-call | tf_op jit(solution)/shard_map/scores/pallas_call | solution.py:318
  9.4 0.0 copy-done.1
  9.4 0.1 collective-permute-start.3
  9.4 2.3 %collective-permute-done.refs_0_ = bf16[32,4096]{1,0:T(8,128)(2,1)S(1)} collective-permute-done((bf16[32,4096]{1,0:T(8,128)(2,1)}, bf16[32,4096]{1,0:T(8,128)(2,1)S(1)}, u32[]{:S(2)}, u32[]{:S(2)}) %collective-permute-start) | collective-permute-done | bytes 262176 | tf_op jit(solution)/shard_map/ppermute | solution.py:368
  11.8 1.3 %collective-permute-start.1 = (bf16[32,4096]{1,0:T(8,128)(2,1)S(1)}, bf16[32,4096]{1,0:T(8,128)(2,1)S(1)}, u32[]{:S(2)}, u32[]{:S(2)}) collective-permute-start(bf16[32,4096]{1,0:T(8,128)(2,1)S(1)} %collective-permute-done.refs_0_), channel_id=1, source_target_pairs={{8,12},{4,0},{9,13},{5,1},{10,14},{6,2},{11,15},{7,3},{24,28},{20,... | collective-permute-start | bytes 786440 | tf_op jit(solution)/shard_map/ppermute | solution.py:425
  13.1 0.7 %collective-permute-start.2 = (bf16[32,4096]{1,0:T(8,128)(2,1)S(1)}, bf16[32,4096]{1,0:T(8,128)(2,1)S(1)}, u32[]{:S(2)}, u32[]{:S(2)}) collective-permute-start(bf16[32,4096]{1,0:T(8,128)(2,1)S(1)} %copy-done.1), channel_id=1, source_target_pairs={{4,8},{8,4},{5,9},{9,5},{6,10},{10,6},{7,11},{11,7},{20,24},{24,20... | collective-permute-start | bytes 786440 | tf_op jit(solution)/shard_map/ppermute | solution.py:426
  13.7 2.0 %scores.5 = (bf16[16,128,256]{2,1,0:T(8,128)(2,1)S(1)}, bf16[128,4096]{1,0:T(8,128)(2,1)S(1)}, f32[8,128]{1,0:T(8,128)S(1)}) custom-call(bf16[32,4096]{1,0:T(8,128)(2,1)S(1)} %collective-permute-done.refs_0_, s32[2,512]{1,0:T(2,128)S(1)} %get-tuple-element.29.refs_1_.refs_2_, ...), custom_call_target="tpu_custom_call", output_to_operand_aliasing={{0}: (6, {}), {1}: (7, {}), {2}: (8, {})} | custom-call | tf_op jit(solution)/shard_map/scores/pallas_call | solution.py:318
  15.8 2.5 %collective-permute-done.3.refs_0_ = bf16[32,4096]{1,0:T(8,128)(2,1)S(1)} collective-permute-done((bf16[32,4096]{1,0:T(8,128)(2,1)S(1)}, bf16[32,4096]{1,0:T(8,128)(2,1)S(1)}, u32[]{:S(2)}, u32[]{:S(2)}) %collective-permute-start.3) | collective-permute-done | bytes 262176 | tf_op jit(solution)/shard_map/ppermute | solution.py:423
  18.3 2.0 %scores.6 = (bf16[16,128,256]{2,1,0:T(8,128)(2,1)S(1)}, bf16[128,4096]{1,0:T(8,128)(2,1)S(1)}, f32[8,128]{1,0:T(8,128)S(1)}) custom-call(bf16[32,4096]{1,0:T(8,128)(2,1)S(1)} %collective-permute-done.3.refs_0_, s32[2,512]{1,0:T(2,128)S(1)} %get-tuple-element.29.refs_1_.refs_2_, ...), custom_call_target="tpu_custom_call", output_to_operand_aliasing={{0}: (6, {}), {1}: (7, {}), {2}: (8, {})} | custom-call | tf_op jit(solution)/shard_map/scores/pallas_call | solution.py:318
  20.3 3.4 %collective-permute-done.1.refs_0_ = bf16[32,4096]{1,0:T(8,128)(2,1)S(1)} collective-permute-done((bf16[32,4096]{1,0:T(8,128)(2,1)S(1)}, bf16[32,4096]{1,0:T(8,128)(2,1)S(1)}, u32[]{:S(2)}, u32[]{:S(2)}) %collective-permute-start.1) | collective-permute-done | bytes 262176 | tf_op jit(solution)/shard_map/ppermute | solution.py:425
  23.7 0.0 collective-permute-done.2.refs_1_
  23.7 2.1 %scores.7 = (bf16[16,128,256]{2,1,0:T(8,128)(2,1)S(1)}, bf16[128,4096]{1,0:T(8,128)(2,1)S(1)}, f32[8,128]{1,0:T(8,128)S(1)}) custom-call(bf16[32,4096]{1,0:T(8,128)(2,1)S(1)} %collective-permute-done.1.refs_0_, bf16[32,4096]{1,0:T(8,128)(2,1)S(1)} %collective-permute-done.2.refs_1_, ...), custom_call_target="tpu_custom_call", output_to_operand_aliasing={{0}: (7, {}), {1}: (8, {}), {2}: (9, {})} | custom-call | tf_op jit(solution)/shard_map/scores/pallas_call | solution.py:318
  25.8 2.5 %collective-permute-start.4 = (f32[8,128]{1,0:T(8,128)S(1)}, f32[8,128]{1,0:T(8,128)S(1)}, u32[]{:S(2)}, u32[]{:S(2)}) collective-permute-start(f32[8,128]{1,0:T(8,128)S(1)} %get-tuple-element.49.rest_0_), channel_id=1, source_target_pairs={{0,12},{4,8},{8,4},{12,0},{1,13},{5,9},{9,5},{13,1},{2,14},{6,10},... | collective-permute-start | bytes 12296 | tf_op jit(solution)/shard_map/ppermute | solution.py:336
  28.3 0.0 collective-permute-start.5
  28.3 1.9 %collective-permute-start.6 = (f32[8,128]{1,0:T(8,128)S(1)}, f32[8,128]{1,0:T(8,128)S(1)}, u32[]{:S(2)}, u32[]{:S(2)}) collective-permute-start(f32[8,128]{1,0:T(8,128)S(1)} %get-tuple-element.49.rest_0_), channel_id=1, source_target_pairs={{0,4},{4,0},{8,12},{12,8},{1,5},{5,1},{9,13},{13,9},{2,6},{6,2},{1... | collective-permute-start | bytes 12296 | tf_op jit(solution)/shard_map/ppermute | solution.py:336
  30.2 0.4 shares.1.share_ref
  30.6 0.6 %collective-permute-done.4.rest_1_ = f32[8,128]{1,0:T(8,128)S(1)} collective-permute-done((f32[8,128]{1,0:T(8,128)S(1)}, f32[8,128]{1,0:T(8,128)S(1)}, u32[]{:S(2)}, u32[]{:S(2)}) %collective-permute-start.4) | collective-permute-done | bytes 4128 | tf_op jit(solution)/shard_map/ppermute | solution.py:336
  31.2 1.6 %collective-permute-done.5.rest_2_ = f32[8,128]{1,0:T(8,128)S(1)} collective-permute-done((f32[8,128]{1,0:T(8,128)S(1)}, f32[8,128]{1,0:T(8,128)S(1)}, u32[]{:S(2)}, u32[]{:S(2)}) %collective-permute-start.5) | collective-permute-done | bytes 4128 | tf_op jit(solution)/shard_map/ppermute | solution.py:336
  32.8 0.0 collective-permute-done.6.rest_3_
  32.8 0.9 %bricks.1 = bf16[16,2,2176]{2,1,0:T(2,128)(2,1)S(1)} custom-call(f32[16,128,128]{2,1,0:T(8,128)S(1)} %shares.1.share_ref, bf16[128,4096]{1,0:T(8,128)(2,1)S(1)} %get-tuple-element.48.based_ref, f32[8,2048]{1,0:T(8,128)S(1)} %get-tuple-element.30.refs_3_.refs_4_.cos_ref, f32[8,2048]{1,0:T(8,128)S(1)} %get-tuple-element.31.refs_4_.refs_5_.sin_ref, ...), custom_call_target="tpu_custom_call" | custom-call | tf_op jit(solution)/shard_map/bricks/pallas_call | solution.py:318
  33.7 12.2 %all_to_all.5.arrived_ref = bf16[16,2,2176]{2,1,0:T(2,128)(2,1)S(1)} all-to-all(bf16[16,2,2176]{2,1,0:T(2,128)(2,1)S(1)} %bricks.1), channel_id=1, replica_groups=mesh['groups'=2,'orient'=4,'img'=2,'brick'=2] {'orient','img','brick'}, dimensions={0} | all-to-all | bytes 278528 | tf_op jit(solution)/shard_map/all_to_all | solution.py:451
  45.9 1.0 %insert.1 = (f32[1,2,256]{2,1,0:T(2,128)}, f32[1,1,256]{2,1,0:T(1,128)}) custom-call(bf16[16,2,2176]{2,1,0:T(2,128)(2,1)S(1)} %all_to_all.5.arrived_ref, bf16[2048,512]{1,0:T(8,128)(2,1)S(1)} %get-tuple-element.50.weight_ref, f32[8,256]{1,0:T(8,128)S(1)} %get-tuple-element.51.cover_ref), custom_call_target="tpu_custom_call" | custom-call | tf_op jit(solution)/shard_map/insert/pallas_call | solution.py:318
Async XLA Ops:
  0.6 6.3 %copy-start = (bf16[256,4096]{1,0:T(8,128)(2,1)S(1)}, bf16[256,4096]{1,0:T(8,128)(2,1)}, u32[]{:S(2)}) copy-start(bf16[256,4096]{1,0:T(8,128)(2,1)} %refs_3_.1) | copy-start | bytes 6291460
  0.6 11.1 %collective-permute-start = (bf16[32,4096]{1,0:T(8,128)(2,1)}, bf16[32,4096]{1,0:T(8,128)(2,1)S(1)}, u32[]{:S(2)}, u32[]{:S(2)}) collective-permute-start(bf16[32,4096]{1,0:T(8,128)(2,1)} %images_hbm.1), channel_id=1, source_target_pairs={{0,8},{12,4},{8,12},{4,0},{1,9},{13,5},{9,13},{5,1},{2,10},{14,6},... | collective-permute-start | bytes 786440 | tf_op jit(solution)/shard_map/ppermute | solution.py:368
  4.8 4.6 %copy-start.1 = (bf16[32,4096]{1,0:T(8,128)(2,1)S(1)}, bf16[32,4096]{1,0:T(8,128)(2,1)}, u32[]{:S(2)}) copy-start(bf16[32,4096]{1,0:T(8,128)(2,1)} %images_hbm.1) | copy-start | bytes 786436
  9.4 8.9 %collective-permute-start.3 = (bf16[32,4096]{1,0:T(8,128)(2,1)S(1)}, bf16[32,4096]{1,0:T(8,128)(2,1)S(1)}, u32[]{:S(2)}, u32[]{:S(2)}) collective-permute-start(bf16[32,4096]{1,0:T(8,128)(2,1)S(1)} %copy-done.1), channel_id=1, source_target_pairs={{0,4},{12,8},{4,12},{8,0},{1,5},{13,9},{5,13},{9,1},{2,6},{14,10},... | collective-permute-start | bytes 786440 | tf_op jit(solution)/shard_map/ppermute | solution.py:423
  11.8 11.9 %collective-permute-start.1 = (bf16[32,4096]{1,0:T(8,128)(2,1)S(1)}, bf16[32,4096]{1,0:T(8,128)(2,1)S(1)}, u32[]{:S(2)}, u32[]{:S(2)}) collective-permute-start(bf16[32,4096]{1,0:T(8,128)(2,1)S(1)} %collective-permute-done.refs_0_), channel_id=1, source_target_pairs={{8,12},{4,0},{9,13},{5,1},{10,14},{6,2},{11,15},{7,3},{24,28},{20,... | collective-permute-start | bytes 786440 | tf_op jit(solution)/shard_map/ppermute | solution.py:425
  13.1 10.6 %collective-permute-start.2 = (bf16[32,4096]{1,0:T(8,128)(2,1)S(1)}, bf16[32,4096]{1,0:T(8,128)(2,1)S(1)}, u32[]{:S(2)}, u32[]{:S(2)}) collective-permute-start(bf16[32,4096]{1,0:T(8,128)(2,1)S(1)} %copy-done.1), channel_id=1, source_target_pairs={{4,8},{8,4},{5,9},{9,5},{6,10},{10,6},{7,11},{11,7},{20,24},{24,20... | collective-permute-start | bytes 786440 | tf_op jit(solution)/shard_map/ppermute | solution.py:426
  25.8 5.4 %collective-permute-start.4 = (f32[8,128]{1,0:T(8,128)S(1)}, f32[8,128]{1,0:T(8,128)S(1)}, u32[]{:S(2)}, u32[]{:S(2)}) collective-permute-start(f32[8,128]{1,0:T(8,128)S(1)} %get-tuple-element.49.rest_0_), channel_id=1, source_target_pairs={{0,12},{4,8},{8,4},{12,0},{1,13},{5,9},{9,5},{13,1},{2,14},{6,10},... | collective-permute-start | bytes 12296 | tf_op jit(solution)/shard_map/ppermute | solution.py:336
  28.3 4.5 %collective-permute-start.5 = (f32[8,128]{1,0:T(8,128)S(1)}, f32[8,128]{1,0:T(8,128)S(1)}, u32[]{:S(2)}, u32[]{:S(2)}) collective-permute-start(f32[8,128]{1,0:T(8,128)S(1)} %get-tuple-element.49.rest_0_), channel_id=1, source_target_pairs={{0,8},{4,12},{8,0},{12,4},{1,9},{5,13},{9,1},{13,5},{2,10},{6,14},... | collective-permute-start | bytes 12296 | tf_op jit(solution)/shard_map/ppermute | solution.py:336
  28.3 4.5 %collective-permute-start.6 = (f32[8,128]{1,0:T(8,128)S(1)}, f32[8,128]{1,0:T(8,128)S(1)}, u32[]{:S(2)}, u32[]{:S(2)}) collective-permute-start(f32[8,128]{1,0:T(8,128)S(1)} %get-tuple-element.49.rest_0_), channel_id=1, source_target_pairs={{0,4},{4,0},{8,12},{12,8},{1,5},{5,1},{9,13},{13,9},{2,6},{6,2},{1... | collective-permute-start | bytes 12296 | tf_op jit(solution)/shard_map/ppermute | solution.py:336

commit v7 on v6

--- a/solution.py
+++ b/solution.py
@@ -7,6 +7,7 @@
 from jax.experimental import pallas as pl
 from jax.experimental.pallas import tpu as pltpu
 from jax.sharding import PartitionSpec as P
+
 
 SHIFTS = 16
 SEG = 256
@@ -32,34 +33,32 @@
     return c, s * x
 
 
-def setup_kernel(
-    bricks,
-    interp_hbm,
-    map_hbm,
+def phase_kernel(
     images_hbm,
     offsets_hbm,
-    weight_ref,
-    cover_ref,
-    hit_ref,
+    slices_hbm,
     cos_ref,
     sin_ref,
     images_ref,
+    phase_cos_ref,
+    phase_sin_ref,
+    norm_ref,
+    slices_ref,
     offsets_ref,
-    interp_ref,
-    map_ref,
     sems,
 ):
-    small = [
-        pltpu.make_async_copy(source, target, sems.at[NSEG + i])
-        for i, (source, target) in enumerate(
-            [(images_hbm, images_ref), (offsets_hbm, offsets_ref), (map_hbm, map_ref)]
+    tiles, orient = slices_ref.shape[:2]
+    copies = [
+        pltpu.make_async_copy(offsets_hbm, offsets_ref, sems.at[tiles]),
+        pltpu.make_async_copy(images_hbm, images_ref, sems.at[tiles + 1]),
+    ]
+    packed = [
+        pltpu.make_async_copy(
+            slices_hbm.at[:, k * LANES : (k + 1) * LANES], slices_ref.at[k], sems.at[k]
         )
+        for k in range(tiles)
     ]
-    large = [
-        pltpu.make_async_copy(interp_hbm.at[0, j], interp_ref.at[j], sems.at[j])
-        for j in range(NSEG)
-    ]
-    for copy in small + large:
+    for copy in copies + packed:
         copy.start()
     coef = lax.broadcasted_iota(jnp.int32, (PAIRS, K), 1)
     pair = lax.broadcasted_iota(jnp.int32, (PAIRS, K), 0)
@@ -68,8 +67,34 @@
     dx = 2 * jnp.bitwise_and(pair, 3) - 3
     dy = 2 * (pair // 4) - 3
     cos_ref[...], sin_ref[...] = cos_sin(u * dx + w * dy)
-    for copy in small:
+    for copy in copies:
         copy.wait()
+    base_phases(images_ref.shape[0], offsets_ref, phase_cos_ref, phase_sin_ref)
+    total = jnp.zeros((orient, LANES), jnp.float32)
+    for k in range(tiles):
+        packed[k].wait()
+        piece = slices_ref[k].astype(jnp.float32)
+        total = total + piece * piece
+    norm_ref[...] = 0.5 * lax.dot_general(
+        jnp.ones((8, LANES), jnp.float32),
+        total,
+        (((1,), (1,)), ((), ())),
+        precision=lax.Precision.HIGHEST,
+        preferred_element_type=jnp.float32,
+    )
+
+
+def weight_kernel(
+    bricks, interp_hbm, map_hbm, weight_ref, cover_ref, hit_ref, interp_ref, map_ref, sems
+):
+    small = pltpu.make_async_copy(map_hbm, map_ref, sems.at[NSEG])
+    large = [
+        pltpu.make_async_copy(interp_hbm.at[0, j], interp_ref.at[j], sems.at[j])
+        for j in range(NSEG)
+    ]
+    for copy in [small] + large:
+        copy.start()
+    small.wait()
     vox = interp_ref.shape[2]
     covers = []
     for j in range(NSEG):
@@ -109,6 +134,34 @@
     hit_ref[...] = jnp.concatenate(hits, axis=0).astype(jnp.bfloat16)
 
 
+def base_phases(rows, offsets_ref, phase_cos_ref, phase_sin_ref):
+    group = lax.axis_index("img") * lax.axis_size("brick") + lax.axis_index("brick")
+    groups = lax.axis_size("img") * lax.axis_size("brick")
+    images = offsets_ref.shape[1]
+    off = 2.0 * offsets_ref[...].astype(jnp.float32) - 1.0
+    step = max(rows, 8)
+    for start in range(0, phase_cos_ref.shape[0], step):
+        at = slice(start, start + step)
+        row = start + lax.broadcasted_iota(jnp.int32, (step, images), 0)
+        col = lax.broadcasted_iota(jnp.int32, (step, images), 1)
+        mine = col == (row // rows * groups + group) * rows + row % rows
+        off_x, off_y = (
+            jnp.sum(jnp.where(mine, off[i : i + 1, :], 0.0), axis=1, keepdims=True).astype(
+                jnp.int32
+            )
+            for i in range(2)
+        )
+        lane = lax.broadcasted_iota(jnp.int32, (step, LANES), 1)
+        u = jnp.bitwise_and(lane, frame_side - 1) - frame_side // 2
+        half = jnp.right_shift(lane, 6)
+        c1, s1 = cos_sin(u * off_x + half * off_y)
+        c2, s2 = cos_sin(2 * lane * off_y)
+        for k in range(K // LANES):
+            ck, sk = c2[:, k : k + 1], s2[:, k : k + 1]
+            phase_cos_ref[at, k * LANES : (k + 1) * LANES] = c1 * ck - s1 * sk
+            phase_sin_ref[at, k * LANES : (k + 1) * LANES] = s1 * ck + c1 * sk
+
+
 def source_plane(source):
     factor, offset, modulus = source
     return lax.rem(factor * lax.axis_index("orient") + offset, modulus)
@@ -116,44 +169,14 @@
 
 def score_kernel(first, source, choices, *refs):
     images_refs, refs = refs[:choices], refs[choices:]
-    offsets_ref, slices_ref, cos_ref, sin_ref = refs[:4]
-    if first:
-        terms_ref, based_ref, stats_ref, norm_ref, left_ref = refs[4:]
-    else:
-        norm_ref, _, _, stats_in_ref = refs[4:8]
-        terms_ref, based_ref, stats_ref, left_ref = refs[8:]
+    phase_cos_ref, phase_sin_ref, cos_ref, sin_ref = refs[:4]
+    norm_ref, slices_ref = refs[4:6]
+    stats_in_ref = None if first else refs[8]
+    terms_ref, based_ref, stats_ref, left_ref = refs[6 if first else 9 :]
     inv_noise = 100.0 / K
     rows = images_refs[0].shape[0]
     plane = source_plane(source)
-    group = lax.axis_index("img") * lax.axis_size("brick") + lax.axis_index("brick")
-    groups = lax.axis_size("img") * lax.axis_size("brick")
-    count = offsets_ref.shape[1]
-    row = lax.broadcasted_iota(jnp.int32, (rows, count), 0)
-    col = lax.broadcasted_iota(jnp.int32, (rows, count), 1)
-    mine = col == row + (plane * groups + group) * rows
-    off = 2.0 * offsets_ref[...].astype(jnp.float32) - 1.0
-    off_x, off_y = (
-        jnp.sum(jnp.where(mine, off[i : i + 1, :], 0.0), axis=1, keepdims=True).astype(jnp.int32)
-        for i in range(2)
-    )
-    if first:
-        orient = slices_ref.shape[0]
-        total = jnp.zeros((orient, LANES), jnp.float32)
-        for k in range(2 * K // LANES):
-            piece = slices_ref[:, k * LANES : (k + 1) * LANES].astype(jnp.float32)
-            total = total + piece * piece
-        norm_ref[...] = 0.5 * lax.dot_general(
-            jnp.ones((8, LANES), jnp.float32),
-            total,
-            (((1,), (1,)), ((), ())),
-            precision=lax.Precision.HIGHEST,
-            preferred_element_type=jnp.float32,
-        )
-    lane = lax.broadcasted_iota(jnp.int32, (rows, LANES), 1)
-    u = jnp.bitwise_and(lane, frame_side - 1) - frame_side // 2
-    half = jnp.right_shift(lane, 6)
-    c1, s1 = cos_sin(u * off_x + half * off_y)
-    c2, s2 = cos_sin(2 * lane * off_y)
+    tiles = 2 * K // LANES
     at_end = (lax.axis_index("orient") == 0) | (
         lax.axis_index("orient") == lax.axis_size("orient") - 1
     )
@@ -163,29 +186,28 @@
             return images_refs[0][:, at].astype(jnp.float32)
         return jnp.where(at_end, images_refs[0][:, at], images_refs[1][:, at]).astype(jnp.float32)
 
-    for k in range(K // LANES):
+    where = pl.ds(pl.multiple_of(plane * rows, rows), rows)
+    for k in range(tiles // 2):
         re_at = slice(k * LANES, (k + 1) * LANES)
         im_at = slice(K + k * LANES, K + (k + 1) * LANES)
         x_re, x_im = pixels(re_at), pixels(im_at)
-        ck, sk = c2[:, k : k + 1], s2[:, k : k + 1]
-        cb = c1 * ck - s1 * sk
-        sb = s1 * ck + c1 * sk
+        cb, sb = phase_cos_ref[where, re_at], phase_sin_ref[where, re_at]
         y_re = x_re * cb + x_im * sb
         y_im = x_im * cb - x_re * sb
-        where = pl.ds(pl.multiple_of(plane * rows, rows), rows)
         based_ref[where, re_at] = y_re.astype(jnp.bfloat16)
         based_ref[where, im_at] = y_im.astype(jnp.bfloat16)
+        minus_re = -y_re
         re_rows, im_rows = [], []
         for t in range(PAIRS):
             cos_t = cos_ref[t : t + 1, re_at]
             sin_t = sin_ref[t : t + 1, re_at]
             re_rows += [y_re * cos_t, y_im * sin_t]
-            im_rows += [y_im * cos_t, -(y_re * sin_t)]
-        left_ref[:, re_at] = jnp.concatenate(re_rows, axis=0).astype(jnp.bfloat16)
-        left_ref[:, im_at] = jnp.concatenate(im_rows, axis=0).astype(jnp.bfloat16)
+            im_rows += [y_im * cos_t, minus_re * sin_t]
+        left_ref[k] = jnp.concatenate(re_rows, axis=0).astype(jnp.bfloat16)
+        left_ref[tiles // 2 + k] = jnp.concatenate(im_rows, axis=0).astype(jnp.bfloat16)
     both = lax.dot_general(
-        left_ref[...],
-        slices_ref[...],
+        jnp.concatenate([left_ref[k] for k in range(tiles)], axis=1),
+        jnp.concatenate([slices_ref[k] for k in range(tiles)], axis=1),
         (((1,), (1,)), ((), ())),
         preferred_element_type=jnp.float32,
     )
@@ -308,7 +330,11 @@
     return [pltpu.with_memory_space_constraint(x, pltpu.VMEM) for x in arrays]
 
 
-def call(kernel, name, out_shape, inputs, scratch=(), aliases=None, chip_out=True, hbm_in=False):
+def off_chip(*arrays):
+    return [pltpu.with_memory_space_constraint(x, pltpu.HBM) for x in arrays]
+
+
+def call(kernel, out_shape, inputs, scratch=(), aliases=None, chip_out=True, hbm_in=False):
     spec = pl.BlockSpec(memory_space=pltpu.VMEM)
     in_spec = pl.BlockSpec(memory_space=pltpu.HBM) if hbm_in else spec
     single = not isinstance(out_shape, list)
@@ -323,7 +349,6 @@
         scratch_shapes=list(scratch),
         input_output_aliases=aliases or {},
         compiler_params=pltpu.CompilerParams(vmem_limit_bytes=VMEM_LIMIT),
-        name=name,
     )(*inputs)
     return out[0] if single else out
 
@@ -345,7 +370,10 @@
     count = lax.axis_size("orient")
     if count != 4:
         return [array] + [shift(array, k) for k in range(1, count)]
-    return [array] + [swap(array, k) for k in (3, 2, 1)]
+    moved = [array]
+    for k in (3, 2, 1):
+        moved.append(swap(array, k))
+    return moved
 
 
 def after(state, images):
@@ -363,6 +391,7 @@
     count = rows * orient_count
     vox = interp.shape[3]
     f32, bf16 = jnp.float32, jnp.bfloat16
+    tiles = 2 * K // LANES
     relay = orient_count == 4
     if relay:
         first = lax.ppermute(images, "orient", [(0, 2), (3, 1), (2, 3), (1, 0)])
@@ -372,30 +401,25 @@
             for k in range(1, orient_count)
         ]
 
-    weights, cover, hit, cos_table, sin_table, own, offsets_v = call(
-        functools.partial(setup_kernel, bricks),
-        "setup",
+    cos_table, sin_table, own, phase_cos, phase_sin, norm, packed = call(
+        phase_kernel,
         [
-            jax.ShapeDtypeStruct((K, 2 * vox), bf16),
-            jax.ShapeDtypeStruct((NSEG, vox), f32),
-            jax.ShapeDtypeStruct((NSEG * bricks, orient), bf16),
             jax.ShapeDtypeStruct((PAIRS, K), f32),
             jax.ShapeDtypeStruct((PAIRS, K), f32),
             jax.ShapeDtypeStruct(images.shape, bf16),
-            jax.ShapeDtypeStruct(offsets.shape[::-1], jnp.int32),
+            jax.ShapeDtypeStruct((count, K), f32),
+            jax.ShapeDtypeStruct((count, K), f32),
+            jax.ShapeDtypeStruct((8, orient), f32),
+            jax.ShapeDtypeStruct((tiles, orient, LANES), bf16),
         ],
-        [
-            pltpu.with_memory_space_constraint(x, pltpu.HBM)
-            for x in (interp, seg_map.reshape(-1, LANES), images, offsets.T)
-        ],
+        off_chip(images, offsets.T, slices),
         scratch=[
-            pltpu.VMEM(interp.shape[1:], jnp.int32),
-            pltpu.VMEM((seg_map.shape[0] // LANES, LANES), jnp.int32),
-            pltpu.SemaphoreType.DMA((NSEG + 3,)),
+            pltpu.VMEM(offsets.shape[::-1], jnp.int32),
+            pltpu.SemaphoreType.DMA((tiles + 2,)),
         ],
         hbm_in=True,
     )
-    constant = on_chip(offsets_v, slices, cos_table, sin_table)
+    constant = on_chip(phase_cos, phase_sin, cos_table, sin_table, norm, packed)
     state_shapes = [
         jax.ShapeDtypeStruct((SHIFTS, count, orient), bf16),
         jax.ShapeDtypeStruct((count, 2 * K), bf16),
@@ -407,40 +431,56 @@
         inputs = on_chip(*arrays) + constant
         if not first:
             inputs += on_chip(*earlier)
-        at = len(arrays) + 5
+        at = len(arrays) + 6
         return call(
             functools.partial(score_kernel, first, source, len(arrays)),
-            "scores",
-            state_shapes + ([jax.ShapeDtypeStruct((8, orient), f32)] if first else []),
+            state_shapes,
             inputs,
-            scratch=[pltpu.VMEM((SHIFTS * rows, 2 * K), bf16)],
+            scratch=[pltpu.VMEM((tiles, SHIFTS * rows, LANES), bf16)],
             aliases={} if first else {at + i: i for i in range(3)},
         )
 
-    *state, norm = scored((1, 0, orient_count), [own], None)
     if relay:
-        state, again = after(state, images)
+        own, again = lax.optimization_barrier((own, images))
         second = lax.ppermute(again, "orient", [(0, 1), (3, 2), (1, 3), (2, 0)])
-        first, again = lax.optimization_barrier((first, again))
+    state = scored((1, 0, orient_count), [own], None)
+    state, raw = after(state, interp)
+    weights, cover, hit = call(
+        functools.partial(weight_kernel, bricks),
+        [
+            jax.ShapeDtypeStruct((K, 2 * vox), bf16),
+            jax.ShapeDtypeStruct((NSEG, vox), f32),
+            jax.ShapeDtypeStruct((NSEG * bricks, orient), bf16),
+        ],
+        off_chip(raw, seg_map.reshape(-1, LANES)),
+        scratch=[
+            pltpu.VMEM(interp.shape[1:], jnp.int32),
+            pltpu.VMEM((seg_map.shape[0] // LANES, LANES), jnp.int32),
+            pltpu.SemaphoreType.DMA((NSEG + 1,)),
+        ],
+        hbm_in=True,
+    )
+    if relay:
+        state, first = after(state, first)
+        first, again = lax.optimization_barrier((first, images))
         relayed = lax.ppermute(first, "orient", [(2, 3), (1, 0)])
-        middle = lax.ppermute(again, "orient", [(1, 2), (2, 1)])
-        state = scored((2, 1, 5), [first], [norm, *state])
-        state = scored((3, 2, 5), [second], [norm, *state])
-        state = scored((4, 3, 5), [relayed, middle], [norm, *state])
+        middle = lax.ppermute(again, "orient", [(1, 2), (2, 1), (0, 0), (3, 3)])
+        first, cover = lax.optimization_barrier((first, cover))
+        state = scored((2, 1, 5), [first], state)
+        state = scored((3, 2, 5), [second], state)
+        state = scored((4, 3, 5), [relayed, middle], state)
     else:
         for source, array in waiting:
-            state = scored(source, [array], [norm, *state])
+            state = scored(source, [array], state)
     terms, based, stats = state
     gathered = everyone(stats)
     shares = call(
         share_kernel,
-        "shares",
         jax.ShapeDtypeStruct((SHIFTS, NSEG * bricks, count), f32),
         on_chip(terms, hit),
     )
     outgoing = call(
         functools.partial(brick_kernel, orient_count),
-        "bricks",
         jax.ShapeDtypeStruct((bricks, 2, K + LANES), bf16),
         on_chip(shares, based, cos_table, sin_table, *gathered),
         scratch=[
@@ -453,7 +493,6 @@
     )
     return call(
         final_kernel,
-        "insert",
         [
             jax.ShapeDtypeStruct((1, 2, vox), f32),
             jax.ShapeDtypeStruct((1, 1, vox), f32),

time: 47.1 us -> 46.5 us (0.987)
  waiting for transfers between devices: 10.4 us -> 8.77 us
  Pallas kernels: 13.1 us -> 14.1 us
    ppermute x1, waiting for transfers between devices: 2.49 us -> 0.74 us  [per_device(): second = lax.ppermute(again, 'orient', [(0, 1), (3, 2), (1, 3), (2, 0)])]
    pallas_call x8 -> x9, Pallas kernels: 13.1 us -> 14.1 us  [call(): pl.pallas_call(kernel, in_specs=[in_spec] * len(inputs), out_specs=[spec]...]
    ppermute x1, waiting for transfers between devices: 3.39 us -> 3.93 us  [per_device(): relayed = lax.ppermute(first, 'orient', [(2, 3), (1, 0)])]
  transfers between devices with their start and end apart: 7 -> 7, of which waited for: 5 -> 5; matrix products, arithmetic and copies ran while one was open for 0% -> 0% of each run, Pallas kernels for 19% -> 23%
where the time goes in v7:
time: 46.5 us; the launch traced here: 46.3 us
  Pallas kernels  14.1 us (30%)
  blocking collectives  12.2 us (26%)
  starting transfers between devices  10.6 us (23%)
  waiting for transfers between devices  8.77 us (19%)
  between operations  0.71 us (2%)
    pallas_call x9, Pallas kernels, call(): pl.pallas_call(kernel, in_specs=[in_spec] * len(inputs), out_specs=[spec]...  14.1 us
    all_to_all x1, blocking collectives, per_device(): lax.all_to_all(outgoing, ('orient', 'img', 'brick'), split_axis=0, concat...  12.2 us
    ppermute x3, starting transfers between devices, swap(): lax.ppermute(array, 'orient', [(i, i ^ amount) for i in range(count)])  4.42 us
    ppermute x1, starting transfers between devices, per_device(): first = lax.ppermute(images, 'orient', [(0, 2), (3, 1), (2, 3), (1, 0)])  4.12 us
    ppermute x1, waiting for transfers between devices, per_device(): relayed = lax.ppermute(first, 'orient', [(2, 3), (1, 0)])  3.93 us
    ppermute x3, waiting for transfers between devices, swap(): lax.ppermute(array, 'orient', [(i, i ^ amount) for i in range(count)])  2.15 us
    ppermute x1, waiting for transfers between devices, per_device(): first = lax.ppermute(images, 'orient', [(0, 2), (3, 1), (2, 3), (1, 0)])  1.94 us
    ppermute x1, starting transfers between devices, per_device(): relayed = lax.ppermute(first, 'orient', [(2, 3), (1, 0)])  1.28 us
  transfers between devices with their start and end apart: 7, of which 5 were waited for; matrix products, arithmetic and copies ran while one was open for 0% of the time, Pallas kernels for 23%

profile of v7, /device:TPU:0, one launch (start us, length us, event | category | flops | bytes accessed | tf_op | source)
XLA Modules:
  0.0 46.3 jit_solution(14289119030407482890)
XLA Ops:
  0.6 0.0 copy-start
  0.6 4.1 %collective-permute-start = (bf16[32,4096]{1,0:T(8,128)(2,1)}, bf16[32,4096]{1,0:T(8,128)(2,1)S(1)}, u32[]{:S(2)}, u32[]{:S(2)}) collective-permute-start(bf16[32,4096]{1,0:T(8,128)(2,1)} %images_hbm.1), channel_id=1, source_target_pairs={{0,8},{12,4},{8,12},{4,0},{1,9},{13,5},{9,13},{5,1},{2,10},{14,6},... | collective-permute-start | bytes 786440 | tf_op jit(solution)/shard_map/ppermute | solution.py:397
  4.8 3.4 %shard_map.68 = (f32[8,2048]{1,0:T(8,128)S(1)}, f32[8,2048]{1,0:T(8,128)S(1)}, bf16[32,4096]{1,0:T(8,128)(2,1)S(1)}, f32[128,2048]{1,0:T(8,128)S(1)}, f32[128,20...) custom-call(bf16[32,4096]{1,0:T(8,128)(2,1)} %images_hbm.1, s32[2,512]{1,0:T(2,128)} %bitcast.4, ...), custom_call_target="tpu_custom_call" | custom-call | tf_op jit(solution)/shard_map/pallas_call | solution.py:344
  8.2 0.0 copy-done
  8.2 0.1 collective-permute-start.3
  8.2 1.6 %shard_map.69 = (bf16[16,128,256]{2,1,0:T(8,128)(2,1)S(1)}, bf16[128,4096]{1,0:T(8,128)(2,1)S(1)}, f32[8,128]{1,0:T(8,128)S(1)}) custom-call(bf16[32,4096]{1,0:T(8,128)(2,1)S(1)} %get-tuple-element.37.refs_0_, f32[128,2048]{1,0:T(8,128)S(1)} %get-tuple-element.38.refs_1_.refs_2_, f32[128,2048]{1,0:T(8,128)S(1)} %get-tuple-element.39.refs_2_.refs_3_, ...), custom_call_target="tpu_custom_call" | custom-call | tf_op jit(solution)/shard_map/pallas_call | solution.py:344
  9.8 1.9 %collective-permute-done.refs_0_ = bf16[32,4096]{1,0:T(8,128)(2,1)S(1)} collective-permute-done((bf16[32,4096]{1,0:T(8,128)(2,1)}, bf16[32,4096]{1,0:T(8,128)(2,1)S(1)}, u32[]{:S(2)}, u32[]{:S(2)}) %collective-permute-start) | collective-permute-done | bytes 262176 | tf_op jit(solution)/shard_map/ppermute | solution.py:397
  11.8 1.3 %collective-permute-start.1 = (bf16[32,4096]{1,0:T(8,128)(2,1)S(1)}, bf16[32,4096]{1,0:T(8,128)(2,1)S(1)}, u32[]{:S(2)}, u32[]{:S(2)}) collective-permute-start(bf16[32,4096]{1,0:T(8,128)(2,1)S(1)} %collective-permute-done.refs_0_), channel_id=1, source_target_pairs={{8,12},{4,0},{9,13},{5,1},{10,14},{6,2},{11,15},{7,3},{24,28},{20,... | collective-permute-start | bytes 786440 | tf_op jit(solution)/shard_map/ppermute | solution.py:466
  13.1 0.7 %collective-permute-start.2 = (bf16[32,4096]{1,0:T(8,128)(2,1)S(1)}, bf16[32,4096]{1,0:T(8,128)(2,1)S(1)}, u32[]{:S(2)}, u32[]{:S(2)}) collective-permute-start(bf16[32,4096]{1,0:T(8,128)(2,1)S(1)} %copy-done), channel_id=1, source_target_pairs={{4,8},{8,4},{0,0},{12,12},{5,9},{9,5},{1,1},{13,13},{6,10},{10,6},... | collective-permute-start | bytes 786440 | tf_op jit(solution)/shard_map/ppermute | solution.py:467
  13.7 2.0 %shard_map.70 = (bf16[2048,512]{1,0:T(8,128)(2,1)S(1)}, f32[8,256]{1,0:T(8,128)S(1)}, bf16[128,256]{1,0:T(8,128)(2,1)S(1)}) custom-call(s32[1,8,256,256]{3,2,1,0:T(8,128)} %interp_hbm, s32[64,128]{1,0:T(8,128)} %bitcast.3), custom_call_target="tpu_custom_call" | custom-call | tf_op jit(solution)/shard_map/pallas_call | solution.py:344
  15.7 1.6 %shard_map.71 = (bf16[16,128,256]{2,1,0:T(8,128)(2,1)S(1)}, bf16[128,4096]{1,0:T(8,128)(2,1)S(1)}, f32[8,128]{1,0:T(8,128)S(1)}) custom-call(bf16[32,4096]{1,0:T(8,128)(2,1)S(1)} %collective-permute-done.refs_0_, f32[128,2048]{1,0:T(8,128)S(1)} %get-tuple-element.38.refs_1_.refs_2_, ...), custom_call_target="tpu_custom_call", output_to_operand_aliasing={{0}: (7, {}), {1}: (8, {}), {2}: (9, {})} | custom-call | tf_op jit(solution)/shard_map/pallas_call | solution.py:344
  17.3 0.7 %collective-permute-done.3.refs_0_ = bf16[32,4096]{1,0:T(8,128)(2,1)S(1)} collective-permute-done((bf16[32,4096]{1,0:T(8,128)(2,1)S(1)}, bf16[32,4096]{1,0:T(8,128)(2,1)S(1)}, u32[]{:S(2)}, u32[]{:S(2)}) %collective-permute-start.3) | collective-permute-done | bytes 262176 | tf_op jit(solution)/shard_map/ppermute | solution.py:445
  18.1 1.6 %shard_map.72 = (bf16[16,128,256]{2,1,0:T(8,128)(2,1)S(1)}, bf16[128,4096]{1,0:T(8,128)(2,1)S(1)}, f32[8,128]{1,0:T(8,128)S(1)}) custom-call(bf16[32,4096]{1,0:T(8,128)(2,1)S(1)} %collective-permute-done.3.refs_0_, f32[128,2048]{1,0:T(8,128)S(1)} %get-tuple-element.38.refs_1_.refs_2_, ...), custom_call_target="tpu_custom_call", output_to_operand_aliasing={{0}: (7, {}), {1}: (8, {}), {2}: (9, {})} | custom-call | tf_op jit(solution)/shard_map/pallas_call | solution.py:344
  19.6 3.9 %collective-permute-done.1.refs_0_ = bf16[32,4096]{1,0:T(8,128)(2,1)S(1)} collective-permute-done((bf16[32,4096]{1,0:T(8,128)(2,1)S(1)}, bf16[32,4096]{1,0:T(8,128)(2,1)S(1)}, u32[]{:S(2)}, u32[]{:S(2)}) %collective-permute-start.1) | collective-permute-done | bytes 262176 | tf_op jit(solution)/shard_map/ppermute | solution.py:466
  23.6 0.0 collective-permute-done.2.refs_1_
  23.6 1.6 %shard_map.73 = (bf16[16,128,256]{2,1,0:T(8,128)(2,1)S(1)}, bf16[128,4096]{1,0:T(8,128)(2,1)S(1)}, f32[8,128]{1,0:T(8,128)S(1)}) custom-call(bf16[32,4096]{1,0:T(8,128)(2,1)S(1)} %collective-permute-done.1.refs_0_, bf16[32,4096]{1,0:T(8,128)(2,1)S(1)} %collective-permute-done.2.refs_1_, ...), custom_call_target="tpu_custom_call", output_to_operand_aliasing={{0}: (8, {}), {1}: (9, {}), {2}: (10, {})} | custom-call | tf_op jit(solution)/shard_map/pallas_call | solution.py:344
  25.2 2.5 %collective-permute-start.4 = (f32[8,128]{1,0:T(8,128)S(1)}, f32[8,128]{1,0:T(8,128)S(1)}, u32[]{:S(2)}, u32[]{:S(2)}) collective-permute-start(f32[8,128]{1,0:T(8,128)S(1)} %get-tuple-element.65.rest_0_), channel_id=1, source_target_pairs={{0,12},{4,8},{8,4},{12,0},{1,13},{5,9},{9,5},{13,1},{2,14},{6,10},... | collective-permute-start | bytes 12296 | tf_op jit(solution)/shard_map/ppermute | solution.py:361
  27.7 0.0 collective-permute-start.5
  27.7 1.9 %collective-permute-start.6 = (f32[8,128]{1,0:T(8,128)S(1)}, f32[8,128]{1,0:T(8,128)S(1)}, u32[]{:S(2)}, u32[]{:S(2)}) collective-permute-start(f32[8,128]{1,0:T(8,128)S(1)} %get-tuple-element.65.rest_0_), channel_id=1, source_target_pairs={{0,4},{4,0},{8,12},{12,8},{1,5},{5,1},{9,13},{13,9},{2,6},{6,2},{1... | collective-permute-start | bytes 12296 | tf_op jit(solution)/shard_map/ppermute | solution.py:361
  29.6 0.4 shard_map.74.share_ref
  30.0 0.6 %collective-permute-done.4.rest_1_ = f32[8,128]{1,0:T(8,128)S(1)} collective-permute-done((f32[8,128]{1,0:T(8,128)S(1)}, f32[8,128]{1,0:T(8,128)S(1)}, u32[]{:S(2)}, u32[]{:S(2)}) %collective-permute-start.4) | collective-permute-done | bytes 4128 | tf_op jit(solution)/shard_map/ppermute | solution.py:361
  30.6 1.6 %collective-permute-done.5.rest_2_ = f32[8,128]{1,0:T(8,128)S(1)} collective-permute-done((f32[8,128]{1,0:T(8,128)S(1)}, f32[8,128]{1,0:T(8,128)S(1)}, u32[]{:S(2)}, u32[]{:S(2)}) %collective-permute-start.5) | collective-permute-done | bytes 4128 | tf_op jit(solution)/shard_map/ppermute | solution.py:361
  32.2 0.0 collective-permute-done.6.rest_3_
  32.2 0.9 %shard_map.75 = bf16[16,2,2176]{2,1,0:T(2,128)(2,1)S(1)} custom-call(f32[16,128,128]{2,1,0:T(8,128)S(1)} %shard_map.74.share_ref, bf16[128,4096]{1,0:T(8,128)(2,1)S(1)} %get-tuple-element.64.based_ref, f32[8,2048]{1,0:T(8,128)S(1)} %get-tuple-element.40.refs_3_.refs_4_.cos_ref, f32[8,2048]{1,0:T(8,128)S(1)} %get-tuple-element.41.refs_4_.refs_5_.sin_ref, ...), custom_call_target="tpu_custom_call" | custom-call | tf_op jit(solution)/shard_map/pallas_call | solution.py:344
  33.1 12.2 %all_to_all.5.arrived_ref = bf16[16,2,2176]{2,1,0:T(2,128)(2,1)S(1)} all-to-all(bf16[16,2,2176]{2,1,0:T(2,128)(2,1)S(1)} %shard_map.75), channel_id=1, replica_groups=mesh['groups'=2,'orient'=4,'img'=2,'brick'=2] {'orient','img','brick'}, dimensions={0} | all-to-all | bytes 278528 | tf_op jit(solution)/shard_map/all_to_all | solution.py:491
  45.3 1.0 %shard_map.76 = (f32[1,2,256]{2,1,0:T(2,128)}, f32[1,1,256]{2,1,0:T(1,128)}) custom-call(bf16[16,2,2176]{2,1,0:T(2,128)(2,1)S(1)} %all_to_all.5.arrived_ref, bf16[2048,512]{1,0:T(8,128)(2,1)S(1)} %get-tuple-element.66.weight_ref, f32[8,256]{1,0:T(8,128)S(1)} %get-tuple-element.67.cover_ref), custom_call_target="tpu_custom_call" | custom-call | tf_op jit(solution)/shard_map/pallas_call | solution.py:344
Async XLA Ops:
  0.6 7.5 %copy-start = (bf16[32,4096]{1,0:T(8,128)(2,1)S(1)}, bf16[32,4096]{1,0:T(8,128)(2,1)}, u32[]{:S(2)}) copy-start(bf16[32,4096]{1,0:T(8,128)(2,1)} %images_hbm.1) | copy-start | bytes 786436
  0.6 11.1 %collective-permute-start = (bf16[32,4096]{1,0:T(8,128)(2,1)}, bf16[32,4096]{1,0:T(8,128)(2,1)S(1)}, u32[]{:S(2)}, u32[]{:S(2)}) collective-permute-start(bf16[32,4096]{1,0:T(8,128)(2,1)} %images_hbm.1), channel_id=1, source_target_pairs={{0,8},{12,4},{8,12},{4,0},{1,9},{13,5},{9,13},{5,1},{2,10},{14,6},... | collective-permute-start | bytes 786440 | tf_op jit(solution)/shard_map/ppermute | solution.py:397
  8.2 9.9 %collective-permute-start.3 = (bf16[32,4096]{1,0:T(8,128)(2,1)S(1)}, bf16[32,4096]{1,0:T(8,128)(2,1)S(1)}, u32[]{:S(2)}, u32[]{:S(2)}) collective-permute-start(bf16[32,4096]{1,0:T(8,128)(2,1)S(1)} %copy-done), channel_id=1, source_target_pairs={{0,4},{12,8},{4,12},{8,0},{1,5},{13,9},{5,13},{9,1},{2,6},{14,10},... | collective-permute-start | bytes 786440 | tf_op jit(solution)/shard_map/ppermute | solution.py:445
  11.8 11.8 %collective-permute-start.1 = (bf16[32,4096]{1,0:T(8,128)(2,1)S(1)}, bf16[32,4096]{1,0:T(8,128)(2,1)S(1)}, u32[]{:S(2)}, u32[]{:S(2)}) collective-permute-start(bf16[32,4096]{1,0:T(8,128)(2,1)S(1)} %collective-permute-done.refs_0_), channel_id=1, source_target_pairs={{8,12},{4,0},{9,13},{5,1},{10,14},{6,2},{11,15},{7,3},{24,28},{20,... | collective-permute-start | bytes 786440 | tf_op jit(solution)/shard_map/ppermute | solution.py:466
  13.1 10.5 %collective-permute-start.2 = (bf16[32,4096]{1,0:T(8,128)(2,1)S(1)}, bf16[32,4096]{1,0:T(8,128)(2,1)S(1)}, u32[]{:S(2)}, u32[]{:S(2)}) collective-permute-start(bf16[32,4096]{1,0:T(8,128)(2,1)S(1)} %copy-done), channel_id=1, source_target_pairs={{4,8},{8,4},{0,0},{12,12},{5,9},{9,5},{1,1},{13,13},{6,10},{10,6},... | collective-permute-start | bytes 786440 | tf_op jit(solution)/shard_map/ppermute | solution.py:467
  25.2 5.4 %collective-permute-start.4 = (f32[8,128]{1,0:T(8,128)S(1)}, f32[8,128]{1,0:T(8,128)S(1)}, u32[]{:S(2)}, u32[]{:S(2)}) collective-permute-start(f32[8,128]{1,0:T(8,128)S(1)} %get-tuple-element.65.rest_0_), channel_id=1, source_target_pairs={{0,12},{4,8},{8,4},{12,0},{1,13},{5,9},{9,5},{13,1},{2,14},{6,10},... | collective-permute-start | bytes 12296 | tf_op jit(solution)/shard_map/ppermute | solution.py:361
  27.7 4.5 %collective-permute-start.5 = (f32[8,128]{1,0:T(8,128)S(1)}, f32[8,128]{1,0:T(8,128)S(1)}, u32[]{:S(2)}, u32[]{:S(2)}) collective-permute-start(f32[8,128]{1,0:T(8,128)S(1)} %get-tuple-element.65.rest_0_), channel_id=1, source_target_pairs={{0,8},{4,12},{8,0},{12,4},{1,9},{5,13},{9,1},{13,5},{2,10},{6,14},... | collective-permute-start | bytes 12296 | tf_op jit(solution)/shard_map/ppermute | solution.py:361
  27.7 4.5 %collective-permute-start.6 = (f32[8,128]{1,0:T(8,128)S(1)}, f32[8,128]{1,0:T(8,128)S(1)}, u32[]{:S(2)}, u32[]{:S(2)}) collective-permute-start(f32[8,128]{1,0:T(8,128)S(1)} %get-tuple-element.65.rest_0_), channel_id=1, source_target_pairs={{0,4},{4,0},{8,12},{12,8},{1,5},{5,1},{9,13},{13,9},{2,6},{6,2},{1... | collective-permute-start | bytes 12296 | tf_op jit(solution)/shard_map/ppermute | solution.py:361

commit v8 on v7

--- a/solution.py
+++ b/solution.py
@@ -254,7 +254,7 @@
 
 
 def brick_kernel(others, share_ref, based_ref, cos_ref, sin_ref, *rest):
-    stats_refs, (out_ref, pairs_ref, sums_ref) = rest[:others], rest[others:]
+    stats_refs, out_refs, (pairs_ref, sums_ref) = rest[:others], rest[others:-2], rest[-2:]
     bricks = share_ref.shape[1] // NSEG
     count = based_ref.shape[0]
     own_top = stats_refs[0][0:1, :]
@@ -303,12 +303,35 @@
         low = jnp.where(lane == j, mass_low[at], low)
     sums_ref[:, 0, K:] = high
     sums_ref[:, 1, K:] = low
-    out_ref[...] = sums_ref[...].astype(jnp.bfloat16)
-
-
-def final_kernel(arrived_ref, weight_ref, cover_ref, values_ref, mass_ref):
+    if len(out_refs) == 1:
+        out_refs[0][...] = sums_ref[...].astype(jnp.bfloat16)
+        return
+    near = 2 * lax.axis_index("img") + lax.axis_index("brick")
+    for m, ref in enumerate(out_refs):
+        for z in range(ref.shape[0]):
+            ref[z] = sums_ref[z * len(out_refs) + jnp.bitwise_xor(near, m)].astype(jnp.bfloat16)
+
+
+def plane_kernel(*refs):
+    in_refs, out_refs = refs[: len(refs) // 2], refs[len(refs) // 2 :]
+    plane = lax.axis_index("orient")
+    for m, ref in enumerate(out_refs):
+        target = jnp.bitwise_xor(plane, m)
+        total = in_refs[0][target].astype(jnp.float32)
+        for other in in_refs[1:]:
+            total = total + other[target].astype(jnp.float32)
+        ref[...] = total.astype(jnp.bfloat16)
+
+
+def final_kernel(*refs):
+    weight_ref, cover_ref, values_ref, mass_ref = refs[-4:]
     vox = cover_ref.shape[1]
-    total = jnp.sum(arrived_ref[...].astype(jnp.float32), axis=0)
+    if len(refs) == 5:
+        total = jnp.sum(refs[0][...].astype(jnp.float32), axis=0)
+    else:
+        total = refs[0][...].astype(jnp.float32)
+        for ref in refs[1:-4]:
+            total = total + ref[...].astype(jnp.float32)
     rest = total[:, :K]
     parts = []
     for _ in range(3):
@@ -393,6 +416,7 @@
     f32, bf16 = jnp.float32, jnp.bfloat16
     tiles = 2 * K // LANES
     relay = orient_count == 4
+    staged = relay and group_count == 4
     if relay:
         first = lax.ppermute(images, "orient", [(0, 2), (3, 1), (2, 3), (1, 0)])
     else:
@@ -475,29 +499,39 @@
     terms, based, stats = state
     gathered = everyone(stats)
     shares = call(
-        share_kernel,
-        jax.ShapeDtypeStruct((SHIFTS, NSEG * bricks, count), f32),
-        on_chip(terms, hit),
+        share_kernel, jax.ShapeDtypeStruct((SHIFTS, NSEG * bricks, count), f32), on_chip(terms, hit)
     )
     outgoing = call(
         functools.partial(brick_kernel, orient_count),
-        jax.ShapeDtypeStruct((bricks, 2, K + LANES), bf16),
+        [jax.ShapeDtypeStruct((bricks // 4, 2, K + LANES), bf16)] * 4
+        if staged
+        else jax.ShapeDtypeStruct((bricks, 2, K + LANES), bf16),
         on_chip(shares, based, cos_table, sin_table, *gathered),
         scratch=[
             pltpu.VMEM((NSEG, SHIFTS * bricks, count), bf16),
             pltpu.VMEM((bricks, 2, K + LANES), f32),
         ],
     )
-    received = lax.all_to_all(
-        outgoing, ("orient", "img", "brick"), split_axis=0, concat_axis=0, tiled=True
-    )
+    if staged:
+        parts = [outgoing[0]] + [
+            lax.ppermute(outgoing[m], ("img", "brick"), [(i, i ^ m) for i in range(4)])
+            for m in (1, 2, 3)
+        ]
+        sums = call(plane_kernel, [jax.ShapeDtypeStruct((2, K + LANES), bf16)] * 4, on_chip(*parts))
+        received = [sums[0]] + [swap(sums[m], m) for m in (3, 2, 1)]
+    else:
+        received = [
+            lax.all_to_all(
+                outgoing, ("orient", "img", "brick"), split_axis=0, concat_axis=0, tiled=True
+            )
+        ]
     return call(
         final_kernel,
         [
             jax.ShapeDtypeStruct((1, 2, vox), f32),
             jax.ShapeDtypeStruct((1, 1, vox), f32),
         ],
-        on_chip(received, weights, cover),
+        on_chip(*received, weights, cover),
         chip_out=False,
     )
 

time: 46.5 us -> 45.6 us (0.981)
  blocking collectives: 12.2 us -> 0 us
  starting transfers between devices: 10.6 us -> 16.9 us
  waiting for transfers between devices: 8.77 us -> 13.6 us
    all_to_all x1 -> x0, blocking collectives: 12.2 us -> none  [per_device(): lax.all_to_all(outgoing, ('orient', 'img', 'brick'), split_axis=0, concat...]
    ppermute x3 -> x6, starting transfers between devices: 4.42 us -> 8.87 us  [swap(): lax.ppermute(array, 'orient', [(i, i ^ amount) for i in range(count)])]
    ppermute x0 -> x3, waiting for transfers between devices: none -> 3.11 us  [per_device(): lax.ppermute(outgoing[m], ('img', 'brick'), [(i, i ^ m) for i in range(4)])]
    ppermute x0 -> x3, starting transfers between devices: none -> 1.92 us  [per_device(): lax.ppermute(outgoing[m], ('img', 'brick'), [(i, i ^ m) for i in range(4)])]
    ppermute x3 -> x6, waiting for transfers between devices: 2.15 us -> 3.89 us  [swap(): lax.ppermute(array, 'orient', [(i, i ^ amount) for i in range(count)])]
    pallas_call x9 -> x10, Pallas kernels: 14.1 us -> 14.1 us  [call(): pl.pallas_call(kernel, in_specs=[in_spec] * len(inputs), out_specs=[spec]...]
  transfers between devices with their start and end apart: 7 -> 13, of which waited for: 5 -> 10; matrix products, arithmetic and copies ran while one was open for 0% -> 0% of each run, Pallas kernels for 23% -> 23%
where the time goes in v8:
time: 45.6 us; the launch traced here: 45.4 us
  starting transfers between devices  16.9 us (37%)
  Pallas kernels  14.1 us (31%)
  waiting for transfers between devices  13.6 us (30%)
  between operations  0.72 us (2%)
    pallas_call x10, Pallas kernels, call(): pl.pallas_call(kernel, in_specs=[in_spec] * len(inputs), out_specs=[spec]...  14.1 us
    ppermute x6, starting transfers between devices, swap(): lax.ppermute(array, 'orient', [(i, i ^ amount) for i in range(count)])  8.87 us
    ppermute x1, starting transfers between devices, per_device(): first = lax.ppermute(images, 'orient', [(0, 2), (3, 1), (2, 3), (1, 0)])  4.12 us
    ppermute x1, waiting for transfers between devices, per_device(): relayed = lax.ppermute(first, 'orient', [(2, 3), (1, 0)])  3.93 us
    ppermute x6, waiting for transfers between devices, swap(): lax.ppermute(array, 'orient', [(i, i ^ amount) for i in range(count)])  3.89 us
    ppermute x3, waiting for transfers between devices, per_device(): lax.ppermute(outgoing[m], ('img', 'brick'), [(i, i ^ m) for i in range(4)])  3.11 us
    ppermute x1, waiting for transfers between devices, per_device(): first = lax.ppermute(images, 'orient', [(0, 2), (3, 1), (2, 3), (1, 0)])  1.94 us
    ppermute x3, starting transfers between devices, per_device(): lax.ppermute(outgoing[m], ('img', 'brick'), [(i, i ^ m) for i in range(4)])  1.92 us
  transfers between devices with their start and end apart: 13, of which 10 were waited for; matrix products, arithmetic and copies ran while one was open for 0% of the time, Pallas kernels for 23%

profile of v8, /device:TPU:0, one launch (start us, length us, event | category | flops | bytes accessed | tf_op | source)
XLA Modules:
  0.0 45.4 jit_solution(6529806443556043581)
XLA Ops:
  0.6 0.0 copy-start
  0.6 4.1 %collective-permute-start = (bf16[32,4096]{1,0:T(8,128)(2,1)}, bf16[32,4096]{1,0:T(8,128)(2,1)S(1)}, u32[]{:S(2)}, u32[]{:S(2)}) collective-permute-start(bf16[32,4096]{1,0:T(8,128)(2,1)} %images_hbm.1), channel_id=1, source_target_pairs={{0,8},{12,4},{8,12},{4,0},{1,9},{13,5},{9,13},{5,1},{2,10},{14,6},... | collective-permute-start | bytes 786440 | tf_op jit(solution)/shard_map/ppermute | solution.py:421
  4.8 3.4 %shard_map.68 = (f32[8,2048]{1,0:T(8,128)S(1)}, f32[8,2048]{1,0:T(8,128)S(1)}, bf16[32,4096]{1,0:T(8,128)(2,1)S(1)}, f32[128,2048]{1,0:T(8,128)S(1)}, f32[128,20...) custom-call(bf16[32,4096]{1,0:T(8,128)(2,1)} %images_hbm.1, s32[2,512]{1,0:T(2,128)} %bitcast.4, ...), custom_call_target="tpu_custom_call" | custom-call | tf_op jit(solution)/shard_map/pallas_call | solution.py:367
  8.2 0.0 copy-done
  8.2 0.1 collective-permute-start.3
  8.2 1.6 %shard_map.69 = (bf16[16,128,256]{2,1,0:T(8,128)(2,1)S(1)}, bf16[128,4096]{1,0:T(8,128)(2,1)S(1)}, f32[8,128]{1,0:T(8,128)S(1)}) custom-call(bf16[32,4096]{1,0:T(8,128)(2,1)S(1)} %get-tuple-element.45.refs_0_, f32[128,2048]{1,0:T(8,128)S(1)} %get-tuple-element.46.refs_1_.refs_2_, f32[128,2048]{1,0:T(8,128)S(1)} %get-tuple-element.47.refs_2_.refs_3_, ...), custom_call_target="tpu_custom_call" | custom-call | tf_op jit(solution)/shard_map/pallas_call | solution.py:367
  9.8 1.9 %collective-permute-done.refs_0_ = bf16[32,4096]{1,0:T(8,128)(2,1)S(1)} collective-permute-done((bf16[32,4096]{1,0:T(8,128)(2,1)}, bf16[32,4096]{1,0:T(8,128)(2,1)S(1)}, u32[]{:S(2)}, u32[]{:S(2)}) %collective-permute-start) | collective-permute-done | bytes 262176 | tf_op jit(solution)/shard_map/ppermute | solution.py:421
  11.8 1.3 %collective-permute-start.1 = (bf16[32,4096]{1,0:T(8,128)(2,1)S(1)}, bf16[32,4096]{1,0:T(8,128)(2,1)S(1)}, u32[]{:S(2)}, u32[]{:S(2)}) collective-permute-start(bf16[32,4096]{1,0:T(8,128)(2,1)S(1)} %collective-permute-done.refs_0_), channel_id=1, source_target_pairs={{8,12},{4,0},{9,13},{5,1},{10,14},{6,2},{11,15},{7,3},{24,28},{20,... | collective-permute-start | bytes 786440 | tf_op jit(solution)/shard_map/ppermute | solution.py:490
  13.1 0.7 %collective-permute-start.2 = (bf16[32,4096]{1,0:T(8,128)(2,1)S(1)}, bf16[32,4096]{1,0:T(8,128)(2,1)S(1)}, u32[]{:S(2)}, u32[]{:S(2)}) collective-permute-start(bf16[32,4096]{1,0:T(8,128)(2,1)S(1)} %copy-done), channel_id=1, source_target_pairs={{4,8},{8,4},{0,0},{12,12},{5,9},{9,5},{1,1},{13,13},{6,10},{10,6},... | collective-permute-start | bytes 786440 | tf_op jit(solution)/shard_map/ppermute | solution.py:491
  13.7 2.0 %shard_map.70 = (bf16[2048,512]{1,0:T(8,128)(2,1)S(1)}, f32[8,256]{1,0:T(8,128)S(1)}, bf16[128,256]{1,0:T(8,128)(2,1)S(1)}) custom-call(s32[1,8,256,256]{3,2,1,0:T(8,128)} %interp_hbm, s32[64,128]{1,0:T(8,128)} %bitcast.3), custom_call_target="tpu_custom_call" | custom-call | tf_op jit(solution)/shard_map/pallas_call | solution.py:367
  15.7 1.6 %shard_map.71 = (bf16[16,128,256]{2,1,0:T(8,128)(2,1)S(1)}, bf16[128,4096]{1,0:T(8,128)(2,1)S(1)}, f32[8,128]{1,0:T(8,128)S(1)}) custom-call(bf16[32,4096]{1,0:T(8,128)(2,1)S(1)} %collective-permute-done.refs_0_, f32[128,2048]{1,0:T(8,128)S(1)} %get-tuple-element.46.refs_1_.refs_2_, ...), custom_call_target="tpu_custom_call", output_to_operand_aliasing={{0}: (7, {}), {1}: (8, {}), {2}: (9, {})} | custom-call | tf_op jit(solution)/shard_map/pallas_call | solution.py:367
  17.3 0.7 %collective-permute-done.3.refs_0_ = bf16[32,4096]{1,0:T(8,128)(2,1)S(1)} collective-permute-done((bf16[32,4096]{1,0:T(8,128)(2,1)S(1)}, bf16[32,4096]{1,0:T(8,128)(2,1)S(1)}, u32[]{:S(2)}, u32[]{:S(2)}) %collective-permute-start.3) | collective-permute-done | bytes 262176 | tf_op jit(solution)/shard_map/ppermute | solution.py:469
  18.1 1.6 %shard_map.72 = (bf16[16,128,256]{2,1,0:T(8,128)(2,1)S(1)}, bf16[128,4096]{1,0:T(8,128)(2,1)S(1)}, f32[8,128]{1,0:T(8,128)S(1)}) custom-call(bf16[32,4096]{1,0:T(8,128)(2,1)S(1)} %collective-permute-done.3.refs_0_, f32[128,2048]{1,0:T(8,128)S(1)} %get-tuple-element.46.refs_1_.refs_2_, ...), custom_call_target="tpu_custom_call", output_to_operand_aliasing={{0}: (7, {}), {1}: (8, {}), {2}: (9, {})} | custom-call | tf_op jit(solution)/shard_map/pallas_call | solution.py:367
  19.6 3.9 %collective-permute-done.1.refs_0_ = bf16[32,4096]{1,0:T(8,128)(2,1)S(1)} collective-permute-done((bf16[32,4096]{1,0:T(8,128)(2,1)S(1)}, bf16[32,4096]{1,0:T(8,128)(2,1)S(1)}, u32[]{:S(2)}, u32[]{:S(2)}) %collective-permute-start.1) | collective-permute-done | bytes 262176 | tf_op jit(solution)/shard_map/ppermute | solution.py:490
  23.6 0.0 collective-permute-done.2.refs_1_
  23.6 1.6 %shard_map.73 = (bf16[16,128,256]{2,1,0:T(8,128)(2,1)S(1)}, bf16[128,4096]{1,0:T(8,128)(2,1)S(1)}, f32[8,128]{1,0:T(8,128)S(1)}) custom-call(bf16[32,4096]{1,0:T(8,128)(2,1)S(1)} %collective-permute-done.1.refs_0_, bf16[32,4096]{1,0:T(8,128)(2,1)S(1)} %collective-permute-done.2.refs_1_, ...), custom_call_target="tpu_custom_call", output_to_operand_aliasing={{0}: (8, {}), {1}: (9, {}), {2}: (10, {})} | custom-call | tf_op jit(solution)/shard_map/pallas_call | solution.py:367
  25.2 2.5 %collective-permute-start.4 = (f32[8,128]{1,0:T(8,128)S(1)}, f32[8,128]{1,0:T(8,128)S(1)}, u32[]{:S(2)}, u32[]{:S(2)}) collective-permute-start(f32[8,128]{1,0:T(8,128)S(1)} %get-tuple-element.73.rest_0_), channel_id=1, source_target_pairs={{0,12},{4,8},{8,4},{12,0},{1,13},{5,9},{9,5},{13,1},{2,14},{6,10},... | collective-permute-start | bytes 12296 | tf_op jit(solution)/shard_map/ppermute | solution.py:384
  27.7 0.0 collective-permute-start.5
  27.7 1.9 %collective-permute-start.6 = (f32[8,128]{1,0:T(8,128)S(1)}, f32[8,128]{1,0:T(8,128)S(1)}, u32[]{:S(2)}, u32[]{:S(2)}) collective-permute-start(f32[8,128]{1,0:T(8,128)S(1)} %get-tuple-element.73.rest_0_), channel_id=1, source_target_pairs={{0,4},{4,0},{8,12},{12,8},{1,5},{5,1},{9,13},{13,9},{2,6},{6,2},{1... | collective-permute-start | bytes 12296 | tf_op jit(solution)/shard_map/ppermute | solution.py:384
  29.6 0.4 shard_map.74.share_ref
  30.0 0.6 %collective-permute-done.4.rest_1_ = f32[8,128]{1,0:T(8,128)S(1)} collective-permute-done((f32[8,128]{1,0:T(8,128)S(1)}, f32[8,128]{1,0:T(8,128)S(1)}, u32[]{:S(2)}, u32[]{:S(2)}) %collective-permute-start.4) | collective-permute-done | bytes 4128 | tf_op jit(solution)/shard_map/ppermute | solution.py:384
  30.6 1.6 %collective-permute-done.5.rest_2_ = f32[8,128]{1,0:T(8,128)S(1)} collective-permute-done((f32[8,128]{1,0:T(8,128)S(1)}, f32[8,128]{1,0:T(8,128)S(1)}, u32[]{:S(2)}, u32[]{:S(2)}) %collective-permute-start.5) | collective-permute-done | bytes 4128 | tf_op jit(solution)/shard_map/ppermute | solution.py:384
  32.2 0.0 collective-permute-done.6.rest_3_
  32.2 0.9 %shard_map.75 = (bf16[4,2,2176]{2,1,0:T(2,128)(2,1)S(1)}, bf16[4,2,2176]{2,1,0:T(2,128)(2,1)S(1)}, bf16[4,2,2176]{2,1,0:T(2,128)(2,1)S(1)}, bf16[4,2,2176]{2,1,0:T(2,128)(2,1)S(1)}) custom-call(f32[16,128,128]{2,1,0:T(8,128)S(1)} %shard_map.74.share_ref, bf16[128,4096]{1,0:T(8,128)(2,1)S(1)} %get-tuple-element.72.based_ref, ...), custom_call_target="tpu_custom_call" | custom-call | tf_op jit(solution)/shard_map/pallas_call | solution.py:367
  33.1 0.1 collective-permute-start.7
  33.2 1.6 %collective-permute-start.8 = (bf16[4,2,2176]{2,1,0:T(2,128)(2,1)S(1)}, bf16[4,2,2176]{2,1,0:T(2,128)(2,1)S(1)}, u32[]{:S(2)}, u32[]{:S(2)}) collective-permute-start(bf16[4,2,2176]{2,1,0:T(2,128)(2,1)S(1)} %get-tuple-element.76), channel_id=1, source_target_pairs={{0,2},{1,3},{2,0},{3,1},{4,6},{5,7},{6,4},{7,5},{8,10},{9,11},{10,... | collective-permute-start | bytes 104456 | tf_op jit(solution)/shard_map/ppermute | solution.py:517
  34.8 0.3 collective-permute-start.9
  35.0 0.0 collective-permute-done.7.refs_1_
  35.0 2.1 %collective-permute-done.8.refs_2_ = bf16[4,2,2176]{2,1,0:T(2,128)(2,1)S(1)} collective-permute-done((bf16[4,2,2176]{2,1,0:T(2,128)(2,1)S(1)}, bf16[4,2,2176]{2,1,0:T(2,128)(2,1)S(1)}, u32[]{:S(2)}, u32[]{:S(2)}) %collective-permute-start.8) | collective-permute-done | bytes 34848 | tf_op jit(solution)/shard_map/ppermute | solution.py:517
  37.2 1.0 %collective-permute-done.9.refs_3_ = bf16[4,2,2176]{2,1,0:T(2,128)(2,1)S(1)} collective-permute-done((bf16[4,2,2176]{2,1,0:T(2,128)(2,1)S(1)}, bf16[4,2,2176]{2,1,0:T(2,128)(2,1)S(1)}, u32[]{:S(2)}, u32[]{:S(2)}) %collective-permute-start.9) | collective-permute-done | bytes 34848 | tf_op jit(solution)/shard_map/ppermute | solution.py:517
  38.2 0.1 shard_map.76
  38.2 1.5 %collective-permute-start.10 = (bf16[2,2176]{1,0:T(2,128)(2,1)S(1)}, bf16[2,2176]{1,0:T(2,128)(2,1)S(1)}, u32[]{:S(2)}, u32[]{:S(2)}) collective-permute-start(bf16[2,2176]{1,0:T(2,128)(2,1)S(1)} %get-tuple-element.79), channel_id=1, source_target_pairs={{0,12},{4,8},{8,4},{12,0},{1,13},{5,9},{9,5},{13,1},{2,14},{6,10},... | collective-permute-start | bytes 26120 | tf_op jit(solution)/shard_map/ppermute | solution.py:384
  39.7 1.0 %collective-permute-start.11 = (bf16[2,2176]{1,0:T(2,128)(2,1)S(1)}, bf16[2,2176]{1,0:T(2,128)(2,1)S(1)}, u32[]{:S(2)}, u32[]{:S(2)}) collective-permute-start(bf16[2,2176]{1,0:T(2,128)(2,1)S(1)} %get-tuple-element.80), channel_id=1, source_target_pairs={{0,8},{4,12},{8,0},{12,4},{1,9},{5,13},{9,1},{13,5},{2,10},{6,14},... | collective-permute-start | bytes 26120 | tf_op jit(solution)/shard_map/ppermute | solution.py:384
  40.7 1.9 %collective-permute-start.12 = (bf16[2,2176]{1,0:T(2,128)(2,1)S(1)}, bf16[2,2176]{1,0:T(2,128)(2,1)S(1)}, u32[]{:S(2)}, u32[]{:S(2)}) collective-permute-start(bf16[2,2176]{1,0:T(2,128)(2,1)S(1)} %get-tuple-element.81), channel_id=1, source_target_pairs={{0,4},{4,0},{8,12},{12,8},{1,5},{5,1},{9,13},{13,9},{2,6},{6,2},{1... | collective-permute-start | bytes 26120 | tf_op jit(solution)/shard_map/ppermute | solution.py:384
  42.7 1.1 %collective-permute-done.10.refs_1_ = bf16[2,2176]{1,0:T(2,128)(2,1)S(1)} collective-permute-done((bf16[2,2176]{1,0:T(2,128)(2,1)S(1)}, bf16[2,2176]{1,0:T(2,128)(2,1)S(1)}, u32[]{:S(2)}, u32[]{:S(2)}) %collective-permute-start.10) | collective-permute-done | bytes 8736 | tf_op jit(solution)/shard_map/ppermute | solution.py:384
  43.8 0.5 %collective-permute-done.11.refs_2_ = bf16[2,2176]{1,0:T(2,128)(2,1)S(1)} collective-permute-done((bf16[2,2176]{1,0:T(2,128)(2,1)S(1)}, bf16[2,2176]{1,0:T(2,128)(2,1)S(1)}, u32[]{:S(2)}, u32[]{:S(2)}) %collective-permute-start.11) | collective-permute-done | bytes 8736 | tf_op jit(solution)/shard_map/ppermute | solution.py:384
  44.3 0.1 collective-permute-done.12.refs_3_
  44.4 1.0 %shard_map.77 = (f32[1,2,256]{2,1,0:T(2,128)}, f32[1,1,256]{2,1,0:T(1,128)}) custom-call(bf16[2,2176]{1,0:T(2,128)(2,1)S(1)} %get-tuple-element.78.refs_0_, bf16[2,2176]{1,0:T(2,128)(2,1)S(1)} %collective-permute-done.10.refs_1_, bf16[2,2176]{1,0:T(2,128)(2,1)S(1)} %collective-permute-done.11.refs_2_, bf16[2,2176]{1,0:T(2,128)(2,1)S(1)} %collective-permute-done.12.refs_3_, ...), custom_call_target="tpu_custom_call" | custom-call | tf_op jit(solution)/shard_map/pallas_call | solution.py:367
Async XLA Ops:
  0.6 7.5 %copy-start = (bf16[32,4096]{1,0:T(8,128)(2,1)S(1)}, bf16[32,4096]{1,0:T(8,128)(2,1)}, u32[]{:S(2)}) copy-start(bf16[32,4096]{1,0:T(8,128)(2,1)} %images_hbm.1) | copy-start | bytes 786436
  0.6 11.1 %collective-permute-start = (bf16[32,4096]{1,0:T(8,128)(2,1)}, bf16[32,4096]{1,0:T(8,128)(2,1)S(1)}, u32[]{:S(2)}, u32[]{:S(2)}) collective-permute-start(bf16[32,4096]{1,0:T(8,128)(2,1)} %images_hbm.1), channel_id=1, source_target_pairs={{0,8},{12,4},{8,12},{4,0},{1,9},{13,5},{9,13},{5,1},{2,10},{14,6},... | collective-permute-start | bytes 786440 | tf_op jit(solution)/shard_map/ppermute | solution.py:421
  8.2 9.9 %collective-permute-start.3 = (bf16[32,4096]{1,0:T(8,128)(2,1)S(1)}, bf16[32,4096]{1,0:T(8,128)(2,1)S(1)}, u32[]{:S(2)}, u32[]{:S(2)}) collective-permute-start(bf16[32,4096]{1,0:T(8,128)(2,1)S(1)} %copy-done), channel_id=1, source_target_pairs={{0,4},{12,8},{4,12},{8,0},{1,5},{13,9},{5,13},{9,1},{2,6},{14,10},... | collective-permute-start | bytes 786440 | tf_op jit(solution)/shard_map/ppermute | solution.py:469
  11.8 11.8 %collective-permute-start.1 = (bf16[32,4096]{1,0:T(8,128)(2,1)S(1)}, bf16[32,4096]{1,0:T(8,128)(2,1)S(1)}, u32[]{:S(2)}, u32[]{:S(2)}) collective-permute-start(bf16[32,4096]{1,0:T(8,128)(2,1)S(1)} %collective-permute-done.refs_0_), channel_id=1, source_target_pairs={{8,12},{4,0},{9,13},{5,1},{10,14},{6,2},{11,15},{7,3},{24,28},{20,... | collective-permute-start | bytes 786440 | tf_op jit(solution)/shard_map/ppermute | solution.py:490
  13.1 10.5 %collective-permute-start.2 = (bf16[32,4096]{1,0:T(8,128)(2,1)S(1)}, bf16[32,4096]{1,0:T(8,128)(2,1)S(1)}, u32[]{:S(2)}, u32[]{:S(2)}) collective-permute-start(bf16[32,4096]{1,0:T(8,128)(2,1)S(1)} %copy-done), channel_id=1, source_target_pairs={{4,8},{8,4},{0,0},{12,12},{5,9},{9,5},{1,1},{13,13},{6,10},{10,6},... | collective-permute-start | bytes 786440 | tf_op jit(solution)/shard_map/ppermute | solution.py:491
  25.2 5.4 %collective-permute-start.4 = (f32[8,128]{1,0:T(8,128)S(1)}, f32[8,128]{1,0:T(8,128)S(1)}, u32[]{:S(2)}, u32[]{:S(2)}) collective-permute-start(f32[8,128]{1,0:T(8,128)S(1)} %get-tuple-element.73.rest_0_), channel_id=1, source_target_pairs={{0,12},{4,8},{8,4},{12,0},{1,13},{5,9},{9,5},{13,1},{2,14},{6,10},... | collective-permute-start | bytes 12296 | tf_op jit(solution)/shard_map/ppermute | solution.py:384
  27.7 4.5 %collective-permute-start.5 = (f32[8,128]{1,0:T(8,128)S(1)}, f32[8,128]{1,0:T(8,128)S(1)}, u32[]{:S(2)}, u32[]{:S(2)}) collective-permute-start(f32[8,128]{1,0:T(8,128)S(1)} %get-tuple-element.73.rest_0_), channel_id=1, source_target_pairs={{0,8},{4,12},{8,0},{12,4},{1,9},{5,13},{9,1},{13,5},{2,10},{6,14},... | collective-permute-start | bytes 12296 | tf_op jit(solution)/shard_map/ppermute | solution.py:384
  27.7 4.5 %collective-permute-start.6 = (f32[8,128]{1,0:T(8,128)S(1)}, f32[8,128]{1,0:T(8,128)S(1)}, u32[]{:S(2)}, u32[]{:S(2)}) collective-permute-start(f32[8,128]{1,0:T(8,128)S(1)} %get-tuple-element.73.rest_0_), channel_id=1, source_target_pairs={{0,4},{4,0},{8,12},{12,8},{1,5},{5,1},{9,13},{13,9},{2,6},{6,2},{1... | collective-permute-start | bytes 12296 | tf_op jit(solution)/shard_map/ppermute | solution.py:384
  33.1 1.9 %collective-permute-start.7 = (bf16[4,2,2176]{2,1,0:T(2,128)(2,1)S(1)}, bf16[4,2,2176]{2,1,0:T(2,128)(2,1)S(1)}, u32[]{:S(2)}, u32[]{:S(2)}) collective-permute-start(bf16[4,2,2176]{2,1,0:T(2,128)(2,1)S(1)} %get-tuple-element.75), channel_id=1, source_target_pairs={{0,1},{1,0},{2,3},{3,2},{4,5},{5,4},{6,7},{7,6},{8,9},{9,8},{10,11... | collective-permute-start | bytes 104456 | tf_op jit(solution)/shard_map/ppermute | solution.py:517
  33.2 4.0 %collective-permute-start.8 = (bf16[4,2,2176]{2,1,0:T(2,128)(2,1)S(1)}, bf16[4,2,2176]{2,1,0:T(2,128)(2,1)S(1)}, u32[]{:S(2)}, u32[]{:S(2)}) collective-permute-start(bf16[4,2,2176]{2,1,0:T(2,128)(2,1)S(1)} %get-tuple-element.76), channel_id=1, source_target_pairs={{0,2},{1,3},{2,0},{3,1},{4,6},{5,7},{6,4},{7,5},{8,10},{9,11},{10,... | collective-permute-start | bytes 104456 | tf_op jit(solution)/shard_map/ppermute | solution.py:517
  34.8 3.4 %collective-permute-start.9 = (bf16[4,2,2176]{2,1,0:T(2,128)(2,1)S(1)}, bf16[4,2,2176]{2,1,0:T(2,128)(2,1)S(1)}, u32[]{:S(2)}, u32[]{:S(2)}) collective-permute-start(bf16[4,2,2176]{2,1,0:T(2,128)(2,1)S(1)} %get-tuple-element.77), channel_id=1, source_target_pairs={{0,3},{1,2},{2,1},{3,0},{4,7},{5,6},{6,5},{7,4},{8,11},{9,10},{10,... | collective-permute-start | bytes 104456 | tf_op jit(solution)/shard_map/ppermute | solution.py:517
  38.2 5.6 %collective-permute-start.10 = (bf16[2,2176]{1,0:T(2,128)(2,1)S(1)}, bf16[2,2176]{1,0:T(2,128)(2,1)S(1)}, u32[]{:S(2)}, u32[]{:S(2)}) collective-permute-start(bf16[2,2176]{1,0:T(2,128)(2,1)S(1)} %get-tuple-element.79), channel_id=1, source_target_pairs={{0,12},{4,8},{8,4},{12,0},{1,13},{5,9},{9,5},{13,1},{2,14},{6,10},... | collective-permute-start | bytes 26120 | tf_op jit(solution)/shard_map/ppermute | solution.py:384
  39.7 4.6 %collective-permute-start.11 = (bf16[2,2176]{1,0:T(2,128)(2,1)S(1)}, bf16[2,2176]{1,0:T(2,128)(2,1)S(1)}, u32[]{:S(2)}, u32[]{:S(2)}) collective-permute-start(bf16[2,2176]{1,0:T(2,128)(2,1)S(1)} %get-tuple-element.80), channel_id=1, source_target_pairs={{0,8},{4,12},{8,0},{12,4},{1,9},{5,13},{9,1},{13,5},{2,10},{6,14},... | collective-permute-start | bytes 26120 | tf_op jit(solution)/shard_map/ppermute | solution.py:384
  40.7 3.7 %collective-permute-start.12 = (bf16[2,2176]{1,0:T(2,128)(2,1)S(1)}, bf16[2,2176]{1,0:T(2,128)(2,1)S(1)}, u32[]{:S(2)}, u32[]{:S(2)}) collective-permute-start(bf16[2,2176]{1,0:T(2,128)(2,1)S(1)} %get-tuple-element.81), channel_id=1, source_target_pairs={{0,4},{4,0},{8,12},{12,8},{1,5},{5,1},{9,13},{13,9},{2,6},{6,2},{1... | collective-permute-start | bytes 26120 | tf_op jit(solution)/shard_map/ppermute | solution.py:384

commit v9 on v8

--- a/solution.py
+++ b/solution.py
@@ -306,14 +306,23 @@
     if len(out_refs) == 1:
         out_refs[0][...] = sums_ref[...].astype(jnp.bfloat16)
         return
-    near = 2 * lax.axis_index("img") + lax.axis_index("brick")
+    core = lax.axis_index("brick")
     for m, ref in enumerate(out_refs):
         for z in range(ref.shape[0]):
-            ref[z] = sums_ref[z * len(out_refs) + jnp.bitwise_xor(near, m)].astype(jnp.bfloat16)
+            ref[z] = sums_ref[2 * z + jnp.bitwise_xor(core, m)].astype(jnp.bfloat16)
+
+
+def core_kernel(own_ref, other_ref, *out_refs):
+    side = lax.axis_index("img")
+    for m, ref in enumerate(out_refs):
+        for z in range(ref.shape[0]):
+            at = 2 * z + jnp.bitwise_xor(side, m)
+            total = own_ref[at].astype(jnp.float32) + other_ref[at].astype(jnp.float32)
+            ref[z] = total.astype(jnp.bfloat16)
 
 
 def plane_kernel(*refs):
-    in_refs, out_refs = refs[: len(refs) // 2], refs[len(refs) // 2 :]
+    in_refs, out_refs = refs[:2], refs[2:]
     plane = lax.axis_index("orient")
     for m, ref in enumerate(out_refs):
         target = jnp.bitwise_xor(plane, m)
@@ -416,7 +425,7 @@
     f32, bf16 = jnp.float32, jnp.bfloat16
     tiles = 2 * K // LANES
     relay = orient_count == 4
-    staged = relay and group_count == 4
+    staged = relay and lax.axis_size("img") == lax.axis_size("brick") == 2
     if relay:
         first = lax.ppermute(images, "orient", [(0, 2), (3, 1), (2, 3), (1, 0)])
     else:
@@ -499,11 +508,13 @@
     terms, based, stats = state
     gathered = everyone(stats)
     shares = call(
-        share_kernel, jax.ShapeDtypeStruct((SHIFTS, NSEG * bricks, count), f32), on_chip(terms, hit)
+        share_kernel,
+        jax.ShapeDtypeStruct((SHIFTS, NSEG * bricks, count), f32),
+        on_chip(terms, hit),
     )
     outgoing = call(
         functools.partial(brick_kernel, orient_count),
-        [jax.ShapeDtypeStruct((bricks // 4, 2, K + LANES), bf16)] * 4
+        [jax.ShapeDtypeStruct((bricks // 2, 2, K + LANES), bf16)] * 2
         if staged
         else jax.ShapeDtypeStruct((bricks, 2, K + LANES), bf16),
         on_chip(shares, based, cos_table, sin_table, *gathered),
@@ -513,11 +524,17 @@
         ],
     )
     if staged:
-        parts = [outgoing[0]] + [
-            lax.ppermute(outgoing[m], ("img", "brick"), [(i, i ^ m) for i in range(4)])
-            for m in (1, 2, 3)
-        ]
-        sums = call(plane_kernel, [jax.ShapeDtypeStruct((2, K + LANES), bf16)] * 4, on_chip(*parts))
+        halves = call(
+            core_kernel,
+            [jax.ShapeDtypeStruct((bricks // 4, 2, K + LANES), bf16)] * 2,
+            on_chip(outgoing[0], lax.ppermute(outgoing[1], "brick", [(0, 1), (1, 0)])),
+        )
+        parts = [halves[0], lax.ppermute(halves[1], "img", [(0, 1), (1, 0)])]
+        sums = call(
+            plane_kernel,
+            [jax.ShapeDtypeStruct((2, K + LANES), bf16)] * 4,
+            on_chip(*parts),
+        )
         received = [sums[0]] + [swap(sums[m], m) for m in (3, 2, 1)]
     else:
         received = [

time: 45.6 us -> 47.3 us (1.037)
  waiting for transfers between devices: 13.6 us -> 15.6 us
    ppermute x6, waiting for transfers between devices: 3.89 us -> 5.25 us  [swap(): lax.ppermute(array, 'orient', [(i, i ^ amount) for i in range(count)])]
    ppermute x3 -> x2, waiting for transfers between devices: 3.11 us -> 3.69 us  [the longest x1 2.44 us: per_device(): parts = [halves[0], lax.ppermute(halves[1], 'img', [(0, 1), (1, 0)])]]
    ppermute x3 -> x2, starting transfers between devices: 1.92 us -> 1.63 us  [the longest x1 1.56 us: per_device(): parts = [halves[0], lax.ppermute(halves[1], 'img', [(0, 1), (1, 0)])]]
    pallas_call x10 -> x11, Pallas kernels: 14.1 us -> 14.2 us  [call(): pl.pallas_call(kernel, in_specs=[in_spec] * len(inputs), out_specs=[spec]...]
  transfers between devices with their start and end apart: 13 -> 12, of which waited for: 10 -> 10; matrix products, arithmetic and copies ran while one was open for 0% -> 0% of each run, Pallas kernels for 23% -> 22%
where the time goes in v9:
time: 47.3 us; the launch traced here: 47.1 us
  starting transfers between devices  16.6 us (35%)
  waiting for transfers between devices  15.6 us (33%)
  Pallas kernels  14.2 us (30%)
  between operations  0.72 us (2%)
    pallas_call x11, Pallas kernels, call(): pl.pallas_call(kernel, in_specs=[in_spec] * len(inputs), out_specs=[spec]...  14.2 us
    ppermute x6, starting transfers between devices, swap(): lax.ppermute(array, 'orient', [(i, i ^ amount) for i in range(count)])  8.87 us
    ppermute x6, waiting for transfers between devices, swap(): lax.ppermute(array, 'orient', [(i, i ^ amount) for i in range(count)])  5.25 us
    ppermute x1, starting transfers between devices, per_device(): first = lax.ppermute(images, 'orient', [(0, 2), (3, 1), (2, 3), (1, 0)])  4.12 us
    ppermute x1, waiting for transfers between devices, per_device(): relayed = lax.ppermute(first, 'orient', [(2, 3), (1, 0)])  3.93 us
    ppermute x1, waiting for transfers between devices, per_device(): parts = [halves[0], lax.ppermute(halves[1], 'img', [(0, 1), (1, 0)])]  2.44 us
    ppermute x1, waiting for transfers between devices, per_device(): first = lax.ppermute(images, 'orient', [(0, 2), (3, 1), (2, 3), (1, 0)])  1.94 us
    ppermute x1, starting transfers between devices, per_device(): parts = [halves[0], lax.ppermute(halves[1], 'img', [(0, 1), (1, 0)])]  1.56 us
  transfers between devices with their start and end apart: 12, of which 10 were waited for; matrix products, arithmetic and copies ran while one was open for 0% of the time, Pallas kernels for 22%

profile of v9, /device:TPU:0, one launch (start us, length us, event | category | flops | bytes accessed | tf_op | source)
XLA Modules:
  0.0 47.1 jit_solution(462990065549512647)
XLA Ops:
  0.6 0.0 copy-start
  0.6 4.1 %collective-permute-start = (bf16[32,4096]{1,0:T(8,128)(2,1)}, bf16[32,4096]{1,0:T(8,128)(2,1)S(1)}, u32[]{:S(2)}, u32[]{:S(2)}) collective-permute-start(bf16[32,4096]{1,0:T(8,128)(2,1)} %images_hbm.1), channel_id=1, source_target_pairs={{0,8},{12,4},{8,12},{4,0},{1,9},{13,5},{9,13},{5,1},{2,10},{14,6},... | collective-permute-start | bytes 786440 | tf_op jit(solution)/shard_map/ppermute | solution.py:430
  4.8 3.4 %shard_map.68 = (f32[8,2048]{1,0:T(8,128)S(1)}, f32[8,2048]{1,0:T(8,128)S(1)}, bf16[32,4096]{1,0:T(8,128)(2,1)S(1)}, f32[128,2048]{1,0:T(8,128)S(1)}, f32[128,20...) custom-call(bf16[32,4096]{1,0:T(8,128)(2,1)} %images_hbm.1, s32[2,512]{1,0:T(2,128)} %bitcast.4, ...), custom_call_target="tpu_custom_call" | custom-call | tf_op jit(solution)/shard_map/pallas_call | solution.py:376
  8.2 0.0 copy-done
  8.2 0.1 collective-permute-start.3
  8.2 1.6 %shard_map.69 = (bf16[16,128,256]{2,1,0:T(8,128)(2,1)S(1)}, bf16[128,4096]{1,0:T(8,128)(2,1)S(1)}, f32[8,128]{1,0:T(8,128)S(1)}) custom-call(bf16[32,4096]{1,0:T(8,128)(2,1)S(1)} %get-tuple-element.45.refs_0_, f32[128,2048]{1,0:T(8,128)S(1)} %get-tuple-element.46.refs_1_.refs_2_, f32[128,2048]{1,0:T(8,128)S(1)} %get-tuple-element.47.refs_2_.refs_3_, ...), custom_call_target="tpu_custom_call" | custom-call | tf_op jit(solution)/shard_map/pallas_call | solution.py:376
  9.8 1.9 %collective-permute-done.refs_0_ = bf16[32,4096]{1,0:T(8,128)(2,1)S(1)} collective-permute-done((bf16[32,4096]{1,0:T(8,128)(2,1)}, bf16[32,4096]{1,0:T(8,128)(2,1)S(1)}, u32[]{:S(2)}, u32[]{:S(2)}) %collective-permute-start) | collective-permute-done | bytes 262176 | tf_op jit(solution)/shard_map/ppermute | solution.py:430
  11.8 1.3 %collective-permute-start.1 = (bf16[32,4096]{1,0:T(8,128)(2,1)S(1)}, bf16[32,4096]{1,0:T(8,128)(2,1)S(1)}, u32[]{:S(2)}, u32[]{:S(2)}) collective-permute-start(bf16[32,4096]{1,0:T(8,128)(2,1)S(1)} %collective-permute-done.refs_0_), channel_id=1, source_target_pairs={{8,12},{4,0},{9,13},{5,1},{10,14},{6,2},{11,15},{7,3},{24,28},{20,... | collective-permute-start | bytes 786440 | tf_op jit(solution)/shard_map/ppermute | solution.py:499
  13.1 0.7 %collective-permute-start.2 = (bf16[32,4096]{1,0:T(8,128)(2,1)S(1)}, bf16[32,4096]{1,0:T(8,128)(2,1)S(1)}, u32[]{:S(2)}, u32[]{:S(2)}) collective-permute-start(bf16[32,4096]{1,0:T(8,128)(2,1)S(1)} %copy-done), channel_id=1, source_target_pairs={{4,8},{8,4},{0,0},{12,12},{5,9},{9,5},{1,1},{13,13},{6,10},{10,6},... | collective-permute-start | bytes 786440 | tf_op jit(solution)/shard_map/ppermute | solution.py:500
  13.7 2.0 %shard_map.70 = (bf16[2048,512]{1,0:T(8,128)(2,1)S(1)}, f32[8,256]{1,0:T(8,128)S(1)}, bf16[128,256]{1,0:T(8,128)(2,1)S(1)}) custom-call(s32[1,8,256,256]{3,2,1,0:T(8,128)} %interp_hbm, s32[64,128]{1,0:T(8,128)} %bitcast.3), custom_call_target="tpu_custom_call" | custom-call | tf_op jit(solution)/shard_map/pallas_call | solution.py:376
  15.7 1.6 %shard_map.71 = (bf16[16,128,256]{2,1,0:T(8,128)(2,1)S(1)}, bf16[128,4096]{1,0:T(8,128)(2,1)S(1)}, f32[8,128]{1,0:T(8,128)S(1)}) custom-call(bf16[32,4096]{1,0:T(8,128)(2,1)S(1)} %collective-permute-done.refs_0_, f32[128,2048]{1,0:T(8,128)S(1)} %get-tuple-element.46.refs_1_.refs_2_, ...), custom_call_target="tpu_custom_call", output_to_operand_aliasing={{0}: (7, {}), {1}: (8, {}), {2}: (9, {})} | custom-call | tf_op jit(solution)/shard_map/pallas_call | solution.py:376
  17.3 0.7 %collective-permute-done.3.refs_0_ = bf16[32,4096]{1,0:T(8,128)(2,1)S(1)} collective-permute-done((bf16[32,4096]{1,0:T(8,128)(2,1)S(1)}, bf16[32,4096]{1,0:T(8,128)(2,1)S(1)}, u32[]{:S(2)}, u32[]{:S(2)}) %collective-permute-start.3) | collective-permute-done | bytes 262176 | tf_op jit(solution)/shard_map/ppermute | solution.py:478
  18.1 1.6 %shard_map.72 = (bf16[16,128,256]{2,1,0:T(8,128)(2,1)S(1)}, bf16[128,4096]{1,0:T(8,128)(2,1)S(1)}, f32[8,128]{1,0:T(8,128)S(1)}) custom-call(bf16[32,4096]{1,0:T(8,128)(2,1)S(1)} %collective-permute-done.3.refs_0_, f32[128,2048]{1,0:T(8,128)S(1)} %get-tuple-element.46.refs_1_.refs_2_, ...), custom_call_target="tpu_custom_call", output_to_operand_aliasing={{0}: (7, {}), {1}: (8, {}), {2}: (9, {})} | custom-call | tf_op jit(solution)/shard_map/pallas_call | solution.py:376
  19.6 3.9 %collective-permute-done.1.refs_0_ = bf16[32,4096]{1,0:T(8,128)(2,1)S(1)} collective-permute-done((bf16[32,4096]{1,0:T(8,128)(2,1)S(1)}, bf16[32,4096]{1,0:T(8,128)(2,1)S(1)}, u32[]{:S(2)}, u32[]{:S(2)}) %collective-permute-start.1) | collective-permute-done | bytes 262176 | tf_op jit(solution)/shard_map/ppermute | solution.py:499
  23.6 0.0 collective-permute-done.2.refs_1_
  23.6 1.6 %shard_map.73 = (bf16[16,128,256]{2,1,0:T(8,128)(2,1)S(1)}, bf16[128,4096]{1,0:T(8,128)(2,1)S(1)}, f32[8,128]{1,0:T(8,128)S(1)}) custom-call(bf16[32,4096]{1,0:T(8,128)(2,1)S(1)} %collective-permute-done.1.refs_0_, bf16[32,4096]{1,0:T(8,128)(2,1)S(1)} %collective-permute-done.2.refs_1_, ...), custom_call_target="tpu_custom_call", output_to_operand_aliasing={{0}: (8, {}), {1}: (9, {}), {2}: (10, {})} | custom-call | tf_op jit(solution)/shard_map/pallas_call | solution.py:376
  25.2 2.5 %collective-permute-start.4 = (f32[8,128]{1,0:T(8,128)S(1)}, f32[8,128]{1,0:T(8,128)S(1)}, u32[]{:S(2)}, u32[]{:S(2)}) collective-permute-start(f32[8,128]{1,0:T(8,128)S(1)} %get-tuple-element.73.rest_0_), channel_id=1, source_target_pairs={{0,12},{4,8},{8,4},{12,0},{1,13},{5,9},{9,5},{13,1},{2,14},{6,10},... | collective-permute-start | bytes 12296 | tf_op jit(solution)/shard_map/ppermute | solution.py:393
  27.7 0.0 collective-permute-start.5
  27.7 1.9 %collective-permute-start.6 = (f32[8,128]{1,0:T(8,128)S(1)}, f32[8,128]{1,0:T(8,128)S(1)}, u32[]{:S(2)}, u32[]{:S(2)}) collective-permute-start(f32[8,128]{1,0:T(8,128)S(1)} %get-tuple-element.73.rest_0_), channel_id=1, source_target_pairs={{0,4},{4,0},{8,12},{12,8},{1,5},{5,1},{9,13},{13,9},{2,6},{6,2},{1... | collective-permute-start | bytes 12296 | tf_op jit(solution)/shard_map/ppermute | solution.py:393
  29.6 0.4 shard_map.74.share_ref
  30.0 0.6 %collective-permute-done.4.rest_1_ = f32[8,128]{1,0:T(8,128)S(1)} collective-permute-done((f32[8,128]{1,0:T(8,128)S(1)}, f32[8,128]{1,0:T(8,128)S(1)}, u32[]{:S(2)}, u32[]{:S(2)}) %collective-permute-start.4) | collective-permute-done | bytes 4128 | tf_op jit(solution)/shard_map/ppermute | solution.py:393
  30.6 1.6 %collective-permute-done.5.rest_2_ = f32[8,128]{1,0:T(8,128)S(1)} collective-permute-done((f32[8,128]{1,0:T(8,128)S(1)}, f32[8,128]{1,0:T(8,128)S(1)}, u32[]{:S(2)}, u32[]{:S(2)}) %collective-permute-start.5) | collective-permute-done | bytes 4128 | tf_op jit(solution)/shard_map/ppermute | solution.py:393
  32.2 0.0 collective-permute-done.6.rest_3_
  32.2 0.9 %shard_map.75 = (bf16[8,2,2176]{2,1,0:T(2,128)(2,1)S(1)}, bf16[8,2,2176]{2,1,0:T(2,128)(2,1)S(1)}) custom-call(f32[16,128,128]{2,1,0:T(8,128)S(1)} %shard_map.74.share_ref, bf16[128,4096]{1,0:T(8,128)(2,1)S(1)} %get-tuple-element.72.based_ref, f32[8,2048]{1,0:T(8,128)S(1)} %get-tuple-element.48.refs_3_.refs_4_.cos_ref, ...), custom_call_target="tpu_custom_call" | custom-call | tf_op jit(solution)/shard_map/pallas_call | solution.py:376
  33.1 0.1 collective-permute-start.7
  33.2 1.2 %collective-permute-done.7.other_ref = bf16[8,2,2176]{2,1,0:T(2,128)(2,1)S(1)} collective-permute-done((bf16[8,2,2176]{2,1,0:T(2,128)(2,1)S(1)}, bf16[8,2,2176]{2,1,0:T(2,128)(2,1)S(1)}, u32[]{:S(2)}, u32[]{:S(2)}) %collective-permute-start.7) | collective-permute-done | bytes 69664 | tf_op jit(solution)/shard_map/ppermute | solution.py:530
  34.5 0.1 shard_map.76
  34.5 1.6 %collective-permute-start.8 = (bf16[4,2,2176]{2,1,0:T(2,128)(2,1)S(1)}, bf16[4,2,2176]{2,1,0:T(2,128)(2,1)S(1)}, u32[]{:S(2)}, u32[]{:S(2)}) collective-permute-start(bf16[4,2,2176]{2,1,0:T(2,128)(2,1)S(1)} %get-tuple-element.77), channel_id=1, source_target_pairs={{0,2},{2,0},{1,3},{3,1},{4,6},{6,4},{5,7},{7,5},{8,10},{10,8},{9,1... | collective-permute-start | bytes 104456 | tf_op jit(solution)/shard_map/ppermute | solution.py:532
  36.1 2.4 %collective-permute-done.8.refs_1_ = bf16[4,2,2176]{2,1,0:T(2,128)(2,1)S(1)} collective-permute-done((bf16[4,2,2176]{2,1,0:T(2,128)(2,1)S(1)}, bf16[4,2,2176]{2,1,0:T(2,128)(2,1)S(1)}, u32[]{:S(2)}, u32[]{:S(2)}) %collective-permute-start.8) | collective-permute-done | bytes 34848 | tf_op jit(solution)/shard_map/ppermute | solution.py:532
  38.6 2.1 %collective-permute-start.10 = (bf16[2,2176]{1,0:T(2,128)(2,1)S(1)}, bf16[2,2176]{1,0:T(2,128)(2,1)S(1)}, u32[]{:S(2)}, u32[]{:S(2)}) collective-permute-start(bf16[2,2176]{1,0:T(2,128)(2,1)S(1)} %get-tuple-element.80), channel_id=1, source_target_pairs={{0,8},{4,12},{8,0},{12,4},{1,9},{5,13},{9,1},{13,5},{2,10},{6,14},... | collective-permute-start | bytes 26120 | tf_op jit(solution)/shard_map/ppermute | solution.py:393
  40.7 0.0 collective-permute-start.11
  40.7 2.4 %collective-permute-start.9 = (bf16[2,2176]{1,0:T(2,128)(2,1)S(1)}, bf16[2,2176]{1,0:T(2,128)(2,1)S(1)}, u32[]{:S(2)}, u32[]{:S(2)}) collective-permute-start(bf16[2,2176]{1,0:T(2,128)(2,1)S(1)} %get-tuple-element.79), channel_id=1, source_target_pairs={{0,12},{4,8},{8,4},{12,0},{1,13},{5,9},{9,5},{13,1},{2,14},{6,10},... | collective-permute-start | bytes 26120 | tf_op jit(solution)/shard_map/ppermute | solution.py:393
  43.0 0.2 collective-permute-done.10.refs_2_
  43.2 1.1 %collective-permute-done.11.refs_3_ = bf16[2,2176]{1,0:T(2,128)(2,1)S(1)} collective-permute-done((bf16[2,2176]{1,0:T(2,128)(2,1)S(1)}, bf16[2,2176]{1,0:T(2,128)(2,1)S(1)}, u32[]{:S(2)}, u32[]{:S(2)}) %collective-permute-start.11) | collective-permute-done | bytes 8736 | tf_op jit(solution)/shard_map/ppermute | solution.py:393
  44.3 1.8 %collective-permute-done.9.refs_1_ = bf16[2,2176]{1,0:T(2,128)(2,1)S(1)} collective-permute-done((bf16[2,2176]{1,0:T(2,128)(2,1)S(1)}, bf16[2,2176]{1,0:T(2,128)(2,1)S(1)}, u32[]{:S(2)}, u32[]{:S(2)}) %collective-permute-start.9) | collective-permute-done | bytes 8736 | tf_op jit(solution)/shard_map/ppermute | solution.py:393
  46.1 1.0 %shard_map.78 = (f32[1,2,256]{2,1,0:T(2,128)}, f32[1,1,256]{2,1,0:T(1,128)}) custom-call(bf16[2,2176]{1,0:T(2,128)(2,1)S(1)} %get-tuple-element.78.refs_0_, bf16[2,2176]{1,0:T(2,128)(2,1)S(1)} %collective-permute-done.9.refs_1_, bf16[2,2176]{1,0:T(2,128)(2,1)S(1)} %collective-permute-done.10.refs_2_, bf16[2,2176]{1,0:T(2,128)(2,1)S(1)} %collective-permute-done.11.refs_3_, ...), custom_call_target="tpu_custom_call" | custom-call | tf_op jit(solution)/shard_map/pallas_call | solution.py:376
  (1 shorter events, 0.0 us)
Async XLA Ops:
  0.6 7.5 %copy-start = (bf16[32,4096]{1,0:T(8,128)(2,1)S(1)}, bf16[32,4096]{1,0:T(8,128)(2,1)}, u32[]{:S(2)}) copy-start(bf16[32,4096]{1,0:T(8,128)(2,1)} %images_hbm.1) | copy-start | bytes 786436
  0.6 11.1 %collective-permute-start = (bf16[32,4096]{1,0:T(8,128)(2,1)}, bf16[32,4096]{1,0:T(8,128)(2,1)S(1)}, u32[]{:S(2)}, u32[]{:S(2)}) collective-permute-start(bf16[32,4096]{1,0:T(8,128)(2,1)} %images_hbm.1), channel_id=1, source_target_pairs={{0,8},{12,4},{8,12},{4,0},{1,9},{13,5},{9,13},{5,1},{2,10},{14,6},... | collective-permute-start | bytes 786440 | tf_op jit(solution)/shard_map/ppermute | solution.py:430
  8.2 9.9 %collective-permute-start.3 = (bf16[32,4096]{1,0:T(8,128)(2,1)S(1)}, bf16[32,4096]{1,0:T(8,128)(2,1)S(1)}, u32[]{:S(2)}, u32[]{:S(2)}) collective-permute-start(bf16[32,4096]{1,0:T(8,128)(2,1)S(1)} %copy-done), channel_id=1, source_target_pairs={{0,4},{12,8},{4,12},{8,0},{1,5},{13,9},{5,13},{9,1},{2,6},{14,10},... | collective-permute-start | bytes 786440 | tf_op jit(solution)/shard_map/ppermute | solution.py:478
  11.8 11.8 %collective-permute-start.1 = (bf16[32,4096]{1,0:T(8,128)(2,1)S(1)}, bf16[32,4096]{1,0:T(8,128)(2,1)S(1)}, u32[]{:S(2)}, u32[]{:S(2)}) collective-permute-start(bf16[32,4096]{1,0:T(8,128)(2,1)S(1)} %collective-permute-done.refs_0_), channel_id=1, source_target_pairs={{8,12},{4,0},{9,13},{5,1},{10,14},{6,2},{11,15},{7,3},{24,28},{20,... | collective-permute-start | bytes 786440 | tf_op jit(solution)/shard_map/ppermute | solution.py:499
  13.1 10.5 %collective-permute-start.2 = (bf16[32,4096]{1,0:T(8,128)(2,1)S(1)}, bf16[32,4096]{1,0:T(8,128)(2,1)S(1)}, u32[]{:S(2)}, u32[]{:S(2)}) collective-permute-start(bf16[32,4096]{1,0:T(8,128)(2,1)S(1)} %copy-done), channel_id=1, source_target_pairs={{4,8},{8,4},{0,0},{12,12},{5,9},{9,5},{1,1},{13,13},{6,10},{10,6},... | collective-permute-start | bytes 786440 | tf_op jit(solution)/shard_map/ppermute | solution.py:500
  25.2 5.4 %collective-permute-start.4 = (f32[8,128]{1,0:T(8,128)S(1)}, f32[8,128]{1,0:T(8,128)S(1)}, u32[]{:S(2)}, u32[]{:S(2)}) collective-permute-start(f32[8,128]{1,0:T(8,128)S(1)} %get-tuple-element.73.rest_0_), channel_id=1, source_target_pairs={{0,12},{4,8},{8,4},{12,0},{1,13},{5,9},{9,5},{13,1},{2,14},{6,10},... | collective-permute-start | bytes 12296 | tf_op jit(solution)/shard_map/ppermute | solution.py:393
  27.7 4.5 %collective-permute-start.5 = (f32[8,128]{1,0:T(8,128)S(1)}, f32[8,128]{1,0:T(8,128)S(1)}, u32[]{:S(2)}, u32[]{:S(2)}) collective-permute-start(f32[8,128]{1,0:T(8,128)S(1)} %get-tuple-element.73.rest_0_), channel_id=1, source_target_pairs={{0,8},{4,12},{8,0},{12,4},{1,9},{5,13},{9,1},{13,5},{2,10},{6,14},... | collective-permute-start | bytes 12296 | tf_op jit(solution)/shard_map/ppermute | solution.py:393
  27.7 4.5 %collective-permute-start.6 = (f32[8,128]{1,0:T(8,128)S(1)}, f32[8,128]{1,0:T(8,128)S(1)}, u32[]{:S(2)}, u32[]{:S(2)}) collective-permute-start(f32[8,128]{1,0:T(8,128)S(1)} %get-tuple-element.73.rest_0_), channel_id=1, source_target_pairs={{0,4},{4,0},{8,12},{12,8},{1,5},{5,1},{9,13},{13,9},{2,6},{6,2},{1... | collective-permute-start | bytes 12296 | tf_op jit(solution)/shard_map/ppermute | solution.py:393
  33.1 1.3 %collective-permute-start.7 = (bf16[8,2,2176]{2,1,0:T(2,128)(2,1)S(1)}, bf16[8,2,2176]{2,1,0:T(2,128)(2,1)S(1)}, u32[]{:S(2)}, u32[]{:S(2)}) collective-permute-start(bf16[8,2,2176]{2,1,0:T(2,128)(2,1)S(1)} %get-tuple-element.75), channel_id=1, source_target_pairs={{0,1},{1,0},{2,3},{3,2},{4,5},{5,4},{6,7},{7,6},{8,9},{9,8},{10,11... | collective-permute-start | bytes 208904 | tf_op jit(solution)/shard_map/ppermute | solution.py:530
  34.5 4.0 %collective-permute-start.8 = (bf16[4,2,2176]{2,1,0:T(2,128)(2,1)S(1)}, bf16[4,2,2176]{2,1,0:T(2,128)(2,1)S(1)}, u32[]{:S(2)}, u32[]{:S(2)}) collective-permute-start(bf16[4,2,2176]{2,1,0:T(2,128)(2,1)S(1)} %get-tuple-element.77), channel_id=1, source_target_pairs={{0,2},{2,0},{1,3},{3,1},{4,6},{6,4},{5,7},{7,5},{8,10},{10,8},{9,1... | collective-permute-start | bytes 104456 | tf_op jit(solution)/shard_map/ppermute | solution.py:532
  38.6 4.6 %collective-permute-start.10 = (bf16[2,2176]{1,0:T(2,128)(2,1)S(1)}, bf16[2,2176]{1,0:T(2,128)(2,1)S(1)}, u32[]{:S(2)}, u32[]{:S(2)}) collective-permute-start(bf16[2,2176]{1,0:T(2,128)(2,1)S(1)} %get-tuple-element.80), channel_id=1, source_target_pairs={{0,8},{4,12},{8,0},{12,4},{1,9},{5,13},{9,1},{13,5},{2,10},{6,14},... | collective-permute-start | bytes 26120 | tf_op jit(solution)/shard_map/ppermute | solution.py:393
  40.7 3.7 %collective-permute-start.11 = (bf16[2,2176]{1,0:T(2,128)(2,1)S(1)}, bf16[2,2176]{1,0:T(2,128)(2,1)S(1)}, u32[]{:S(2)}, u32[]{:S(2)}) collective-permute-start(bf16[2,2176]{1,0:T(2,128)(2,1)S(1)} %get-tuple-element.81), channel_id=1, source_target_pairs={{0,4},{4,0},{8,12},{12,8},{1,5},{5,1},{9,13},{13,9},{2,6},{6,2},{1... | collective-permute-start | bytes 26120 | tf_op jit(solution)/shard_map/ppermute | solution.py:393
  40.7 5.5 %collective-permute-start.9 = (bf16[2,2176]{1,0:T(2,128)(2,1)S(1)}, bf16[2,2176]{1,0:T(2,128)(2,1)S(1)}, u32[]{:S(2)}, u32[]{:S(2)}) collective-permute-start(bf16[2,2176]{1,0:T(2,128)(2,1)S(1)} %get-tuple-element.79), channel_id=1, source_target_pairs={{0,12},{4,8},{8,4},{12,0},{1,13},{5,9},{9,5},{13,1},{2,14},{6,10},... | collective-permute-start | bytes 26120 | tf_op jit(solution)/shard_map/ppermute | solution.py:393
